TPU v7x, 32 devices: a whole 2x2x4 slice. The times are simulated.
32 devices in a mesh: dp: 8 (over z, x), space: 4 (over y, core).
Axes of the slice: x: 2, y: 2, z: 4, core: 2. Of those that a mesh axis runs over, the one named last changes fastest.
Arguments:
- scenes: bfloat16 [16, 64, 64, 320], P('dp', 'space'), may hold values from -6 to 6
- params: bfloat16 [1658880], P(('dp', 'space')), may hold values from -3 to 3
- cotangent: bfloat16 [16, 64, 64, 320], P('dp', 'space'), may hold values from -6 to 6
Outputs:
- block_out: bfloat16 [16, 64, 64, 320], P('dp', 'space')
- input_grad: float32 [16, 64, 64, 320], P('dp', 'space')
- param_grad: float32 [1658880], P(('dp', 'space'))
All inputs are finite; a program needn't handle non-finite values.
Results may differ from a plain program's by a relative error of at most 0.013.
Values may be sent and summed in bfloat16 or wider, within the bound.
A program may use at most 192 MiB of HBM per device.

v0:
```python
import functools
import math

import jax
import jax.numpy as jnp
from jax import lax
from jax.experimental import pallas as pl
from jax.experimental.pallas import tpu as pltpu
from jax.sharding import PartitionSpec as P

C = 320
HEADS = 5
HD = 64
FF = 1280
W = 64
EPSILON = 1e-06
F32 = jnp.float32
BF16 = jnp.bfloat16

ROWS = 5184
USED_ROWS = 5175
BLOCKS = 32
BLOCK_ROWS = ROWS // BLOCKS
R_QUERY = 0
R_REDUCE = 321
R_KEYVAL = 1604
R_OUTPUT = 2245
R_EXPAND = 2570
R_HIDDEN = 3850
R_SHRINK = 3894
VECTOR_ROWS = (320, 1601, 1602, 1603, 2244, 2565, 2566, 2567, 2568, 2569, 5174)
(
    V_QUERY,
    V_REDUCE,
    V_RGAIN,
    V_RSHIFT,
    V_VALUE,
    V_OUTPUT,
    V_GAIN1,
    V_SHIFT1,
    V_GAIN2,
    V_SHIFT2,
    V_SHRINK,
) = range(11)
HIDDEN_ROWS = 11

PARAMS = pltpu.CompilerParams(vmem_limit_bytes=60 * 1024 * 1024)


def shape_of(dims, kind):
    return jax.ShapeDtypeStruct(dims, kind)


def mm(left, right):
    return jnp.dot(left, right, preferred_element_type=F32)


def mm_tn(left, right):
    return lax.dot_general(left, right, (((0,), (0,)), ((), ())), preferred_element_type=F32)


def mm_nt(left, right):
    return lax.dot_general(left, right, (((1,), (1,)), ((), ())), preferred_element_type=F32)


def mm_tt(left, right):
    return lax.dot_general(left, right, (((0,), (1,)), ((), ())), preferred_element_type=F32)


def norm_parts(values):
    center = values - jnp.mean(values, axis=-1, keepdims=True)
    rstd = lax.rsqrt(jnp.mean(center * center, axis=-1, keepdims=True) + EPSILON)
    return center * rstd, rstd


def norm_back(grad, unit, rstd, gain):
    scaled = grad * gain
    first = jnp.mean(scaled, axis=-1, keepdims=True)
    second = jnp.mean(scaled * unit, axis=-1, keepdims=True)
    return rstd * (scaled - first - unit * second)


def row_sum(values):
    return jnp.sum(values, axis=0, keepdims=True)


def full(dims):
    return pl.BlockSpec(dims, lambda *_: (0,) * len(dims))


def unpack_kernel(g_ref, wq, wr, wk, wv, wo, we, ws, vec, hid, rows, tiles):
    for i in range(BLOCKS):
        at = i * BLOCK_ROWS
        block = g_ref[i].astype(F32)
        rows[at : at + BLOCK_ROWS, :] = block
        tiles[0, at : at + BLOCK_ROWS, :] = block[:, 0:128]
        tiles[1, at : at + BLOCK_ROWS, :] = block[:, 128:256]
        tiles[2, at : at + BLOCK_ROWS, 0:64] = block[:, 256:320]

    def strided(start, count, step):
        parts = [tiles[t, pl.ds(start, count, stride=step), :] for t in range(3)]
        return jnp.concatenate([parts[0], parts[1], parts[2][:, 0:64]], axis=1)

    wq[...] = rows[R_QUERY : R_QUERY + C, :].astype(BF16)
    wr[...] = rows[R_REDUCE : R_REDUCE + 4 * C, :].astype(BF16)
    wk[...] = strided(R_KEYVAL, C, 2).astype(BF16)
    wv[...] = strided(R_KEYVAL + 1, C, 2).astype(BF16)
    wo[...] = rows[R_OUTPUT : R_OUTPUT + C, :].astype(BF16)
    ws[...] = rows[R_SHRINK : R_SHRINK + FF, :].astype(BF16)
    we[...] = jnp.concatenate([strided(R_EXPAND + j, C, 4) for j in range(4)], axis=1).astype(BF16)
    hid[0:HIDDEN_ROWS, :] = jnp.concatenate(
        [strided(R_HIDDEN + j, HIDDEN_ROWS, 4) for j in range(4)], axis=1
    )
    for i, row in enumerate(VECTOR_ROWS):
        vec[i : i + 1, :] = rows[row : row + 1, :]


def unpack(blocks):
    return pl.pallas_call(
        unpack_kernel,
        name="unpack",
        out_shape=(
            shape_of((C, C), BF16),
            shape_of((4 * C, C), BF16),
            shape_of((C, C), BF16),
            shape_of((C, C), BF16),
            shape_of((C, C), BF16),
            shape_of((C, FF), BF16),
            shape_of((FF, C), BF16),
            shape_of((16, C), F32),
            shape_of((16, FF), F32),
        ),
        scratch_shapes=[pltpu.VMEM((ROWS, C), F32), pltpu.VMEM((3, ROWS, 128), F32)],
        compiler_params=PARAMS,
    )(blocks)


def pack_kernel(gwq, gwr, gwk, gwv, gwo, gwe, gws, gvec0, gvec1, gvec2, ghid, out, tiles):
    def put(start, value):
        count = value.shape[0]
        tiles[0, start : start + count, :] = value[:, 0:128]
        tiles[1, start : start + count, :] = value[:, 128:256]
        tiles[2, start : start + count, 0:64] = value[:, 256:320]

    def put_strided(start, step, value):
        count = value.shape[0]
        tiles[0, pl.ds(start, count, stride=step), :] = value[:, 0:128]
        tiles[1, pl.ds(start, count, stride=step), :] = value[:, 128:256]
        tail = jnp.concatenate([value[:, 256:320], jnp.zeros((count, 64), F32)], axis=1)
        tiles[2, pl.ds(start, count, stride=step), :] = tail

    put(R_QUERY, gwq[...])
    put(R_REDUCE, gwr[...])
    put_strided(R_KEYVAL, 2, gwk[...])
    put_strided(R_KEYVAL + 1, 2, gwv[...])
    put(R_OUTPUT, gwo[...])
    put(R_SHRINK, gws[...])
    for j in range(4):
        put_strided(R_EXPAND + j, 4, gwe[:, C * j : C * j + C])
        put_strided(R_HIDDEN + j, 4, ghid[0:HIDDEN_ROWS, C * j : C * j + C])
    for source, names in (
        (gvec0, (V_QUERY, V_REDUCE, V_RGAIN, V_RSHIFT, V_GAIN1, V_SHIFT1)),
        (gvec1, (V_VALUE, V_OUTPUT)),
        (gvec2, (V_GAIN2, V_SHIFT2, V_SHRINK)),
    ):
        for i, name in enumerate(names):
            put(VECTOR_ROWS[name], source[i : i + 1, :])
    put(USED_ROWS, jnp.zeros((ROWS - USED_ROWS, C), F32))
    for i in range(BLOCKS):
        at = i * BLOCK_ROWS
        out[i, :, 0:128] = tiles[0, at : at + BLOCK_ROWS, :].astype(BF16)
        out[i, :, 128:256] = tiles[1, at : at + BLOCK_ROWS, :].astype(BF16)
        out[i, :, 256:320] = tiles[2, at : at + BLOCK_ROWS, 0:64].astype(BF16)


def pack(*pieces):
    return pl.pallas_call(
        pack_kernel,
        name="pack",
        out_shape=shape_of((BLOCKS, BLOCK_ROWS, C), BF16),
        scratch_shapes=[pltpu.VMEM((3, ROWS, 128), F32)],
        compiler_params=PARAMS,
    )(*pieces)


TILE = 8 * W
RTILE = TILE // 4


def split_tiles(scr, value):
    scr[0, :, :] = value[:, 0:128]
    scr[1, :, :] = value[:, 128:256]
    scr[2, :, 0:64] = value[:, 256:320]


def patch_pieces(scr):
    pieces = {}
    for b in range(2):
        parts = [scr[t, pl.ds(b, TILE // 2, stride=2), :] for t in range(3)]
        cols = jnp.concatenate([parts[0], parts[1], parts[2][:, 0:64]], axis=1)
        cols = cols.reshape(TILE // (2 * W), 2, W // 2, C)
        for a in range(2):
            pieces[2 * a + b] = cols[:, a].reshape(RTILE, C)
    return pieces


def front_kernel(x_ref, vec, wq, wr, q_out, red_out, rn_out, scr):
    unit, _ = norm_parts(x_ref[...].astype(F32))
    normed = (unit * vec[V_GAIN1 : V_GAIN1 + 1, :] + vec[V_SHIFT1 : V_SHIFT1 + 1, :]).astype(BF16)
    queries = (mm(normed, wq[...]) + vec[V_QUERY : V_QUERY + 1, :]).astype(BF16)
    q_out[...] = queries * jnp.asarray(1.0 / math.sqrt(HD), BF16)
    split_tiles(scr, normed.astype(F32))
    pieces = patch_pieces(scr)
    reduced = vec[V_REDUCE : V_REDUCE + 1, :]
    for k in range(4):
        reduced = reduced + mm(pieces[k].astype(BF16), wr[k * C : (k + 1) * C, :])
    red_out[...] = reduced
    unit, _ = norm_parts(reduced)
    rn_out[...] = (unit * vec[V_RGAIN : V_RGAIN + 1, :] + vec[V_RSHIFT : V_RSHIFT + 1, :]).astype(
        BF16
    )


def front(x, vec, wq, wr):
    tokens = x.shape[0]
    return pl.pallas_call(
        front_kernel,
        name="front",
        grid=(tokens // TILE,),
        in_specs=[
            pl.BlockSpec((TILE, C), lambda i: (i, 0)),
            full((16, C)),
            full((C, C)),
            full((4 * C, C)),
        ],
        out_specs=[
            pl.BlockSpec((TILE, C), lambda i: (i, 0)),
            pl.BlockSpec((RTILE, C), lambda i: (i, 0)),
            pl.BlockSpec((RTILE, C), lambda i: (i, 0)),
        ],
        out_shape=(
            shape_of((tokens, C), BF16),
            shape_of((tokens // 4, C), F32),
            shape_of((tokens // 4, C), BF16),
        ),
        scratch_shapes=[pltpu.VMEM((3, TILE, 128), F32)],
        compiler_params=PARAMS,
    )(x, vec, wq, wr)


QT = 256


def attend_kernel(
    x_ref, q_ref, rn_ref, vec, wk, wv, wo, mixed_out, lse_out, mid_out, n2_out, kt, vones
):
    keys = rn_ref.shape[0] * rn_ref.shape[2]

    @pl.when(pl.program_id(1) == 0)
    def _():
        rn = rn_ref[:, 0].reshape(keys, C)
        key = mm(rn, wk[...]).astype(BF16)
        value = (mm(rn, wv[...]) + vec[V_VALUE : V_VALUE + 1, :]).astype(BF16)
        kt[...] = key.T
        for h in range(HEADS):
            vones[h, :, 0:HD] = value[:, h * HD : (h + 1) * HD]
            vones[h, :, HD:] = jnp.ones((keys, HD), BF16)

    lane = lax.broadcasted_iota(jnp.int32, (QT, 128), 1)
    lses = jnp.zeros((QT, 128), F32)
    outs = []
    for h in range(HEADS):
        scores = mm(q_ref[:, h * HD : (h + 1) * HD], kt[h * HD : (h + 1) * HD, :])
        top = jnp.max(scores, axis=-1, keepdims=True)
        probs = jnp.exp(scores - top).astype(BF16)
        both = mm(probs, vones[h])
        outs.append(both[:, 0:HD] / both[:, HD:])
        lses = jnp.where(lane == h, top + jnp.log(both[:, HD : HD + 1]), lses)
    mixed = jnp.concatenate(outs, axis=1).astype(BF16)
    mixed_out[...] = mixed
    lse_out[...] = lses
    middle = x_ref[...].astype(F32) + mm(mixed, wo[...]) + vec[V_OUTPUT : V_OUTPUT + 1, :]
    mid_out[...] = middle
    unit, _ = norm_parts(middle)
    n2_out[...] = (unit * vec[V_GAIN2 : V_GAIN2 + 1, :] + vec[V_SHIFT2 : V_SHIFT2 + 1, :]).astype(
        BF16
    )


def attend(x, q, rn_all, vec, wk, wv, wo):
    tokens = x.shape[0]
    bands, scenes, per_band, _ = rn_all.shape
    keys = bands * per_band
    steps = tokens // scenes // QT
    tile = lambda s, i: (s * steps + i, 0)
    return pl.pallas_call(
        attend_kernel,
        name="attend",
        grid=(scenes, steps),
        in_specs=[
            pl.BlockSpec((QT, C), tile),
            pl.BlockSpec((QT, C), tile),
            pl.BlockSpec((bands, 1, per_band, C), lambda s, i: (0, s, 0, 0)),
            full((16, C)),
            full((C, C)),
            full((C, C)),
            full((C, C)),
        ],
        out_specs=[
            pl.BlockSpec((QT, C), tile),
            pl.BlockSpec((QT, 128), tile),
            pl.BlockSpec((QT, C), tile),
            pl.BlockSpec((QT, C), tile),
        ],
        out_shape=(
            shape_of((tokens, C), BF16),
            shape_of((tokens, 128), F32),
            shape_of((tokens, C), F32),
            shape_of((tokens, C), BF16),
        ),
        scratch_shapes=[pltpu.VMEM((C, keys), BF16), pltpu.VMEM((HEADS, keys, 2 * HD), BF16)],
        compiler_params=PARAMS,
    )(x, q, rn_all, vec, wk, wv, wo)


CH = 256


def gelu_parts(x):
    size = jnp.abs(x)
    t = 1.0 / (1.0 + (0.3275911 * math.sqrt(0.5)) * size)
    poly = t * (
        0.5 * 0.254829592
        + t
        * (
            0.5 * -0.284496736
            + t * (0.5 * 1.421413741 + t * (0.5 * -1.453152027 + t * (0.5 * 1.061405429)))
        )
    )
    bell = jnp.exp(-0.5 * (x * x))
    tail = poly * bell
    return jnp.where(x >= 0, 1.0 - tail, tail), bell * (1.0 / math.sqrt(2.0 * math.pi))


def mix_kernel(
    n2, n2_top, n2_low, cot, cot_top, cot_low, mid, edge, vec, hid, we, ws,
    y_out, gmid_out, gwe_out, gws_out, ghid_out, gvec_out,
    e_scr, ga_scr, gc_scr, act_scr, ge_scr, branch, gn2,
):
    step = pl.program_id(0)
    scenes, rows = n2.shape[0], n2.shape[1]
    ext = (rows + 4) * W
    gext = (rows + 2) * W
    own = rows * W
    wcol = we[...]
    wrow = ws[...]
    bias = hid[0:1, :]
    top, low = edge[0], edge[1]
    for s in range(scenes):
        body = mm(n2[s].reshape(own, C), wcol) + bias
        e_scr[s * ext + 2 * W : s * ext + 2 * W + own, :] = body.astype(BF16).astype(F32)
        part = mm(n2_top[s].reshape(2 * W, C), wcol) + bias
        e_scr[s * ext : s * ext + 2 * W, :] = part.astype(BF16).astype(F32) * top
        part = mm(n2_low[s].reshape(2 * W, C), wcol) + bias
        e_scr[s * ext + 2 * W + own : (s + 1) * ext, :] = part.astype(BF16).astype(F32) * low
        ga_scr[s * gext + W : s * gext + W + own, :] = mm_nt(cot[s].reshape(own, C), wrow)
        ga_scr[s * gext : s * gext + W, :] = mm_nt(cot_top[s].reshape(W, C), wrow) * top
        ga_scr[s * gext + W + own : (s + 1) * gext, :] = (
            mm_nt(cot_low[s].reshape(W, C), wrow) * low
        )
    col = lax.broadcasted_iota(jnp.int32, (W, 128), 0)
    first, last = col == 0, col == W - 1

    def right(value):
        return jnp.where(first, 0.0, pltpu.roll(value, 1, axis=0))

    def left(value):
        return jnp.where(last, 0.0, pltpu.roll(value, W - 1, axis=0))

    def fold(value):
        return jnp.sum(value.reshape(W // 8, 8, 128), axis=0)

    for half in range(CH // 128):
        lanes = slice(half * 128, half * 128 + 128)
        taps = [hid[1 + k : 2 + k, lanes] for k in range(9)]
        conv_bias = hid[10:11, lanes]

        for s in range(scenes):

            def forward(r, carry):
                at = pl.multiple_of(s * ext + r * W, W)
                lines = [e_scr[pl.ds(at + a * W, W), lanes] for a in range(3)]
                sums = [
                    lines[0] * taps[b] + lines[1] * taps[3 + b] + lines[2] * taps[6 + b]
                    for b in range(3)
                ]
                conv = conv_bias + right(sums[0]) + sums[1] + left(sums[2])
                cdf, density = gelu_parts(conv)
                gat = pl.multiple_of(s * gext + r * W, W)
                gc = ga_scr[pl.ds(gat, W), lanes] * (cdf + conv * density)
                gc = gc.astype(BF16).astype(F32)
                act_scr[pl.ds(gat, W), lanes] = (conv * cdf).astype(BF16)
                gc_scr[0, pl.ds(gat, W), lanes] = left(gc)
                gc_scr[1, pl.ds(gat, W), lanes] = gc
                gc_scr[2, pl.ds(gat, W), lanes] = right(gc)
                return carry

            lax.fori_loop(0, rows + 2, forward, 0)

        def backward(s, r, carry):
            line = e_scr[pl.ds(pl.multiple_of(s * ext + (r + 2) * W, W), W), lanes]
            grads = list(carry)
            total = None
            for a in range(3):
                gat = pl.multiple_of(s * gext + (r + 2 - a) * W, W)
                for b in range(3):
                    g = gc_scr[b, pl.ds(gat, W), lanes]
                    term = g * taps[3 * a + b]
                    total = term if total is None else total + term
                    grads[3 * a + b] = grads[3 * a + b] + fold(g * line)
                    if a == 1 and b == 1:
                        grads[9] = grads[9] + fold(g)
            total = total.astype(BF16)
            ge_scr[pl.ds(pl.multiple_of(s * own + r * W, W), W), lanes] = total
            grads[10] = grads[10] + fold(total.astype(F32))
            return tuple(grads)

        sums = tuple(jnp.zeros((8, 128), F32) for _ in range(11))
        for s in range(scenes):
            sums = lax.fori_loop(0, rows, functools.partial(backward, s), sums)
        ghid_out[0:1, lanes] = row_sum(sums[10])
        for k in range(10):
            ghid_out[1 + k : 2 + k, lanes] = row_sum(sums[k])

    gwe = gws = None
    for s in range(scenes):
        act = act_scr[s * gext + W : s * gext + W + own, :]
        ge = ge_scr[s * own : (s + 1) * own, :]
        term = mm_tn(act, cot[s].reshape(own, C))
        gws = term if gws is None else gws + term
        term = mm_tn(n2[s].reshape(own, C), ge)
        gwe = term if gwe is None else gwe + term
        out_part = mm(act, wrow)
        in_part = mm_nt(ge, wcol)
        at = slice(s * own, (s + 1) * own)

        @pl.when(step == 0)
        def _():
            branch[at, :] = out_part
            gn2[at, :] = in_part

        @pl.when(step > 0)
        def _():
            branch[at, :] += out_part
            gn2[at, :] += in_part

    gws_out[...] = gws
    gwe_out[...] = gwe

    @pl.when(step == pl.num_programs(0) - 1)
    def _():
        size = 4 * W
        per = own // size
        gain = vec[V_GAIN2 : V_GAIN2 + 1, :]

        def finish(i, carry):
            at = pl.multiple_of(i * size, size)
            s = i // per
            line = (i % per) * 4
            middle = mid[pl.ds(at, size), :]
            y_out[pl.ds(at, size), :] = (
                middle + branch[pl.ds(at, size), :] + vec[V_SHRINK : V_SHRINK + 1, :]
            ).astype(BF16)
            grad = gn2[pl.ds(at, size), :]
            unit, rstd = norm_parts(middle)
            direct = cot[s, pl.ds(line, 4)].reshape(size, C).astype(F32)
            gmid_out[pl.ds(at, size), :] = direct + norm_back(grad, unit, rstd, gain)
            return (
                carry[0] + row_sum(grad * unit),
                carry[1] + row_sum(grad),
                carry[2] + row_sum(direct),
            )

        zero = jnp.zeros((1, C), F32)
        sums = lax.fori_loop(0, scenes * per, finish, (zero, zero, zero))
        for i in range(3):
            gvec_out[i : i + 1, :] = sums[i]


def mix(n2, n2_top, n2_low, cot, cot_top, cot_low, mid, edge, vec, hid, we, ws):
    scenes, rows = n2.shape[0], n2.shape[1]
    tokens = scenes * rows * W
    ext = scenes * (rows + 4) * W
    gext = scenes * (rows + 2) * W
    once = dict(pipeline_mode=pl.Buffered(1))
    whole = lambda a: pl.BlockSpec(a.shape, lambda j: (0,) * a.ndim, **once)
    return pl.pallas_call(
        mix_kernel,
        name="mix",
        grid=(FF // CH,),
        in_specs=[
            whole(n2),
            whole(n2_top),
            whole(n2_low),
            whole(cot),
            whole(cot_top),
            whole(cot_low),
            whole(mid),
            pl.BlockSpec(memory_space=pltpu.SMEM),
            whole(vec),
            pl.BlockSpec((16, CH), lambda j: (0, j)),
            pl.BlockSpec((C, CH), lambda j: (0, j)),
            pl.BlockSpec((CH, C), lambda j: (j, 0)),
        ],
        out_specs=[
            full((tokens, C)),
            full((tokens, C)),
            pl.BlockSpec((C, CH), lambda j: (0, j)),
            pl.BlockSpec((CH, C), lambda j: (j, 0)),
            pl.BlockSpec((16, CH), lambda j: (0, j)),
            full((8, C)),
        ],
        out_shape=(
            shape_of((tokens, C), BF16),
            shape_of((tokens, C), F32),
            shape_of((C, FF), F32),
            shape_of((FF, C), F32),
            shape_of((16, FF), F32),
            shape_of((8, C), F32),
        ),
        scratch_shapes=[
            pltpu.VMEM((ext, CH), F32),
            pltpu.VMEM((gext, CH), F32),
            pltpu.VMEM((3, gext, CH), F32),
            pltpu.VMEM((gext, CH), BF16),
            pltpu.VMEM((tokens, CH), BF16),
            pltpu.VMEM((tokens, C), F32),
            pltpu.VMEM((tokens, C), F32),
        ],
        compiler_params=PARAMS,
    )(n2, n2_top, n2_low, cot, cot_top, cot_low, mid, edge, vec, hid, we, ws)


def attend_back_kernel(
    q_ref, lse_ref, mixed_ref, gmid_ref, rn_ref, vec, wk, wv, wo,
    dq_out, grn_out, gwk_out, gwv_out, gwo_out, gvec_out,
    kt, vt, kh, dkt, dvt,
):
    scene, step = pl.program_id(0), pl.program_id(1)
    keys = rn_ref.shape[0] * rn_ref.shape[2]
    start = jnp.logical_and(scene == 0, step == 0)

    @pl.when(start)
    def _():
        for ref in (gwk_out, gwv_out, gwo_out, gvec_out):
            ref[...] = jnp.zeros_like(ref)

    @pl.when(step == 0)
    def _():
        rn = rn_ref[:, 0].reshape(keys, C)
        key = mm(rn, wk[...]).astype(BF16)
        value = (mm(rn, wv[...]) + vec[V_VALUE : V_VALUE + 1, :]).astype(BF16)
        kt[...] = key.T
        vt[...] = value.T
        for h in range(HEADS):
            kh[h] = key[:, h * HD : (h + 1) * HD]
        dkt[...] = jnp.zeros_like(dkt)
        dvt[...] = jnp.zeros_like(dvt)

    gmid = gmid_ref[...]
    gatt = gmid.astype(BF16)
    gvec_out[1:2, :] += row_sum(gatt.astype(F32))
    mixed = mixed_ref[...]
    gwo_out[...] += mm_tn(mixed, gatt)
    gmixed = mm_nt(gatt, wo[...]).astype(BF16)
    prod = gmixed.astype(F32) * mixed.astype(F32)
    q = q_ref[...]
    q_t = q.T
    g_t = gmixed.T
    dqs = []
    for h in range(HEADS):
        cols = slice(h * HD, (h + 1) * HD)
        inner = jnp.sum(prod[:, cols], axis=-1, keepdims=True)
        probs = jnp.exp(mm(q[:, cols], kt[cols, :]) - lse_ref[:, h : h + 1])
        gprobs = mm(gmixed[:, cols], vt[cols, :])
        gscores = (probs * (gprobs - inner)).astype(BF16)
        dqs.append(mm(gscores, kh[h]))
        dkt[cols, :] += mm(q_t[cols, :], gscores)
        dvt[cols, :] += mm(g_t[cols, :], probs.astype(BF16))
    dq_out[...] = (jnp.concatenate(dqs, axis=1) * (1.0 / math.sqrt(HD))).astype(BF16)

    @pl.when(step == pl.num_programs(1) - 1)
    def _():
        rn = rn_ref[:, 0].reshape(keys, C)
        dk = dkt[...].T.astype(BF16)
        dv = dvt[...].T
        gvec_out[0:1, :] += row_sum(dv)
        dv = dv.astype(BF16)
        gwk_out[...] += mm_tn(rn, dk)
        gwv_out[...] += mm_tn(rn, dv)
        grn = mm_nt(dk, wk[...]) + mm_nt(dv, wv[...])
        grn_out[...] = grn.astype(BF16).reshape(grn_out.shape)


def attend_back(q, lse, mixed, gmid, rn_all, vec, wk, wv, wo):
    tokens = q.shape[0]
    bands, scenes, per_band, _ = rn_all.shape
    keys = bands * per_band
    steps = tokens // scenes // QT
    tile = lambda s, i: (s * steps + i, 0)
    return pl.pallas_call(
        attend_back_kernel,
        name="attend_back",
        grid=(scenes, steps),
        in_specs=[
            pl.BlockSpec((QT, C), tile),
            pl.BlockSpec((QT, 128), tile),
            pl.BlockSpec((QT, C), tile),
            pl.BlockSpec((QT, C), tile),
            pl.BlockSpec((bands, 1, per_band, C), lambda s, i: (0, s, 0, 0)),
            full((16, C)),
            full((C, C)),
            full((C, C)),
            full((C, C)),
        ],
        out_specs=[
            pl.BlockSpec((QT, C), tile),
            pl.BlockSpec((bands, 1, per_band, C), lambda s, i: (0, s, 0, 0)),
            full((C, C)),
            full((C, C)),
            full((C, C)),
            full((8, C)),
        ],
        out_shape=(
            shape_of((tokens, C), BF16),
            shape_of(rn_all.shape, BF16),
            shape_of((C, C), F32),
            shape_of((C, C), F32),
            shape_of((C, C), F32),
            shape_of((8, C), F32),
        ),
        scratch_shapes=[
            pltpu.VMEM((C, keys), BF16),
            pltpu.VMEM((C, keys), BF16),
            pltpu.VMEM((HEADS, keys, HD), BF16),
            pltpu.VMEM((C, keys), F32),
            pltpu.VMEM((C, keys), F32),
        ],
        compiler_params=PARAMS,
    )(q, lse, mixed, gmid, rn_all, vec, wk, wv, wo)


def tail_kernel(
    x_ref, gmid_ref, dq_ref, grn_ref, red_ref, vec, wq, wr,
    gx_out, gwq_out, gwr_out, gvec_out, scr, gscr,
):
    @pl.when(pl.program_id(0) == 0)
    def _():
        for ref in (gwq_out, gwr_out, gvec_out):
            ref[...] = jnp.zeros_like(ref)

    runit, rrstd = norm_parts(red_ref[...])
    grn = grn_ref[...].astype(F32)
    gred = norm_back(grn, runit, rrstd, vec[V_RGAIN : V_RGAIN + 1, :]).astype(BF16)
    unit, rstd = norm_parts(x_ref[...].astype(F32))
    gain = vec[V_GAIN1 : V_GAIN1 + 1, :]
    normed = (unit * gain + vec[V_SHIFT1 : V_SHIFT1 + 1, :]).astype(BF16)
    split_tiles(scr, normed.astype(F32))
    pieces = patch_pieces(scr)
    back = {}
    for k in range(4):
        at = slice(k * C, (k + 1) * C)
        gwr_out[at, :] += mm_tn(pieces[k].astype(BF16), gred)
        back[k] = mm_nt(gred, wr[at, :]).reshape(TILE // (2 * W), 1, W // 2, C)
    for b in range(2):
        cols = jnp.concatenate([back[b], back[2 + b]], axis=1).reshape(TILE // 2, C)
        spot = pl.ds(b, TILE // 2, stride=2)
        gscr[0, spot, :] = cols[:, 0:128]
        gscr[1, spot, :] = cols[:, 128:256]
        gscr[2, spot, :] = jnp.concatenate(
            [cols[:, 256:320], jnp.zeros((TILE // 2, 64), F32)], axis=1
        )
    dq = dq_ref[...]
    gwq_out[...] += mm_tn(normed, dq)
    placed = jnp.concatenate([gscr[0], gscr[1], gscr[2][:, 0:64]], axis=1)
    gnormed = mm_nt(dq, wq[...]) + placed
    gx_out[...] = gmid_ref[...] + norm_back(gnormed, unit, rstd, gain)
    gvec_out[0:1, :] += row_sum(dq.astype(F32))
    gvec_out[1:2, :] += row_sum(gred.astype(F32))
    gvec_out[2:3, :] += row_sum(grn * runit)
    gvec_out[3:4, :] += row_sum(grn)
    gvec_out[4:5, :] += row_sum(gnormed * unit)
    gvec_out[5:6, :] += row_sum(gnormed)


def tail(x, gmid, dq, grn, red, vec, wq, wr):
    tokens = x.shape[0]
    tile = pl.BlockSpec((TILE, C), lambda i: (i, 0))
    rtile = pl.BlockSpec((RTILE, C), lambda i: (i, 0))
    return pl.pallas_call(
        tail_kernel,
        name="tail",
        grid=(tokens // TILE,),
        in_specs=[
            tile, tile, tile, rtile, rtile, full((16, C)), full((C, C)), full((4 * C, C))
        ],
        out_specs=[tile, full((C, C)), full((4 * C, C)), full((8, C))],
        out_shape=(
            shape_of((tokens, C), F32),
            shape_of((C, C), F32),
            shape_of((4 * C, C), F32),
            shape_of((8, C), F32),
        ),
        scratch_shapes=[pltpu.VMEM((3, TILE, 128), F32), pltpu.VMEM((3, TILE, 128), F32)],
        compiler_params=PARAMS,
    )(x, gmid, dq, grn, red, vec, wq, wr)


def gather_params(params):
    size = params.shape[0]
    devices = lax.axis_size("dp") * lax.axis_size("space")
    if devices == BLOCKS and size == BLOCK_ROWS * C:
        return lax.all_gather(params.reshape(BLOCK_ROWS, C), ("dp", "space"), axis=0, tiled=False)
    flat = lax.all_gather(params, ("dp", "space"), axis=0, tiled=True)
    want = ROWS * C
    flat = flat[:want] if flat.shape[0] >= want else jnp.pad(flat, (0, want - flat.shape[0]))
    return flat.reshape(BLOCKS, BLOCK_ROWS, C)


def scatter_grads(blocks, size):
    devices = lax.axis_size("dp") * lax.axis_size("space")
    if devices == BLOCKS and size == BLOCK_ROWS * C:
        own = lax.psum_scatter(blocks, ("dp", "space"), scatter_dimension=0, tiled=False)
        return own.astype(F32).reshape(size)
    flat = blocks.reshape(-1)
    want = size * devices
    flat = flat[:want] if flat.shape[0] >= want else jnp.pad(flat, (0, want - flat.shape[0]))
    own = lax.psum_scatter(flat, ("dp", "space"), scatter_dimension=0, tiled=True)
    return own.astype(F32)


def edges(value, width):
    count = lax.axis_size("space")
    rows = value.shape[1]
    above = lax.ppermute(
        value[:, rows - width :], "space", [(i, i + 1) for i in range(count - 1)]
    )
    below = lax.ppermute(value[:, :width], "space", [(i + 1, i) for i in range(count - 1)])
    return above, below


def on_device(scenes, params, cotangent):
    count, rows, breadth = scenes.shape[0], scenes.shape[1], scenes.shape[2]
    tokens = count * rows * breadth
    bands = lax.axis_size("space")
    per_band = rows * breadth // 4
    band = lax.axis_index("space")
    edge = jnp.stack([band > 0, band < bands - 1]).astype(F32)
    wq, wr, wk, wv, wo, we, ws, vec, hid = unpack(gather_params(params))
    x = scenes.reshape(tokens, C)
    q, red, rn = front(x, vec, wq, wr)
    rn_all = lax.all_gather(rn, "space", axis=0, tiled=False)
    rn_all = rn_all.reshape(bands, count, per_band, C)
    cot_top, cot_low = edges(cotangent, 1)
    mixed, lse, mid, n2 = attend(x, q, rn_all, vec, wk, wv, wo)
    n2 = n2.reshape(scenes.shape)
    n2_top, n2_low = edges(n2, 2)
    y, gmid, gwe, gws, ghid, gvec2 = mix(
        n2, n2_top, n2_low, cotangent, cot_top, cot_low, mid, edge, vec, hid, we, ws
    )
    dq, grn_all, gwk, gwv, gwo, gvec1 = attend_back(
        q, lse, mixed, gmid, rn_all, vec, wk, wv, wo
    )
    grn = lax.psum_scatter(grn_all, "space", scatter_dimension=0, tiled=False)
    gx, gwq, gwr, gvec0 = tail(x, gmid, dq, grn.reshape(-1, C), red, vec, wq, wr)
    blocks = pack(gwq, gwr, gwk, gwv, gwo, gwe, gws, gvec0, gvec1, gvec2, ghid)
    shard = scatter_grads(blocks, params.shape[0])
    return y.reshape(scenes.shape), gx.reshape(scenes.shape), shard


def solution(mesh):
    band = P("dp", "space", None, None)
    flat = P(("dp", "space"))
    return jax.shard_map(
        on_device,
        mesh=mesh,
        in_specs=(band, flat, band),
        out_specs=(band, band, flat),
        check_vma=False,
    )
```

profile of v0, /device:TPU:0, one launch (start us, length us, event | category | flops | bytes accessed | tf_op | source)
XLA Modules:
  0.0 418.5 jit_solution(177773682498586314)
XLA Ops:
  7.2 0.0 all-gather.4.cloned.1.call-start
  7.2 1.7 all_gather_reshape.3
  8.9 0.0 all-gather.4.cloned.1.call-update
  8.9 0.0 all-gather.6.cloned.1.call-start
  9.0 66.6 %all-gather.4.cloned.1.call-done.g_ref = bf16[32,162,320]{2,1,0:T(8,128)(2,1)} async-done(((bf16[1,162,320]{2,1,0:T(8,128)(2,1)}), bf16[32,162,320]{2,1,0:T(8,128)(2,1)}) %all-gather.4.cloned.1.call-update) | async-done | bytes 3317776 | tf_op jit(solution)/shard_map/all_gather | solution.py:723
  75.6 5.0 %unpack.1 = (bf16[320,320]{1,0:T(8,128)(2,1)}, bf16[1280,320]{1,0:T(8,128)(2,1)}, bf16[320,320]{1,0:T(8,128)(2,1)}, bf16[320,320]{1,0:T(8,128)(2,1)}, bf16[320,3...) custom-call(bf16[32,162,320]{2,1,0:T(8,128)(2,1)} %all-gather.4.clon, ...), custom_call_target="tpu_custom_call" | custom-call | tf_op jit(solution)/shard_map/unpack/pallas_call | solution.py:119
  80.6 6.6 %front.1 = (bf16[2048,320]{1,0:T(8,128)(2,1)}, f32[512,320]{1,0:T(8,128)}, bf16[512,320]{1,0:T(8,128)(2,1)}) custom-call(bf16[2048,320]{1,0:T(8,128)(2,1)} %bitcast.8, f32[16,320]{1,0:T(8,128)} %get-tuple-element.35.vec, bf16[320,320]{1,0:T(8,128)(2,1)} %get-tuple-element.36.wq, bf16[1280,320]{1,0:T(8,128)(2,1)} %get-tuple-element.37.wr), custom_call_target="tpu_custom_call" | custom-call | tf_op jit(solution)/shard_map/front/pallas_call | solution.py:226
  87.2 0.0 all-gather.6.cloned.1.call-update
  87.2 0.0 reduce-scatter.5.cloned.1.call-start
  87.3 18.5 %all-gather.6.cloned.1.call-done = bf16[2048,320]{1,0:T(8,128)(2,1)} async-done(((bf16[512,320]{1,0:T(8,128)(2,1)}), bf16[2048,320]{1,0:T(8,128)(2,1)}) %all-gather.6.cloned.1.call-update) | async-done | bytes 1310736 | tf_op jit(solution)/shard_map/all_gather | solution.py:762
  105.8 28.7 %attend.1 = (bf16[2048,320]{1,0:T(8,128)(2,1)}, f32[2048,128]{1,0:T(8,128)}, f32[2048,320]{1,0:T(8,128)}, bf16[2048,320]{1,0:T(8,128)(2,1)}) custom-call(bf16[2048,320]{1,0:T(8,128)(2,1)} %bitcast.9, bf16[2048,320]{1,0:T(8,128)(2,1)} %get-tuple-element.38.q_ref, bf16[4,2,256,320]{3,2,1,0:T(8,128)(2,1)} %bitcast.11, f32[16,320]{1,0:T(8,128)} %get-tuple-element.35.vec, ...), custom_call_target="tpu_custom_call" | custom-call | tf_op jit(solution)/shard_map/attend/pallas_call | solution.py:296
  134.5 1.1 fusion.1
  135.6 1.3 collective-permute-start.1
  136.9 3.0 collective-permute-start
  139.9 1.0 fusion
  140.9 1.3 collective-permute-start.3
  142.2 4.2 %collective-permute-start.2 = (bf16[2,1,64,320]{3,2,1,0:T(8,128)(2,1)S(1)}, bf16[2,1,64,320]{3,2,1,0:T(8,128)(2,1)S(1)}, u32[]{:S(2)}, u32[]{:S(2)}) collective-permute-start(bf16[2,1,64,320]{3,2,1,0:T(8,128)(2,1)S(1)} %get-tuple-element.68), channel_id=1, source_target_pairs={{0,1},{1,2},{2,3},{4,5},{5,6},{6,7},{8,9},{9,10},{10,11},{12,13},{... | collective-permute-start | bytes 245768 | tf_op jit(solution)/shard_map/ppermute | solution.py:745
  146.4 0.6 add_convert_fusion.edge
  147.0 0.0 collective-permute-done.3.cot_low
  147.0 0.0 copy-start.2
  147.0 0.2 collective-permute-done.2.cot_top
  147.2 0.0 copy-start.3
  147.2 0.0 collective-permute-done.1.n2_low
  147.2 0.0 copy-start
  147.2 0.0 collective-permute-done.n2_top
  147.2 0.0 copy-start.1
  147.2 0.4 copy-done.2
  147.6 0.2 copy-done.3
  147.8 0.1 copy-done
  147.9 0.0 copy-done.1
  147.9 75.8 %mix.1 = (bf16[2048,320]{1,0:T(8,128)(2,1)}, f32[2048,320]{1,0:T(8,128)}, f32[320,1280]{1,0:T(8,128)}, f32[1280,320]{1,0:T(8,128)}, f32[16,1280]{1,0:T(8,128)}, /*index=5*/f32[8,320]{1,0:T(8,128)}) custom-call(bf16[2,16,64,320]{3,2,1,0:T(8,128)(2,1)} %bitcast.14, bf16[2,2,64,320]{3,2,1,0:T(8,128)(2,1)} %copy-done.1, bf16[2,2,64,320]{3,2,1,0:T(8,128)(2,1)} %copy-done, ...), custom_call_target="tpu_custom_call" | custom-call | tf_op jit(solution)/shard_map/mix/pallas_call | solution.py:497
  223.8 39.1 %attend_back.1 = (bf16[2048,320]{1,0:T(8,128)(2,1)}, bf16[4,2,256,320]{3,2,1,0:T(8,128)(2,1)}, f32[320,320]{1,0:T(8,128)}, f32[320,320]{1,0:T(8,128)}, f32[320,320]{1,0:T(8,128)}, /*index=5*/f32[8,320]{1,0:T(8,128)}) custom-call(bf16[2048,320]{1,0:T(8,128)(2,1)} %get-tuple-element.38.q_ref, f32[2048,128]{1,0:T(8,128)} %get-tuple-element.50.lse_ref, ...), custom_call_target="tpu_custom_call" | custom-call | tf_op jit(solution)/shard_map/attend_back/pallas_call | solution.py:611
  262.9 0.0 reduce-scatter.5.cloned.1.call-update
  262.9 0.0 reduce-scatter.7.cloned.1.call-start
  263.0 32.3 %reduce-scatter.5.cloned.1.call-done = bf16[1,2,256,320]{3,2,1,0:T(8,128)(2,1)} async-done(((bf16[4,2,256,320]{3,2,1,0:T(8,128)(2,1)}), bf16[1,2,256,320]{3,2,1,0:T(8,128)(2,1)}) %reduce-scatter.5.cloned.1.call-update) | async-done | bytes 327696 | tf_op jit(solution)/shard_map/reduce_scatter | solution.py:774
  295.3 10.7 %tail.1 = (f32[2048,320]{1,0:T(8,128)}, f32[320,320]{1,0:T(8,128)}, f32[1280,320]{1,0:T(8,128)}, f32[8,320]{1,0:T(8,128)}) custom-call(bf16[2048,320]{1,0:T(8,128)(2,1)} %bitcast.10, f32[2048,320]{1,0:T(8,128)} %get-tuple-element.49.gmid_ref, bf16[2048,320]{1,0:T(8,128)(2,1)} %get-tuple-element.52.dq_ref, bf16[512,320]{1,0:T(8,128)(2,1)} %bitcast.15, ...), custom_call_target="tpu_custom_call" | custom-call | tf_op jit(solution)/shard_map/tail/pallas_call | solution.py:700
  305.9 6.5 %pack.1 = bf16[32,162,320]{2,1,0:T(8,128)(2,1)} custom-call(f32[320,320]{1,0:T(8,128)} %get-tuple-element.56.gwq, f32[1280,320]{1,0:T(8,128)} %get-tuple-element.57.gwr, f32[320,320]{1,0:T(8,128)} %get-tuple-element.58.gwk, f32[320,320]{1,0:T(8,128)} %get-tuple-element.59.gwv, f32[320,320]{1,0:T(8,128)} %get-tuple-element.60.gwo, ...), custom_call_target="tpu_custom_call" | custom-call | tf_op jit(solution)/shard_map/pack/pallas_call | solution.py:177
  312.4 0.0 reduce-scatter.7.cloned.1.call-update
  312.4 97.8 %reduce-scatter.7.cloned.1.call-done = bf16[1,162,320]{2,1,0:T(8,128)(2,1)} async-done(((bf16[32,162,320]{2,1,0:T(8,128)(2,1)}), bf16[1,162,320]{2,1,0:T(8,128)(2,1)}) %reduce-scatter.7.cloned.1.call-update) | async-done | bytes 103696
  410.3 1.7 reshape.30
Async XLA Ops:
  7.2 68.4 %all-gather.4.cloned.1.call-start = ((), (), s32[]{:S(2)}) async-start(), calls=%async_computation.2 | async-start | bytes 4257792 | tf_op jit(solution)/shard_map/all_gather | solution.py:723
  8.9 96.9 %all-gather.6.cloned.1.call-start = ((), (), s32[]{:S(2)}) async-start(), calls=%async_computation.4 | async-start | bytes 1966080 | tf_op jit(solution)/shard_map/all_gather | solution.py:762
  87.2 208.1 %reduce-scatter.5.cloned.1.call-start = ((), (), s32[]{:S(2)}) async-start(), calls=%async_computation.3 | async-start | bytes 1966080 | tf_op jit(solution)/shard_map/reduce_scatter | solution.py:774
  135.6 11.6 %collective-permute-start.1 = (bf16[2,2,64,320]{3,2,1,0:T(8,128)(2,1)S(1)}, bf16[2,2,64,320]{3,2,1,0:T(8,128)(2,1)S(1)}, u32[]{:S(2)}, u32[]{:S(2)}) collective-permute-start(bf16[2,2,64,320]{3,2,1,0:T(8,128)(2,1)S(1)} %get-tuple-element.69), channel_id=1, source_target_pairs={{1,0},{2,1},{3,2},{5,4},{6,5},{7,6},{9,8},{10,9},{11,10},{13,12},{... | collective-permute-start | bytes 491528 | tf_op jit(solution)/shard_map/ppermute | solution.py:748
  136.9 10.3 %collective-permute-start = (bf16[2,2,64,320]{3,2,1,0:T(8,128)(2,1)S(1)}, bf16[2,2,64,320]{3,2,1,0:T(8,128)(2,1)S(1)}, u32[]{:S(2)}, u32[]{:S(2)}) collective-permute-start(bf16[2,2,64,320]{3,2,1,0:T(8,128)(2,1)S(1)} %get-tuple-element.70), channel_id=1, source_target_pairs={{0,1},{1,2},{2,3},{4,5},{5,6},{6,7},{8,9},{9,10},{10,11},{12,13},{... | collective-permute-start | bytes 491528 | tf_op jit(solution)/shard_map/ppermute | solution.py:745
  140.9 6.1 %collective-permute-start.3 = (bf16[2,1,64,320]{3,2,1,0:T(8,128)(2,1)S(1)}, bf16[2,1,64,320]{3,2,1,0:T(8,128)(2,1)S(1)}, u32[]{:S(2)}, u32[]{:S(2)}) collective-permute-start(bf16[2,1,64,320]{3,2,1,0:T(8,128)(2,1)S(1)} %get-tuple-element.67), channel_id=1, source_target_pairs={{1,0},{2,1},{3,2},{5,4},{6,5},{7,6},{9,8},{10,9},{11,10},{13,12},{... | collective-permute-start | bytes 245768 | tf_op jit(solution)/shard_map/ppermute | solution.py:748
  142.2 4.9 %collective-permute-start.2 = (bf16[2,1,64,320]{3,2,1,0:T(8,128)(2,1)S(1)}, bf16[2,1,64,320]{3,2,1,0:T(8,128)(2,1)S(1)}, u32[]{:S(2)}, u32[]{:S(2)}) collective-permute-start(bf16[2,1,64,320]{3,2,1,0:T(8,128)(2,1)S(1)} %get-tuple-element.68), channel_id=1, source_target_pairs={{0,1},{1,2},{2,3},{4,5},{5,6},{6,7},{8,9},{9,10},{10,11},{12,13},{... | collective-permute-start | bytes 245768 | tf_op jit(solution)/shard_map/ppermute | solution.py:745
  147.0 0.6 copy-start.2
  147.2 0.7 copy-start.3
  147.2 0.7 copy-start
  147.2 0.8 copy-start.1
  262.9 147.3 %reduce-scatter.7.cloned.1.call-start = ((), (), s32[]{:S(2)}) async-start(), calls=%async_computation.5 | async-start | bytes 4257792
Sparse Core Ops, SparseCore 0:
  11.4 64.1 all-gather.3
  87.3 18.4 all-gather.5
  263.0 32.1 reduce-scatter.4
  312.6 97.6 reduce-scatter.6
where the time goes:
time: 419 us
  waiting for transfers between devices  216 us (52%)
  Pallas kernels  172 us (41%)
  between operations  13.8 us (3%)
  starting transfers between devices  9.99 us (2%)
  local copies, waits for them, and re-layouts  6.21 us (1%)
    unnamed x5, waiting for transfers between devices  97.9 us
    pallas_call x1, Pallas kernels, mix(): pl.pallas_call(mix_kernel, name='mix', grid=(FF // CH,), in_specs=[whole(...  75.8 us
    all_gather x1, waiting for transfers between devices, gather_params(): lax.all_gather(params.reshape(BLOCK_ROWS, C), ('dp', 'space'), axis=0, ti...  66.6 us
    pallas_call x1, Pallas kernels, attend_back(): pl.pallas_call(attend_back_kernel, name='attend_back', grid=(scenes, step...  39.1 us
    reduce_scatter x1, waiting for transfers between devices, on_device(): grn = lax.psum_scatter(grn_all, 'space', scatter_dimension=0, tiled=False)  32.3 us
    pallas_call x1, Pallas kernels, attend(): pl.pallas_call(attend_kernel, name='attend', grid=(scenes, steps), in_spe...  28.7 us
    all_gather x1, waiting for transfers between devices, on_device(): rn_all = lax.all_gather(rn, 'space', axis=0, tiled=False)  18.5 us
    pallas_call x1, Pallas kernels, tail(): pl.pallas_call(tail_kernel, name='tail', grid=(tokens // TILE,), in_specs...  10.7 us
  transfers between devices with their start and end apart: 8, of which 5 were waited for; matrix products, arithmetic and copies ran while one was open for 0% of the time, Pallas kernels for 0%

commit v1 on v0

--- a/solution.py
+++ b/solution.py
@@ -356,17 +356,23 @@
     wrow = ws[...]
     bias = hid[0:1, :]
     top, low = edge[0], edge[1]
+
+    def inside(value, there):
+        return jnp.where(there > 0, value, 0.0)
+
     for s in range(scenes):
         body = mm(n2[s].reshape(own, C), wcol) + bias
         e_scr[s * ext + 2 * W : s * ext + 2 * W + own, :] = body.astype(BF16).astype(F32)
         part = mm(n2_top[s].reshape(2 * W, C), wcol) + bias
-        e_scr[s * ext : s * ext + 2 * W, :] = part.astype(BF16).astype(F32) * top
+        e_scr[s * ext : s * ext + 2 * W, :] = inside(part.astype(BF16).astype(F32), top)
         part = mm(n2_low[s].reshape(2 * W, C), wcol) + bias
-        e_scr[s * ext + 2 * W + own : (s + 1) * ext, :] = part.astype(BF16).astype(F32) * low
+        e_scr[s * ext + 2 * W + own : (s + 1) * ext, :] = inside(
+            part.astype(BF16).astype(F32), low
+        )
         ga_scr[s * gext + W : s * gext + W + own, :] = mm_nt(cot[s].reshape(own, C), wrow)
-        ga_scr[s * gext : s * gext + W, :] = mm_nt(cot_top[s].reshape(W, C), wrow) * top
-        ga_scr[s * gext + W + own : (s + 1) * gext, :] = (
-            mm_nt(cot_low[s].reshape(W, C), wrow) * low
+        ga_scr[s * gext : s * gext + W, :] = inside(mm_nt(cot_top[s].reshape(W, C), wrow), top)
+        ga_scr[s * gext + W + own : (s + 1) * gext, :] = inside(
+            mm_nt(cot_low[s].reshape(W, C), wrow), low
         )
     col = lax.broadcasted_iota(jnp.int32, (W, 128), 0)
     first, last = col == 0, col == W - 1
@@ -716,11 +722,497 @@
     )(x, gmid, dq, grn, red, vec, wq, wr)
 
 
+ANY = pl.BlockSpec(memory_space=pl.ANY)
+VM = pl.BlockSpec(memory_space=pltpu.VMEM)
+
+
+def flip(value, by):
+    return value + by * (1 - 2 * value)
+
+
+def remote(src, dst, send, recv, where):
+    return pltpu.make_async_remote_copy(
+        src_ref=src,
+        dst_ref=dst,
+        send_sem=send,
+        recv_sem=recv,
+        device_id=where,
+        device_id_type=pl.DeviceIdType.MESH,
+    )
+
+
+def greet(places):
+    barrier = pltpu.get_barrier_semaphore()
+    count = 0
+    for place, there in places:
+        if there is None:
+            pl.semaphore_signal(
+                barrier, inc=1, device_id=place, device_id_type=pl.DeviceIdType.MESH
+            )
+            count = count + 1
+        else:
+
+            @pl.when(there)
+            def _():
+                pl.semaphore_signal(
+                    barrier, inc=1, device_id=place, device_id_type=pl.DeviceIdType.MESH
+                )
+
+            count = count + there.astype(jnp.int32)
+    pl.semaphore_wait(barrier, count)
+
+
+def comm_params(number):
+    return pltpu.CompilerParams(
+        collective_id=number, has_side_effects=True, vmem_limit_bytes=60 * 1024 * 1024
+    )
+
+
+class Place:
+    def __init__(self):
+        dp, space = lax.axis_index("dp"), lax.axis_index("space")
+        self.z, self.x = dp // 2, dp % 2
+        self.y, self.c = space // 2, space % 2
+        self.line = lax.axis_size("dp") // 2
+
+    def block(self, z, x, y, c):
+        return ((z * 2 + x) * 2 + y) * 2 + c
+
+    def device(self, z, x, y, c):
+        return {"dp": z * 2 + x, "space": y * 2 + c}
+
+    def spot(self, da, db, c):
+        return (
+            flip(self.x, da * (1 - c) + db * c),
+            flip(self.y, db * (1 - c) + da * c),
+        )
+
+    def partners(self):
+        ax, ay = self.spot(1, 0, self.c)
+        bx, by = self.spot(0, 1, self.c)
+        return (
+            self.device(self.z, ax, ay, self.c),
+            self.device(self.z, bx, by, self.c),
+            self.device(self.z, self.x, self.y, 1 - self.c),
+            self.device(self.z + 1, self.x, self.y, self.c),
+            self.device(self.z - 1, self.x, self.y, self.c),
+        )
+
+    def meet(self):
+        first, second, sibling, up, down = self.partners()
+        greet(
+            [
+                (first, None),
+                (second, None),
+                (sibling, None),
+                (up, self.z < self.line - 1),
+                (down, self.z > 0),
+            ]
+        )
+
+
+def gather_kernel(own, out, up_sem, down_sem, a_sem, b_sem, c_sem, recv):
+    at = Place()
+    line = at.line
+    first, second, sibling, up, down = at.partners()
+    at.meet()
+    can_up, can_down = at.z < line - 1, at.z > 0
+
+    def block_of(z, da, db):
+        x, y = at.spot(da, db, at.c)
+        return at.block(z, x, y, at.c)
+
+    def push(index, src, sem, where):
+        remote(src, out.at[index], sem, recv.at[index], where).start()
+
+    def landed(index):
+        remote(out.at[index], out.at[index], c_sem.at[0], recv.at[index], sibling).wait_recv()
+
+    def slot_sends(z, da, db, src):
+        index = block_of(z, da, db)
+        if da == 0 and db == 0:
+            push(index, src, a_sem.at[z], first)
+        if db == 0:
+            push(index, src, b_sem.at[da * line + z], second)
+        push(index, src, c_sem.at[(da * 2 + db) * line + z], sibling)
+
+    mine = block_of(at.z, 0, 0)
+
+    @pl.when(can_up)
+    def _():
+        push(mine, own, up_sem.at[at.z], up)
+
+    @pl.when(can_down)
+    def _():
+        push(mine, own, down_sem.at[at.z], down)
+
+    slot_sends(at.z, 0, 0, own)
+    out[mine] = own[...]
+
+    def along(da, db, act):
+        for d in range(1, line):
+
+            @pl.when(at.z - d >= 0)
+            def _():
+                act(at.z - d, da, db, 1)
+
+            @pl.when(at.z + d < line)
+            def _():
+                act(at.z + d, da, db, -1)
+
+    def relay(z, da, db, way):
+        index = block_of(z, da, db)
+        landed(index)
+        if da == 0 and db == 0:
+            if way > 0:
+
+                @pl.when(can_up)
+                def _():
+                    push(index, out.at[index], up_sem.at[z], up)
+
+            else:
+
+                @pl.when(can_down)
+                def _():
+                    push(index, out.at[index], down_sem.at[z], down)
+
+        slot_sends(z, da, db, out.at[index])
+
+    along(0, 0, relay)
+    for da, db in ((1, 0), (0, 1), (1, 1)):
+        relay(at.z, da, db, 0)
+        along(da, db, relay)
+    for da in range(2):
+        for db in range(2):
+            for z in range(line):
+                x, y = at.spot(da, db, at.c)
+                landed(at.block(z, x, y, 1 - at.c))
+    def sent(sem, where):
+        remote(own, out.at[mine], sem, recv.at[mine], where).wait_send()
+
+    for z in range(line):
+
+        @pl.when(jnp.logical_and(can_up, z <= at.z))
+        def _():
+            sent(up_sem.at[z], up)
+
+        @pl.when(jnp.logical_and(can_down, z >= at.z))
+        def _():
+            sent(down_sem.at[z], down)
+
+        sent(a_sem.at[z], first)
+        for da in range(2):
+            sent(b_sem.at[da * line + z], second)
+            for db in range(2):
+                sent(c_sem.at[(da * 2 + db) * line + z], sibling)
+
+
+def gather_blocks(own):
+    dma = pltpu.SemaphoreType.DMA
+    return pl.pallas_call(
+        gather_kernel,
+        name="gather",
+        out_shape=shape_of((BLOCKS,) + own.shape, own.dtype),
+        in_specs=[VM],
+        out_specs=VM,
+        scratch_shapes=[dma((4,)), dma((4,)), dma((4,)), dma((8,)), dma((16,)), dma((BLOCKS,))],
+        compiler_params=comm_params(1),
+    )(own)
+
+
+def scatter_kernel(
+    parts, out, rc, acc, ra, acc2, rb, acc3, rup, rdown, sup, sdown,
+    c_sem, a_sem, b_sem, up_sem, down_sem, c_in, a_in, b_in, up_in, down_in,
+):
+    at = Place()
+    line = at.line
+    first, second, sibling, up, down = at.partners()
+    at.meet()
+    can_up, can_down = at.z < line - 1, at.z > 0
+    slots = [(da, db, z) for da in (1, 0) for db in (1, 0) for z in range(line)]
+
+    def add(left, right):
+        return (left.astype(F32) + right.astype(F32)).astype(BF16)
+
+    def c_copy(k):
+        da, db, z = slots[k]
+        x, y = at.spot(da, db, 1 - at.c)
+        return remote(
+            parts.at[at.block(z, x, y, 1 - at.c)], rc.at[k], c_sem.at[k], c_in.at[k], sibling
+        )
+
+    def a_copy(j):
+        return remote(acc.at[j], ra.at[j], a_sem.at[j], a_in.at[j], first)
+
+    def b_copy(j):
+        return remote(acc2.at[j], rb.at[j], b_sem.at[j], b_in.at[j], second)
+
+    def up_copy(z):
+        return remote(sup.at[z], rup.at[z], up_sem.at[z], up_in.at[z], up)
+
+    def down_copy(z):
+        return remote(sdown.at[z], rdown.at[z], down_sem.at[z], down_in.at[z], down)
+
+    for k in range(4 * line):
+        c_copy(k).start()
+    for k in range(4 * line):
+        c_copy(k).wait_recv()
+        da, db, z = slots[k]
+        x, y = at.spot(da, db, at.c)
+        acc[k] = add(parts[at.block(z, x, y, at.c)], rc[k])
+        if da:
+            a_copy(k).start()
+    for j in range(2 * line):
+        a_copy(j).wait_recv()
+        acc2[j] = add(acc[2 * line + j], ra[j])
+        if j < line:
+            b_copy(j).start()
+    for z in range(line):
+        b_copy(z).wait_recv()
+        acc3[z] = add(acc2[line + z], rb[z])
+    for z in reversed(range(line)):
+
+        @pl.when(z > at.z)
+        def _():
+            sup[z] = acc3[z]
+
+            @pl.when(can_down)
+            def _():
+                up_copy(z).wait_recv()
+                sup[z] = add(acc3[z], rup[z])
+
+            up_copy(z).start()
+
+        mirror = line - 1 - z
+
+        @pl.when(mirror < at.z)
+        def _():
+            sdown[mirror] = acc3[mirror]
+
+            @pl.when(can_up)
+            def _():
+                down_copy(mirror).wait_recv()
+                sdown[mirror] = add(acc3[mirror], rdown[mirror])
+
+            down_copy(mirror).start()
+
+    for z in range(line):
+
+        @pl.when(z == at.z)
+        def _():
+            out[...] = acc3[z].astype(F32)
+
+            @pl.when(can_down)
+            def _():
+                up_copy(z).wait_recv()
+                out[...] += rup[z].astype(F32)
+
+            @pl.when(can_up)
+            def _():
+                down_copy(z).wait_recv()
+                out[...] += rdown[z].astype(F32)
+
+    for k in range(4 * line):
+        c_copy(k).wait_send()
+    for j in range(2 * line):
+        a_copy(j).wait_send()
+    for z in range(line):
+        b_copy(z).wait_send()
+
+        @pl.when(z > at.z)
+        def _():
+            up_copy(z).wait_send()
+
+        @pl.when(z < at.z)
+        def _():
+            down_copy(z).wait_send()
+
+
+def scatter_blocks(parts):
+    one = parts.shape[1:]
+    dma = pltpu.SemaphoreType.DMA
+    room = lambda n: pltpu.VMEM((n,) + one, BF16)
+    return pl.pallas_call(
+        scatter_kernel,
+        name="scatter",
+        out_shape=shape_of(one, F32),
+        in_specs=[VM],
+        out_specs=VM,
+        scratch_shapes=[
+            room(16), room(16), room(8), room(8), room(4), room(4),
+            room(4), room(4), room(4), room(4),
+        ]
+        + [dma((n,)) for n in (16, 8, 4, 4, 4, 16, 8, 4, 4, 4)],
+        compiler_params=comm_params(2),
+    )(parts)
+
+
+def bands_of():
+    band = lax.axis_index("space")
+    pair, core = band // 2, band % 2
+    return band, pair * 2 + 1 - core, (1 - pair) * 2 + core
+
+
+def swap_kernel(width, value, above, below, up_sem, down_sem, up_in, down_in, ready):
+    band = lax.axis_index("space")
+    rows = value.shape[1]
+    ends = lax.axis_size("space") - 1
+    down = remote(
+        value.at[:, pl.ds(rows - width, width)], above, down_sem, down_in, {"space": band + 1}
+    )
+    up = remote(value.at[:, pl.ds(0, width)], below, up_sem, up_in, {"space": band - 1})
+
+    @pl.when(band < ends)
+    def _():
+        down.start()
+
+    @pl.when(band > 0)
+    def _():
+        up.start()
+
+    def finish():
+        @pl.when(band < ends)
+        def _():
+            down.wait_send()
+            up.wait_recv()
+
+        @pl.when(band > 0)
+        def _():
+            up.wait_send()
+            down.wait_recv()
+
+    return finish
+
+
+def bands_meet(others):
+    band = lax.axis_index("space")
+    ends = lax.axis_size("space") - 1
+    greet(
+        [({"space": o}, None) for o in others]
+        + [({"space": band + 1}, band < ends), ({"space": band - 1}, band > 0)]
+    )
+
+
+def share_kernel(
+    rn, cot, rn_all, above, below, send, recv, own_sem, up_sem, down_sem, up_in, down_in
+):
+    band, sibling, across = bands_of()
+    bands_meet((sibling, across))
+    to_sibling = remote(rn, rn_all.at[band], send.at[0], recv.at[band], {"space": sibling})
+    to_across = remote(rn, rn_all.at[band], send.at[1], recv.at[band], {"space": across})
+    to_across.start()
+    to_sibling.start()
+    own = pltpu.make_async_copy(rn, rn_all.at[band], own_sem)
+    own.start()
+    finish = swap_kernel(1, cot, above, below, up_sem, down_sem, up_in, down_in, None)
+
+    def landed(index):
+        remote(rn, rn_all.at[index], send.at[0], recv.at[index], {"space": sibling}).wait_recv()
+
+    landed(across)
+    onward = remote(
+        rn_all.at[across], rn_all.at[across], send.at[2], recv.at[across], {"space": sibling}
+    )
+    onward.start()
+    landed(sibling)
+    landed(across + sibling - band)
+    own.wait()
+    to_across.wait_send()
+    to_sibling.wait_send()
+    onward.wait_send()
+    finish()
+
+
+def share(rn, cot):
+    bands = lax.axis_size("space")
+    dma = pltpu.SemaphoreType.DMA
+    edge = (cot.shape[0], 1) + cot.shape[2:]
+    return pl.pallas_call(
+        share_kernel,
+        name="share",
+        out_shape=(
+            shape_of((bands,) + rn.shape, rn.dtype),
+            shape_of(edge, cot.dtype),
+            shape_of(edge, cot.dtype),
+        ),
+        in_specs=[VM, ANY],
+        out_specs=(ANY, ANY, ANY),
+        scratch_shapes=[dma((3,)), dma((bands,)), dma, dma, dma, dma, dma],
+        compiler_params=comm_params(3),
+    )(rn, cot)
+
+
+def halo_kernel(value, above, below, up_sem, down_sem, up_in, down_in):
+    bands_meet(())
+    swap_kernel(2, value, above, below, up_sem, down_sem, up_in, down_in, None)()
+
+
+def halo(value):
+    dma = pltpu.SemaphoreType.DMA
+    edge = (value.shape[0], 2) + value.shape[2:]
+    return pl.pallas_call(
+        halo_kernel,
+        name="halo",
+        out_shape=(shape_of(edge, value.dtype), shape_of(edge, value.dtype)),
+        in_specs=[ANY],
+        out_specs=(ANY, ANY),
+        scratch_shapes=[dma, dma, dma, dma],
+        compiler_params=comm_params(4),
+    )(value)
+
+
+def merge_kernel(parts, out, rc, acc, rb, c_sem, c_in, b_sem, b_in):
+    band, sibling, across = bands_of()
+    greet([({"space": sibling}, None), ({"space": across}, None)])
+    far = across + sibling - band
+    first = remote(parts.at[far], rc.at[0], c_sem.at[0], c_in.at[0], {"space": sibling})
+    second = remote(parts.at[sibling], rc.at[1], c_sem.at[1], c_in.at[1], {"space": sibling})
+    onward = remote(acc, rb, b_sem, b_in, {"space": across})
+    first.start()
+    second.start()
+    first.wait_recv()
+    acc[...] = (parts[across].astype(F32) + rc[0].astype(F32)).astype(BF16)
+    onward.start()
+    second.wait_recv()
+    out[...] = parts[band].astype(F32) + rc[1].astype(F32)
+    onward.wait_recv()
+    out[...] += rb[...].astype(F32)
+    first.wait_send()
+    second.wait_send()
+    onward.wait_send()
+
+
+def merge(parts):
+    one = parts.shape[1:]
+    dma = pltpu.SemaphoreType.DMA
+    return pl.pallas_call(
+        merge_kernel,
+        name="merge",
+        out_shape=shape_of(one, F32),
+        in_specs=[VM],
+        out_specs=VM,
+        scratch_shapes=[
+            pltpu.VMEM((2,) + one, BF16),
+            pltpu.VMEM(one, BF16),
+            pltpu.VMEM(one, BF16),
+            dma((2,)),
+            dma((2,)),
+            dma,
+            dma,
+        ],
+        compiler_params=comm_params(5),
+    )(parts)
+
+
+def blocks_fit(size):
+    return (
+        lax.axis_size("dp") == 8 and lax.axis_size("space") == 4 and size == BLOCK_ROWS * C
+    )
+
+
 def gather_params(params):
-    size = params.shape[0]
-    devices = lax.axis_size("dp") * lax.axis_size("space")
-    if devices == BLOCKS and size == BLOCK_ROWS * C:
-        return lax.all_gather(params.reshape(BLOCK_ROWS, C), ("dp", "space"), axis=0, tiled=False)
+    if blocks_fit(params.shape[0]):
+        return gather_blocks(params.reshape(BLOCK_ROWS, C))
     flat = lax.all_gather(params, ("dp", "space"), axis=0, tiled=True)
     want = ROWS * C
     flat = flat[:want] if flat.shape[0] >= want else jnp.pad(flat, (0, want - flat.shape[0]))
@@ -728,25 +1220,13 @@
 
 
 def scatter_grads(blocks, size):
-    devices = lax.axis_size("dp") * lax.axis_size("space")
-    if devices == BLOCKS and size == BLOCK_ROWS * C:
-        own = lax.psum_scatter(blocks, ("dp", "space"), scatter_dimension=0, tiled=False)
-        return own.astype(F32).reshape(size)
+    if blocks_fit(size):
+        return scatter_blocks(blocks).reshape(size)
     flat = blocks.reshape(-1)
-    want = size * devices
+    want = size * lax.axis_size("dp") * lax.axis_size("space")
     flat = flat[:want] if flat.shape[0] >= want else jnp.pad(flat, (0, want - flat.shape[0]))
     own = lax.psum_scatter(flat, ("dp", "space"), scatter_dimension=0, tiled=True)
     return own.astype(F32)
-
-
-def edges(value, width):
-    count = lax.axis_size("space")
-    rows = value.shape[1]
-    above = lax.ppermute(
-        value[:, rows - width :], "space", [(i, i + 1) for i in range(count - 1)]
-    )
-    below = lax.ppermute(value[:, :width], "space", [(i + 1, i) for i in range(count - 1)])
-    return above, below
 
 
 def on_device(scenes, params, cotangent):
@@ -759,20 +1239,19 @@
     wq, wr, wk, wv, wo, we, ws, vec, hid = unpack(gather_params(params))
     x = scenes.reshape(tokens, C)
     q, red, rn = front(x, vec, wq, wr)
-    rn_all = lax.all_gather(rn, "space", axis=0, tiled=False)
+    rn_all, cot_top, cot_low = share(rn, cotangent)
     rn_all = rn_all.reshape(bands, count, per_band, C)
-    cot_top, cot_low = edges(cotangent, 1)
     mixed, lse, mid, n2 = attend(x, q, rn_all, vec, wk, wv, wo)
     n2 = n2.reshape(scenes.shape)
-    n2_top, n2_low = edges(n2, 2)
+    n2_top, n2_low = halo(n2)
     y, gmid, gwe, gws, ghid, gvec2 = mix(
         n2, n2_top, n2_low, cotangent, cot_top, cot_low, mid, edge, vec, hid, we, ws
     )
     dq, grn_all, gwk, gwv, gwo, gvec1 = attend_back(
         q, lse, mixed, gmid, rn_all, vec, wk, wv, wo
     )
-    grn = lax.psum_scatter(grn_all, "space", scatter_dimension=0, tiled=False)
-    gx, gwq, gwr, gvec0 = tail(x, gmid, dq, grn.reshape(-1, C), red, vec, wq, wr)
+    grn = merge(grn_all.reshape(bands, count * per_band, C))
+    gx, gwq, gwr, gvec0 = tail(x, gmid, dq, grn, red, vec, wq, wr)
     blocks = pack(gwq, gwr, gwk, gwv, gwo, gwe, gws, gvec0, gvec1, gvec2, ghid)
     shard = scatter_grads(blocks, params.shape[0])
     return y.reshape(scenes.shape), gx.reshape(scenes.shape), shard

time: 419 us -> 286 us (0.68)
  waiting for transfers between devices: 216 us -> 0 us
  Pallas kernels: 172 us -> 281 us
  between operations: 13.8 us -> 0.69 us
  starting transfers between devices: 9.99 us -> 0 us
    pallas_call x0 -> x5, Pallas kernels: none -> 108 us  [the longest x1 42.3 us: scatter_blocks(): pl.pallas_call(scatter_kernel, name='scatter', out_shape=shape_of(one, F3...]
    unnamed x5 -> x0, waiting for transfers between devices: 97.9 us -> none
    all_gather x2 -> x0, waiting for transfers between devices: 85.2 us -> none  [the longest x1 66.6 us: gather_params(): lax.all_gather(params.reshape(BLOCK_ROWS, C), ('dp', 'space'), axis=0, ti...]
    reduce_scatter x1 -> x0, waiting for transfers between devices: 32.3 us -> none  [on_device(): grn = lax.psum_scatter(grn_all, 'space', scatter_dimension=0, tiled=False)]
    ppermute x4 -> x0, starting transfers between devices: 9.82 us -> none  [the longest x2 7.24 us: edges(): lax.ppermute(value[:, rows - width:], 'space', [(i, i + 1) for i in range...]
  transfers between devices with their start and end apart: 8 -> 0, of which waited for: 5 -> 0; matrix products, arithmetic and copies ran while one was open for 0% -> 0% of each run, Pallas kernels for 0% -> 0%
where the time goes in v1:
time: 286 us; the launch traced here: 285 us
  Pallas kernels  281 us (98%)
  local copies, waits for them, and re-layouts  3.46 us (1%)
    pallas_call x1, Pallas kernels, mix(): pl.pallas_call(mix_kernel, name='mix', grid=(FF // CH,), in_specs=[whole(...  75.9 us
    pallas_call x1, Pallas kernels, scatter_blocks(): pl.pallas_call(scatter_kernel, name='scatter', out_shape=shape_of(one, F3...  42.3 us
    pallas_call x1, Pallas kernels, attend_back(): pl.pallas_call(attend_back_kernel, name='attend_back', grid=(scenes, step...  39.1 us
    pallas_call x1, Pallas kernels, gather_blocks(): pl.pallas_call(gather_kernel, name='gather', out_shape=shape_of((BLOCKS,)...  31.1 us
    pallas_call x1, Pallas kernels, attend(): pl.pallas_call(attend_kernel, name='attend', grid=(scenes, steps), in_spe...  28.8 us
    pallas_call x1, Pallas kernels, merge(): pl.pallas_call(merge_kernel, name='merge', out_shape=shape_of(one, F32),...  17.6 us
    pallas_call x1, Pallas kernels, share(): pl.pallas_call(share_kernel, name='share', out_shape=(shape_of((bands,) +...  14.3 us
    pallas_call x1, Pallas kernels, tail(): pl.pallas_call(tail_kernel, name='tail', grid=(tokens // TILE,), in_specs...  10.8 us

profile of v1, /device:TPU:0, one launch (start us, length us, event | category | flops | bytes accessed | tf_op | source)
XLA Modules:
  0.0 285.3 jit_solution(13358142688739432370)
XLA Ops:
  0.6 0.6 add_convert_fusion.edge
  1.2 1.7 reshape.31.own
  2.9 31.1 %gather.1.g_ref = bf16[32,162,320]{2,1,0:T(8,128)(2,1)} custom-call(bf16[162,320]{1,0:T(8,128)(2,1)} %reshape.31.own), custom_call_target="tpu_custom_call" | custom-call | tf_op jit(solution)/shard_map/gather/pallas_call | solution.py:912
  34.0 5.0 %unpack.1 = (bf16[320,320]{1,0:T(8,128)(2,1)}, bf16[1280,320]{1,0:T(8,128)(2,1)}, bf16[320,320]{1,0:T(8,128)(2,1)}, bf16[320,320]{1,0:T(8,128)(2,1)}, bf16[320,3...) custom-call(bf16[32,162,320]{2,1,0:T(8,128)(2,1)} %gather.1.g_ref), custom_call_target="tpu_custom_call" | custom-call | tf_op jit(solution)/shard_map/unpack/pallas_call | solution.py:119
  39.0 6.6 %front.1 = (bf16[2048,320]{1,0:T(8,128)(2,1)}, f32[512,320]{1,0:T(8,128)}, bf16[512,320]{1,0:T(8,128)(2,1)}) custom-call(bf16[2048,320]{1,0:T(8,128)(2,1)} %bitcast.8, f32[16,320]{1,0:T(8,128)} %get-tuple-element.40.vec, bf16[320,320]{1,0:T(8,128)(2,1)} %get-tuple-element.41.wq, bf16[1280,320]{1,0:T(8,128)(2,1)} %get-tuple-element.42.wr), custom_call_target="tpu_custom_call" | custom-call | tf_op jit(solution)/shard_map/front/pallas_call | solution.py:226
  45.5 14.3 %share.1 = (bf16[4,512,320]{2,1,0:T(8,128)(2,1)}, bf16[2,1,64,320]{3,2,1,0:T(8,128)(2,1)}, bf16[2,1,64,320]{3,2,1,0:T(8,128)(2,1)}) custom-call(bf16[512,320]{1,0:T(8,128)(2,1)} %get-tuple-element.44.rn, bf16[2,16,64,320]{3,2,1,0:T(8,128)(2,1)} %cot.3), custom_call_target="tpu_custom_call" | custom-call | tf_op jit(solution)/shard_map/share/pallas_call | solution.py:1130
  59.9 28.8 %attend.1 = (bf16[2048,320]{1,0:T(8,128)(2,1)}, f32[2048,128]{1,0:T(8,128)}, f32[2048,320]{1,0:T(8,128)}, bf16[2048,320]{1,0:T(8,128)(2,1)}) custom-call(bf16[2048,320]{1,0:T(8,128)(2,1)} %bitcast.9, bf16[2048,320]{1,0:T(8,128)(2,1)} %get-tuple-element.43.q_ref, bf16[4,2,256,320]{3,2,1,0:T(8,128)(2,1)} %bitcast.13, f32[16,320]{1,0:T(8,128)} %get-tuple-element.40.vec, ...), custom_call_target="tpu_custom_call" | custom-call | tf_op jit(solution)/shard_map/attend/pallas_call | solution.py:296
  88.6 2.8 halo.1
  91.5 75.9 %mix.1 = (bf16[2048,320]{1,0:T(8,128)(2,1)}, f32[2048,320]{1,0:T(8,128)}, f32[320,1280]{1,0:T(8,128)}, f32[1280,320]{1,0:T(8,128)}, f32[16,1280]{1,0:T(8,128)}, /*index=5*/f32[8,320]{1,0:T(8,128)}) custom-call(bf16[2,16,64,320]{3,2,1,0:T(8,128)(2,1)} %bitcast.12, bf16[2,2,64,320]{3,2,1,0:T(8,128)(2,1)} %get-tuple-element.50.n2_top, ...), custom_call_target="tpu_custom_call" | custom-call | tf_op jit(solution)/shard_map/mix/pallas_call | solution.py:503
  167.4 39.1 %attend_back.1 = (bf16[2048,320]{1,0:T(8,128)(2,1)}, bf16[4,2,256,320]{3,2,1,0:T(8,128)(2,1)}, f32[320,320]{1,0:T(8,128)}, f32[320,320]{1,0:T(8,128)}, f32[320,320]{1,0:T(8,128)}, /*index=5*/f32[8,320]{1,0:T(8,128)}) custom-call(bf16[2048,320]{1,0:T(8,128)(2,1)} %get-tuple-element.43.q_ref, f32[2048,128]{1,0:T(8,128)} %get-tuple-element.60.lse_ref, ...), custom_call_target="tpu_custom_call" | custom-call | tf_op jit(solution)/shard_map/attend_back/pallas_call | solution.py:617
  206.4 17.6 %merge.1.grn_ref = f32[512,320]{1,0:T(8,128)} custom-call(bf16[4,512,320]{2,1,0:T(8,128)(2,1)} %bitcast.15), custom_call_target="tpu_custom_call" | custom-call | tf_op jit(solution)/shard_map/merge/pallas_call | solution.py:1188
  224.0 10.8 %tail.1 = (f32[2048,320]{1,0:T(8,128)}, f32[320,320]{1,0:T(8,128)}, f32[1280,320]{1,0:T(8,128)}, f32[8,320]{1,0:T(8,128)}) custom-call(bf16[2048,320]{1,0:T(8,128)(2,1)} %bitcast.10, f32[2048,320]{1,0:T(8,128)} %get-tuple-element.59.gmid_ref, bf16[2048,320]{1,0:T(8,128)(2,1)} %get-tuple-element.62.dq_ref, f32[512,320]{1,0:T(8,128)} %merge.1.grn_ref, ...), custom_call_target="tpu_custom_call" | custom-call | tf_op jit(solution)/shard_map/tail/pallas_call | solution.py:706
  234.8 6.5 %pack.1.parts = bf16[32,162,320]{2,1,0:T(8,128)(2,1)} custom-call(f32[320,320]{1,0:T(8,128)} %get-tuple-element.66.gwq, f32[1280,320]{1,0:T(8,128)} %get-tuple-element.67.gwr, f32[320,320]{1,0:T(8,128)} %get-tuple-element.68.gwk, f32[320,320]{1,0:T(8,128)} %get-tuple-element.69.gwv, f32[320,320]{1,0:T(8,128)} %get-tuple-element.70.gwo, ...), custom_call_target="tpu_custom_call" | custom-call | tf_op jit(solution)/shard_map/pack/pallas_call | solution.py:177
  241.2 42.3 %scatter.1 = f32[162,320]{1,0:T(8,128)} custom-call(bf16[32,162,320]{2,1,0:T(8,128)(2,1)} %pack.1.parts), custom_call_target="tpu_custom_call" | custom-call | tf_op jit(solution)/shard_map/scatter/pallas_call | solution.py:1035
  283.5 1.8 reshape.37

commit v2 on v1

--- a/solution.py
+++ b/solution.py
@@ -154,7 +154,7 @@
     put_strided(R_KEYVAL, 2, gwk[...])
     put_strided(R_KEYVAL + 1, 2, gwv[...])
     put(R_OUTPUT, gwo[...])
-    put(R_SHRINK, gws[...])
+    put(R_SHRINK, gws[...].T)
     for j in range(4):
         put_strided(R_EXPAND + j, 4, gwe[:, C * j : C * j + C])
         put_strided(R_HIDDEN + j, 4, ghid[0:HIDDEN_ROWS, C * j : C * j + C])
@@ -326,142 +326,148 @@
 CH = 256
 
 
-def gelu_parts(x):
-    size = jnp.abs(x)
-    t = 1.0 / (1.0 + (0.3275911 * math.sqrt(0.5)) * size)
-    poly = t * (
-        0.5 * 0.254829592
-        + t
-        * (
-            0.5 * -0.284496736
-            + t * (0.5 * 1.421413741 + t * (0.5 * -1.453152027 + t * (0.5 * 1.061405429)))
-        )
-    )
-    bell = jnp.exp(-0.5 * (x * x))
-    tail = poly * bell
-    return jnp.where(x >= 0, 1.0 - tail, tail), bell * (1.0 / math.sqrt(2.0 * math.pi))
+SHRINK_IN = math.sqrt(0.5 * math.log2(math.e))
+SLOPE = 1.0 / (math.sqrt(2.0 * math.pi) * SHRINK_IN)
+ACT_SCALE = SLOPE / SHRINK_IN
+ERF_RATE = 0.3275911 * math.sqrt(0.5) / SHRINK_IN
+ERF_TERMS = [
+    0.5 * k / SLOPE
+    for k in (0.254829592, -0.284496736, 1.421413741, -1.453152027, 1.061405429)
+]
+
+
+def gelu_parts(u):
+    size = jnp.abs(u)
+    t = 1.0 / (1.0 + ERF_RATE * size)
+    poly = ERF_TERMS[4]
+    for term in ERF_TERMS[3::-1]:
+        poly = term + t * poly
+    bell = jnp.exp2(-(u * u))
+    tail = (t * poly) * bell
+    return jnp.where(u >= 0, 1.0 / SLOPE - tail, tail), bell
 
 
 def mix_kernel(
     n2, n2_top, n2_low, cot, cot_top, cot_low, mid, edge, vec, hid, we, ws,
     y_out, gmid_out, gwe_out, gws_out, ghid_out, gvec_out,
-    e_scr, ga_scr, gc_scr, act_scr, ge_scr, branch, gn2,
+    nx, cx, nt, ct, e_scr, e_low, ga_scr, gc_scr, act_scr, ge_scr, branch, gn2,
 ):
     step = pl.program_id(0)
     scenes, rows = n2.shape[0], n2.shape[1]
     ext = (rows + 4) * W
     gext = (rows + 2) * W
     own = rows * W
+    top, low = edge[0], edge[1]
+
+    @pl.when(step == 0)
+    def _():
+        def inside(value, there):
+            return jnp.where(there > 0, value.astype(F32), 0.0).astype(BF16)
+
+        for s in range(scenes):
+            mine = n2[s].reshape(own, C)
+            nx[s * ext : s * ext + 2 * W, :] = n2_top[s].reshape(2 * W, C)
+            nx[s * ext + 2 * W : s * ext + 2 * W + own, :] = mine
+            nx[s * ext + 2 * W + own : (s + 1) * ext, :] = n2_low[s].reshape(2 * W, C)
+            nt[0:C, s * own : (s + 1) * own] = mine.T
+            mine = cot[s].reshape(own, C)
+            cx[s * gext : s * gext + W, :] = inside(cot_top[s].reshape(W, C), top)
+            cx[s * gext + W : s * gext + W + own, :] = mine
+            cx[s * gext + W + own : (s + 1) * gext, :] = inside(cot_low[s].reshape(W, C), low)
+            ct[:, s * own : (s + 1) * own] = mine.T
+        nt[C:, :] = jnp.ones((16, scenes * own), BF16)
+        branch[...] = jnp.zeros_like(branch)
+        gn2[...] = jnp.zeros_like(gn2)
+
     wcol = we[...]
     wrow = ws[...]
-    bias = hid[0:1, :]
-    top, low = edge[0], edge[1]
-
-    def inside(value, there):
-        return jnp.where(there > 0, value, 0.0)
+    body = (mm(nx[...], wcol) + hid[0:1, :]).astype(BF16)
+    e_low[...] = body
+    e_scr[...] = body.astype(F32)
+    ga_scr[...] = mm_nt(cx[...], wrow)
+    for there, start in ((top, 0), (low, 2 * W + own)):
+
+        @pl.when(there == 0)
+        def _():
+            for s in range(scenes):
+                e_scr[s * ext + start : s * ext + start + 2 * W, :] = jnp.zeros((2 * W, CH), F32)
+
+    col = lax.broadcasted_iota(jnp.int32, (8, CH), 0)
+    first, last = col == 0, col == 7
+
+    def right(value):
+        moved = pltpu.roll(value, 1, axis=0)
+        return jnp.concatenate([jnp.where(first, 0.0, moved[0:8]), moved[8:]], axis=0)
+
+    def left(value):
+        moved = pltpu.roll(value, W - 1, axis=0)
+        return jnp.concatenate([moved[: W - 8], jnp.where(last, 0.0, moved[W - 8 :])], axis=0)
+
+    def fold(value):
+        value = value[0:32] + value[32:64]
+        value = value[0:16] + value[16:32]
+        return (value[0:8] + value[8:16]).astype(F32)
+
+    taps = [hid[1 + k : 2 + k, :] * SHRINK_IN for k in range(9)]
+    low_taps = [hid[1 + k : 2 + k, :].astype(BF16) for k in range(9)]
+    conv_bias = hid[10:11, :] * SHRINK_IN
 
     for s in range(scenes):
-        body = mm(n2[s].reshape(own, C), wcol) + bias
-        e_scr[s * ext + 2 * W : s * ext + 2 * W + own, :] = body.astype(BF16).astype(F32)
-        part = mm(n2_top[s].reshape(2 * W, C), wcol) + bias
-        e_scr[s * ext : s * ext + 2 * W, :] = inside(part.astype(BF16).astype(F32), top)
-        part = mm(n2_low[s].reshape(2 * W, C), wcol) + bias
-        e_scr[s * ext + 2 * W + own : (s + 1) * ext, :] = inside(
-            part.astype(BF16).astype(F32), low
-        )
-        ga_scr[s * gext + W : s * gext + W + own, :] = mm_nt(cot[s].reshape(own, C), wrow)
-        ga_scr[s * gext : s * gext + W, :] = inside(mm_nt(cot_top[s].reshape(W, C), wrow), top)
-        ga_scr[s * gext + W + own : (s + 1) * gext, :] = inside(
-            mm_nt(cot_low[s].reshape(W, C), wrow), low
-        )
-    col = lax.broadcasted_iota(jnp.int32, (W, 128), 0)
-    first, last = col == 0, col == W - 1
-
-    def right(value):
-        return jnp.where(first, 0.0, pltpu.roll(value, 1, axis=0))
-
-    def left(value):
-        return jnp.where(last, 0.0, pltpu.roll(value, W - 1, axis=0))
-
-    def fold(value):
-        return jnp.sum(value.reshape(W // 8, 8, 128), axis=0)
-
-    for half in range(CH // 128):
-        lanes = slice(half * 128, half * 128 + 128)
-        taps = [hid[1 + k : 2 + k, lanes] for k in range(9)]
-        conv_bias = hid[10:11, lanes]
-
-        for s in range(scenes):
-
-            def forward(r, carry):
-                at = pl.multiple_of(s * ext + r * W, W)
-                lines = [e_scr[pl.ds(at + a * W, W), lanes] for a in range(3)]
-                sums = [
-                    lines[0] * taps[b] + lines[1] * taps[3 + b] + lines[2] * taps[6 + b]
-                    for b in range(3)
-                ]
-                conv = conv_bias + right(sums[0]) + sums[1] + left(sums[2])
-                cdf, density = gelu_parts(conv)
-                gat = pl.multiple_of(s * gext + r * W, W)
-                gc = ga_scr[pl.ds(gat, W), lanes] * (cdf + conv * density)
-                gc = gc.astype(BF16).astype(F32)
-                act_scr[pl.ds(gat, W), lanes] = (conv * cdf).astype(BF16)
-                gc_scr[0, pl.ds(gat, W), lanes] = left(gc)
-                gc_scr[1, pl.ds(gat, W), lanes] = gc
-                gc_scr[2, pl.ds(gat, W), lanes] = right(gc)
-                return carry
-
-            lax.fori_loop(0, rows + 2, forward, 0)
-
-        def backward(s, r, carry):
-            line = e_scr[pl.ds(pl.multiple_of(s * ext + (r + 2) * W, W), W), lanes]
-            grads = list(carry)
-            total = None
-            for a in range(3):
-                gat = pl.multiple_of(s * gext + (r + 2 - a) * W, W)
-                for b in range(3):
-                    g = gc_scr[b, pl.ds(gat, W), lanes]
-                    term = g * taps[3 * a + b]
-                    total = term if total is None else total + term
-                    grads[3 * a + b] = grads[3 * a + b] + fold(g * line)
-                    if a == 1 and b == 1:
-                        grads[9] = grads[9] + fold(g)
-            total = total.astype(BF16)
-            ge_scr[pl.ds(pl.multiple_of(s * own + r * W, W), W), lanes] = total
-            grads[10] = grads[10] + fold(total.astype(F32))
-            return tuple(grads)
-
-        sums = tuple(jnp.zeros((8, 128), F32) for _ in range(11))
-        for s in range(scenes):
-            sums = lax.fori_loop(0, rows, functools.partial(backward, s), sums)
-        ghid_out[0:1, lanes] = row_sum(sums[10])
-        for k in range(10):
-            ghid_out[1 + k : 2 + k, lanes] = row_sum(sums[k])
-
-    gwe = gws = None
+
+        def forward(r, carry):
+            at = pl.multiple_of(s * ext + r * W, W)
+            lines = [e_scr[pl.ds(at + a * W, W), :] for a in range(3)]
+            sums = [
+                lines[0] * taps[b] + lines[1] * taps[3 + b] + lines[2] * taps[6 + b]
+                for b in range(3)
+            ]
+            u = conv_bias + right(sums[0]) + sums[1] + left(sums[2])
+            cdf, bell = gelu_parts(u)
+            gat = pl.multiple_of(s * gext + r * W, W)
+            gc = ga_scr[pl.ds(gat, W), :] * (cdf + u * bell)
+            act_scr[pl.ds(gat, W), :] = (u * cdf).astype(BF16)
+            gc_scr[0, pl.ds(gat, W), :] = left(gc).astype(BF16)
+            gc_scr[1, pl.ds(gat, W), :] = gc.astype(BF16)
+            gc_scr[2, pl.ds(gat, W), :] = right(gc).astype(BF16)
+            return carry
+
+        lax.fori_loop(0, rows + 2, forward, 0)
+
+    def backward(s, r, carry):
+        line = e_low[pl.ds(pl.multiple_of(s * ext + (r + 2) * W, W), W), :]
+        grads = list(carry)
+        total = None
+        for a in range(3):
+            gat = pl.multiple_of(s * gext + (r + 2 - a) * W, W)
+            for b in range(3):
+                g = gc_scr[b, pl.ds(gat, W), :]
+                term = g * low_taps[3 * a + b]
+                total = term if total is None else total + term
+                grads[3 * a + b] = grads[3 * a + b] + fold(g * line)
+                if a == 1 and b == 1:
+                    grads[9] = grads[9] + fold(g)
+        ge_scr[pl.ds(pl.multiple_of(s * own + r * W, W), W), :] = total
+        return tuple(grads)
+
+    sums = tuple(jnp.zeros((8, CH), F32) for _ in range(10))
     for s in range(scenes):
+        sums = lax.fori_loop(0, rows, functools.partial(backward, s), sums)
+    for k in range(10):
+        ghid_out[1 + k : 2 + k, :] = row_sum(sums[k]) * SLOPE
+
+    ge = ge_scr[...]
+    grads = mm(nt[...], ge)
+    gwe_out[...] = grads[0:C, :] * SLOPE
+    ghid_out[0:1, :] = grads[C : C + 1, :] * SLOPE
+    gn2[...] += mm_nt(ge, wcol)
+    gws = None
+    for s in range(scenes):
+        at = slice(s * own, (s + 1) * own)
         act = act_scr[s * gext + W : s * gext + W + own, :]
-        ge = ge_scr[s * own : (s + 1) * own, :]
-        term = mm_tn(act, cot[s].reshape(own, C))
+        branch[at, :] += mm(act, wrow)
+        term = mm(ct[:, at], act)
         gws = term if gws is None else gws + term
-        term = mm_tn(n2[s].reshape(own, C), ge)
-        gwe = term if gwe is None else gwe + term
-        out_part = mm(act, wrow)
-        in_part = mm_nt(ge, wcol)
-        at = slice(s * own, (s + 1) * own)
-
-        @pl.when(step == 0)
-        def _():
-            branch[at, :] = out_part
-            gn2[at, :] = in_part
-
-        @pl.when(step > 0)
-        def _():
-            branch[at, :] += out_part
-            gn2[at, :] += in_part
-
-    gws_out[...] = gws
-    gwe_out[...] = gwe
+    gws_out[...] = gws * ACT_SCALE
 
     @pl.when(step == pl.num_programs(0) - 1)
     def _():
@@ -475,9 +481,9 @@
             line = (i % per) * 4
             middle = mid[pl.ds(at, size), :]
             y_out[pl.ds(at, size), :] = (
-                middle + branch[pl.ds(at, size), :] + vec[V_SHRINK : V_SHRINK + 1, :]
+                middle + branch[pl.ds(at, size), :] * ACT_SCALE + vec[V_SHRINK : V_SHRINK + 1, :]
             ).astype(BF16)
-            grad = gn2[pl.ds(at, size), :]
+            grad = gn2[pl.ds(at, size), :] * SLOPE
             unit, rstd = norm_parts(middle)
             direct = cot[s, pl.ds(line, 4)].reshape(size, C).astype(F32)
             gmid_out[pl.ds(at, size), :] = direct + norm_back(grad, unit, rstd, gain)
@@ -522,7 +528,7 @@
             full((tokens, C)),
             full((tokens, C)),
             pl.BlockSpec((C, CH), lambda j: (0, j)),
-            pl.BlockSpec((CH, C), lambda j: (j, 0)),
+            pl.BlockSpec((C, CH), lambda j: (0, j)),
             pl.BlockSpec((16, CH), lambda j: (0, j)),
             full((8, C)),
         ],
@@ -530,14 +536,19 @@
             shape_of((tokens, C), BF16),
             shape_of((tokens, C), F32),
             shape_of((C, FF), F32),
-            shape_of((FF, C), F32),
+            shape_of((C, FF), F32),
             shape_of((16, FF), F32),
             shape_of((8, C), F32),
         ),
         scratch_shapes=[
+            pltpu.VMEM((ext, C), BF16),
+            pltpu.VMEM((gext, C), BF16),
+            pltpu.VMEM((C + 16, tokens), BF16),
+            pltpu.VMEM((C, tokens), BF16),
             pltpu.VMEM((ext, CH), F32),
+            pltpu.VMEM((ext, CH), BF16),
             pltpu.VMEM((gext, CH), F32),
-            pltpu.VMEM((3, gext, CH), F32),
+            pltpu.VMEM((3, gext, CH), BF16),
             pltpu.VMEM((gext, CH), BF16),
             pltpu.VMEM((tokens, CH), BF16),
             pltpu.VMEM((tokens, C), F32),

time: 286 us -> 271 us (0.948)
  Pallas kernels: 281 us -> 266 us
    pallas_call x1, Pallas kernels: 75.9 us -> 61.1 us  [mix(): pl.pallas_call(mix_kernel, name='mix', grid=(FF // CH,), in_specs=[whole(...]
where the time goes in v2:
time: 271 us
  Pallas kernels  266 us (98%)
  local copies, waits for them, and re-layouts  3.46 us (1%)
    pallas_call x1, Pallas kernels, mix(): pl.pallas_call(mix_kernel, name='mix', grid=(FF // CH,), in_specs=[whole(...  61.1 us
    pallas_call x1, Pallas kernels, scatter_blocks(): pl.pallas_call(scatter_kernel, name='scatter', out_shape=shape_of(one, F3...  42.4 us
    pallas_call x1, Pallas kernels, attend_back(): pl.pallas_call(attend_back_kernel, name='attend_back', grid=(scenes, step...  39.1 us
    pallas_call x1, Pallas kernels, gather_blocks(): pl.pallas_call(gather_kernel, name='gather', out_shape=shape_of((BLOCKS,)...  31.1 us
    pallas_call x1, Pallas kernels, attend(): pl.pallas_call(attend_kernel, name='attend', grid=(scenes, steps), in_spe...  28.8 us
    pallas_call x1, Pallas kernels, merge(): pl.pallas_call(merge_kernel, name='merge', out_shape=shape_of(one, F32),...  17.6 us
    pallas_call x1, Pallas kernels, share(): pl.pallas_call(share_kernel, name='share', out_shape=(shape_of((bands,) +...  14.3 us
    pallas_call x1, Pallas kernels, tail(): pl.pallas_call(tail_kernel, name='tail', grid=(tokens // TILE,), in_specs...  10.7 us

profile of v2, /device:TPU:0, one launch (start us, length us, event | category | flops | bytes accessed | tf_op | source)
XLA Modules:
  0.0 270.9 jit_solution(14448395437770598894)
XLA Ops:
  0.6 0.6 add_convert_fusion.edge
  1.2 1.7 reshape.31.own
  2.9 31.1 %gather.1.g_ref = bf16[32,162,320]{2,1,0:T(8,128)(2,1)} custom-call(bf16[162,320]{1,0:T(8,128)(2,1)} %reshape.31.own), custom_call_target="tpu_custom_call" | custom-call | tf_op jit(solution)/shard_map/gather/pallas_call | solution.py:923
  34.0 5.0 %unpack.1 = (bf16[320,320]{1,0:T(8,128)(2,1)}, bf16[1280,320]{1,0:T(8,128)(2,1)}, bf16[320,320]{1,0:T(8,128)(2,1)}, bf16[320,320]{1,0:T(8,128)(2,1)}, bf16[320,3...) custom-call(bf16[32,162,320]{2,1,0:T(8,128)(2,1)} %gather.1.g_ref), custom_call_target="tpu_custom_call" | custom-call | tf_op jit(solution)/shard_map/unpack/pallas_call | solution.py:119
  39.0 6.6 %front.1 = (bf16[2048,320]{1,0:T(8,128)(2,1)}, f32[512,320]{1,0:T(8,128)}, bf16[512,320]{1,0:T(8,128)(2,1)}) custom-call(bf16[2048,320]{1,0:T(8,128)(2,1)} %bitcast.8, f32[16,320]{1,0:T(8,128)} %get-tuple-element.40.vec, bf16[320,320]{1,0:T(8,128)(2,1)} %get-tuple-element.41.wq, bf16[1280,320]{1,0:T(8,128)(2,1)} %get-tuple-element.42.wr), custom_call_target="tpu_custom_call" | custom-call | tf_op jit(solution)/shard_map/front/pallas_call | solution.py:226
  45.6 14.3 %share.1 = (bf16[4,512,320]{2,1,0:T(8,128)(2,1)}, bf16[2,1,64,320]{3,2,1,0:T(8,128)(2,1)}, bf16[2,1,64,320]{3,2,1,0:T(8,128)(2,1)}) custom-call(bf16[512,320]{1,0:T(8,128)(2,1)} %get-tuple-element.44.rn, bf16[2,16,64,320]{3,2,1,0:T(8,128)(2,1)} %cot.3), custom_call_target="tpu_custom_call" | custom-call | tf_op jit(solution)/shard_map/share/pallas_call | solution.py:1141
  59.9 28.8 %attend.1 = (bf16[2048,320]{1,0:T(8,128)(2,1)}, f32[2048,128]{1,0:T(8,128)}, f32[2048,320]{1,0:T(8,128)}, bf16[2048,320]{1,0:T(8,128)(2,1)}) custom-call(bf16[2048,320]{1,0:T(8,128)(2,1)} %bitcast.9, bf16[2048,320]{1,0:T(8,128)(2,1)} %get-tuple-element.43.q_ref, bf16[4,2,256,320]{3,2,1,0:T(8,128)(2,1)} %bitcast.13, f32[16,320]{1,0:T(8,128)} %get-tuple-element.40.vec, ...), custom_call_target="tpu_custom_call" | custom-call | tf_op jit(solution)/shard_map/attend/pallas_call | solution.py:296
  88.7 2.7 %halo.1 = (bf16[2,2,64,320]{3,2,1,0:T(8,128)(2,1)}, bf16[2,2,64,320]{3,2,1,0:T(8,128)(2,1)}) custom-call(bf16[2,16,64,320]{3,2,1,0:T(8,128)(2,1)} %bitcast.11), custom_call_target="tpu_custom_call" | custom-call | tf_op jit(solution)/shard_map/halo/pallas_call | solution.py:1164
  91.5 61.1 %mix.1 = (bf16[2048,320]{1,0:T(8,128)(2,1)}, f32[2048,320]{1,0:T(8,128)}, f32[320,1280]{1,0:T(8,128)}, f32[320,1280]{1,0:T(8,128)}, f32[16,1280]{1,0:T(8,128)}, /*index=5*/f32[8,320]{1,0:T(8,128)}) custom-call(bf16[2,16,64,320]{3,2,1,0:T(8,128)(2,1)} %bitcast.12, bf16[2,2,64,320]{3,2,1,0:T(8,128)(2,1)} %get-tuple-element.50.n2_top, ...), custom_call_target="tpu_custom_call" | custom-call | tf_op jit(solution)/shard_map/mix/pallas_call | solution.py:509
  152.6 39.1 %attend_back.1 = (bf16[2048,320]{1,0:T(8,128)(2,1)}, bf16[4,2,256,320]{3,2,1,0:T(8,128)(2,1)}, f32[320,320]{1,0:T(8,128)}, f32[320,320]{1,0:T(8,128)}, f32[320,320]{1,0:T(8,128)}, /*index=5*/f32[8,320]{1,0:T(8,128)}) custom-call(bf16[2048,320]{1,0:T(8,128)(2,1)} %get-tuple-element.43.q_ref, f32[2048,128]{1,0:T(8,128)} %get-tuple-element.60.lse_ref, ...), custom_call_target="tpu_custom_call" | custom-call | tf_op jit(solution)/shard_map/attend_back/pallas_call | solution.py:628
  191.7 17.6 %merge.1.grn_ref = f32[512,320]{1,0:T(8,128)} custom-call(bf16[4,512,320]{2,1,0:T(8,128)(2,1)} %bitcast.15), custom_call_target="tpu_custom_call" | custom-call | tf_op jit(solution)/shard_map/merge/pallas_call | solution.py:1199
  209.2 10.7 %tail.1 = (f32[2048,320]{1,0:T(8,128)}, f32[320,320]{1,0:T(8,128)}, f32[1280,320]{1,0:T(8,128)}, f32[8,320]{1,0:T(8,128)}) custom-call(bf16[2048,320]{1,0:T(8,128)(2,1)} %bitcast.10, f32[2048,320]{1,0:T(8,128)} %get-tuple-element.59.gmid_ref, bf16[2048,320]{1,0:T(8,128)(2,1)} %get-tuple-element.62.dq_ref, f32[512,320]{1,0:T(8,128)} %merge.1.grn_ref, ...), custom_call_target="tpu_custom_call" | custom-call | tf_op jit(solution)/shard_map/tail/pallas_call | solution.py:717
  220.0 6.8 %pack.1.parts = bf16[32,162,320]{2,1,0:T(8,128)(2,1)} custom-call(f32[320,320]{1,0:T(8,128)} %get-tuple-element.66.gwq, f32[1280,320]{1,0:T(8,128)} %get-tuple-element.67.gwr, f32[320,320]{1,0:T(8,128)} %get-tuple-element.68.gwk, f32[320,320]{1,0:T(8,128)} %get-tuple-element.69.gwv, f32[320,320]{1,0:T(8,128)} %get-tuple-element.70.gwo, ...), custom_call_target="tpu_custom_call" | custom-call | tf_op jit(solution)/shard_map/pack/pallas_call | solution.py:177
  226.8 42.4 %scatter.1 = f32[162,320]{1,0:T(8,128)} custom-call(bf16[32,162,320]{2,1,0:T(8,128)(2,1)} %pack.1.parts), custom_call_target="tpu_custom_call" | custom-call | tf_op jit(solution)/shard_map/scatter/pallas_call | solution.py:1046
  269.2 1.8 reshape.37

commit v3 on v2

--- a/solution.py
+++ b/solution.py
@@ -91,7 +91,7 @@
 def unpack_kernel(g_ref, wq, wr, wk, wv, wo, we, ws, vec, hid, rows, tiles):
     for i in range(BLOCKS):
         at = i * BLOCK_ROWS
-        block = g_ref[i].astype(F32)
+        block = restore(g_ref[i].astype(F32).reshape(2 * PART, 128))
         rows[at : at + BLOCK_ROWS, :] = block
         tiles[0, at : at + BLOCK_ROWS, :] = block[:, 0:128]
         tiles[1, at : at + BLOCK_ROWS, :] = block[:, 128:256]
@@ -151,8 +151,8 @@
 
     put(R_QUERY, gwq[...])
     put(R_REDUCE, gwr[...])
-    put_strided(R_KEYVAL, 2, gwk[...])
-    put_strided(R_KEYVAL + 1, 2, gwv[...])
+    put_strided(R_KEYVAL, 2, gwk[...].T)
+    put_strided(R_KEYVAL + 1, 2, gwv[...].T)
     put(R_OUTPUT, gwo[...])
     put(R_SHRINK, gws[...].T)
     for j in range(4):
@@ -160,24 +160,33 @@
         put_strided(R_HIDDEN + j, 4, ghid[0:HIDDEN_ROWS, C * j : C * j + C])
     for source, names in (
         (gvec0, (V_QUERY, V_REDUCE, V_RGAIN, V_RSHIFT, V_GAIN1, V_SHIFT1)),
-        (gvec1, (V_VALUE, V_OUTPUT)),
         (gvec2, (V_GAIN2, V_SHIFT2, V_SHRINK)),
     ):
         for i, name in enumerate(names):
             put(VECTOR_ROWS[name], source[i : i + 1, :])
+    put(VECTOR_ROWS[V_VALUE], gvec1[0:1, :])
+    put(VECTOR_ROWS[V_OUTPUT], gvec1[8:9, :])
     put(USED_ROWS, jnp.zeros((ROWS - USED_ROWS, C), F32))
+    half = BLOCK_ROWS // 2
+    spare = jnp.zeros((2 * PART - 2 * BLOCK_ROWS - half, 128), F32)
     for i in range(BLOCKS):
         at = i * BLOCK_ROWS
-        out[i, :, 0:128] = tiles[0, at : at + BLOCK_ROWS, :].astype(BF16)
-        out[i, :, 128:256] = tiles[1, at : at + BLOCK_ROWS, :].astype(BF16)
-        out[i, :, 256:320] = tiles[2, at : at + BLOCK_ROWS, 0:64].astype(BF16)
+        tail = jnp.concatenate(
+            [
+                tiles[2, at : at + half, 0:64],
+                tiles[2, at + half : at + BLOCK_ROWS, 0:64],
+            ],
+            axis=1,
+        )
+        rows = [tiles[0, at : at + BLOCK_ROWS, :], tiles[1, at : at + BLOCK_ROWS, :], tail, spare]
+        out[i] = jnp.concatenate(rows, axis=0).reshape(2, PART, 128).astype(BF16)
 
 
 def pack(*pieces):
     return pl.pallas_call(
         pack_kernel,
         name="pack",
-        out_shape=shape_of((BLOCKS, BLOCK_ROWS, C), BF16),
+        out_shape=shape_of((BLOCKS, 2, PART, 128), BF16),
         scratch_shapes=[pltpu.VMEM((3, ROWS, 128), F32)],
         compiler_params=PARAMS,
     )(*pieces)
@@ -248,11 +257,12 @@
     )(x, vec, wq, wr)
 
 
-QT = 256
+QT = 512
 
 
 def attend_kernel(
-    x_ref, q_ref, rn_ref, vec, wk, wv, wo, mixed_out, lse_out, mid_out, n2_out, kt, vones
+    x_ref, q_ref, rn_ref, vec, wk, wv, wo,
+    mixed_out, inv_out, mid_out, n2_out, p_out, key_out, vt_out, kt, vones,
 ):
     keys = rn_ref.shape[0] * rn_ref.shape[2]
 
@@ -261,24 +271,26 @@
         rn = rn_ref[:, 0].reshape(keys, C)
         key = mm(rn, wk[...]).astype(BF16)
         value = (mm(rn, wv[...]) + vec[V_VALUE : V_VALUE + 1, :]).astype(BF16)
+        key_out[0] = key
+        vt_out[0] = value.T
         kt[...] = key.T
         for h in range(HEADS):
             vones[h, :, 0:HD] = value[:, h * HD : (h + 1) * HD]
             vones[h, :, HD:] = jnp.ones((keys, HD), BF16)
 
-    lane = lax.broadcasted_iota(jnp.int32, (QT, 128), 1)
-    lses = jnp.zeros((QT, 128), F32)
-    outs = []
+    outs, invs = [], []
     for h in range(HEADS):
         scores = mm(q_ref[:, h * HD : (h + 1) * HD], kt[h * HD : (h + 1) * HD, :])
         top = jnp.max(scores, axis=-1, keepdims=True)
         probs = jnp.exp(scores - top).astype(BF16)
+        p_out[0, h] = probs
         both = mm(probs, vones[h])
-        outs.append(both[:, 0:HD] / both[:, HD:])
-        lses = jnp.where(lane == h, top + jnp.log(both[:, HD : HD + 1]), lses)
+        inv = 1.0 / both[:, HD:]
+        outs.append(both[:, 0:HD] * inv)
+        invs.append(inv)
+    inv_out[...] = jnp.concatenate(invs, axis=1)
     mixed = jnp.concatenate(outs, axis=1).astype(BF16)
     mixed_out[...] = mixed
-    lse_out[...] = lses
     middle = x_ref[...].astype(F32) + mm(mixed, wo[...]) + vec[V_OUTPUT : V_OUTPUT + 1, :]
     mid_out[...] = middle
     unit, _ = norm_parts(middle)
@@ -291,15 +303,16 @@
     tokens = x.shape[0]
     bands, scenes, per_band, _ = rn_all.shape
     keys = bands * per_band
-    steps = tokens // scenes // QT
-    tile = lambda s, i: (s * steps + i, 0)
+    per_scene = tokens // scenes
+    steps = per_scene // QT
+    tile = pl.BlockSpec((QT, C), lambda s, i: (s * steps + i, 0))
     return pl.pallas_call(
         attend_kernel,
         name="attend",
         grid=(scenes, steps),
         in_specs=[
-            pl.BlockSpec((QT, C), tile),
-            pl.BlockSpec((QT, C), tile),
+            tile,
+            tile,
             pl.BlockSpec((bands, 1, per_band, C), lambda s, i: (0, s, 0, 0)),
             full((16, C)),
             full((C, C)),
@@ -307,16 +320,22 @@
             full((C, C)),
         ],
         out_specs=[
-            pl.BlockSpec((QT, C), tile),
-            pl.BlockSpec((QT, 128), tile),
-            pl.BlockSpec((QT, C), tile),
-            pl.BlockSpec((QT, C), tile),
+            tile,
+            tile,
+            tile,
+            tile,
+            pl.BlockSpec((1, HEADS, QT, keys), lambda s, i: (s, 0, i, 0)),
+            pl.BlockSpec((1, keys, C), lambda s, i: (s, 0, 0)),
+            pl.BlockSpec((1, C, keys), lambda s, i: (s, 0, 0)),
         ],
         out_shape=(
             shape_of((tokens, C), BF16),
-            shape_of((tokens, 128), F32),
+            shape_of((tokens, C), F32),
             shape_of((tokens, C), F32),
             shape_of((tokens, C), BF16),
+            shape_of((scenes, HEADS, per_scene, keys), BF16),
+            shape_of((scenes, keys, C), BF16),
+            shape_of((scenes, C, keys), BF16),
         ),
         scratch_shapes=[pltpu.VMEM((C, keys), BF16), pltpu.VMEM((HEADS, keys, 2 * HD), BF16)],
         compiler_params=PARAMS,
@@ -558,95 +577,90 @@
     )(n2, n2_top, n2_low, cot, cot_top, cot_low, mid, edge, vec, hid, we, ws)
 
 
+QTB = 256
+
+
 def attend_back_kernel(
-    q_ref, lse_ref, mixed_ref, gmid_ref, rn_ref, vec, wk, wv, wo,
-    dq_out, grn_out, gwk_out, gwv_out, gwo_out, gvec_out,
-    kt, vt, kh, dkt, dvt,
+    q_ref, inv_ref, mixed_ref, gmid_ref, p_ref, key_ref, vt_ref, rn_ref, wk, wv, wo,
+    dq_out, grn_out, gwk_out, gwv_out, gwo_out, gvec_out, kh, dkt, dvt,
 ):
     scene, step = pl.program_id(0), pl.program_id(1)
     keys = rn_ref.shape[0] * rn_ref.shape[2]
-    start = jnp.logical_and(scene == 0, step == 0)
-
-    @pl.when(start)
+
+    @pl.when(jnp.logical_and(scene == 0, step == 0))
     def _():
         for ref in (gwk_out, gwv_out, gwo_out, gvec_out):
             ref[...] = jnp.zeros_like(ref)
 
     @pl.when(step == 0)
     def _():
-        rn = rn_ref[:, 0].reshape(keys, C)
-        key = mm(rn, wk[...]).astype(BF16)
-        value = (mm(rn, wv[...]) + vec[V_VALUE : V_VALUE + 1, :]).astype(BF16)
-        kt[...] = key.T
-        vt[...] = value.T
         for h in range(HEADS):
-            kh[h] = key[:, h * HD : (h + 1) * HD]
+            kh[h] = key_ref[0, :, h * HD : (h + 1) * HD]
         dkt[...] = jnp.zeros_like(dkt)
         dvt[...] = jnp.zeros_like(dvt)
 
-    gmid = gmid_ref[...]
-    gatt = gmid.astype(BF16)
-    gvec_out[1:2, :] += row_sum(gatt.astype(F32))
+    gatt = gmid_ref[...].astype(BF16)
+    gvec_out[8:9, :] += row_sum(gatt.astype(F32))
     mixed = mixed_ref[...]
     gwo_out[...] += mm_tn(mixed, gatt)
-    gmixed = mm_nt(gatt, wo[...]).astype(BF16)
-    prod = gmixed.astype(F32) * mixed.astype(F32)
-    q = q_ref[...]
-    q_t = q.T
-    g_t = gmixed.T
+    scaled = (mm_nt(gatt, wo[...]) * inv_ref[...]).astype(BF16)
+    prod = scaled.astype(F32) * mixed.astype(F32)
+    q_t = q_ref[...].T
+    g_t = scaled.T
     dqs = []
     for h in range(HEADS):
         cols = slice(h * HD, (h + 1) * HD)
         inner = jnp.sum(prod[:, cols], axis=-1, keepdims=True)
-        probs = jnp.exp(mm(q[:, cols], kt[cols, :]) - lse_ref[:, h : h + 1])
-        gprobs = mm(gmixed[:, cols], vt[cols, :])
-        gscores = (probs * (gprobs - inner)).astype(BF16)
+        probs = p_ref[0, h]
+        gprobs = mm(scaled[:, cols], vt_ref[0, cols, :])
+        gscores = (probs.astype(F32) * (gprobs - inner)).astype(BF16)
         dqs.append(mm(gscores, kh[h]))
         dkt[cols, :] += mm(q_t[cols, :], gscores)
-        dvt[cols, :] += mm(g_t[cols, :], probs.astype(BF16))
+        dvt[cols, :] += mm(g_t[cols, :], probs)
     dq_out[...] = (jnp.concatenate(dqs, axis=1) * (1.0 / math.sqrt(HD))).astype(BF16)
 
     @pl.when(step == pl.num_programs(1) - 1)
     def _():
         rn = rn_ref[:, 0].reshape(keys, C)
-        dk = dkt[...].T.astype(BF16)
-        dv = dvt[...].T
-        gvec_out[0:1, :] += row_sum(dv)
-        dv = dv.astype(BF16)
-        gwk_out[...] += mm_tn(rn, dk)
-        gwv_out[...] += mm_tn(rn, dv)
-        grn = mm_nt(dk, wk[...]) + mm_nt(dv, wv[...])
-        grn_out[...] = grn.astype(BF16).reshape(grn_out.shape)
-
-
-def attend_back(q, lse, mixed, gmid, rn_all, vec, wk, wv, wo):
+        dk = dkt[...].astype(BF16)
+        dv = dvt[...].astype(BF16)
+        gvec_out[0:8, :] += mm_nt(jnp.ones((8, keys), BF16), dv)
+        gwk_out[...] += mm(dk, rn)
+        gwv_out[...] += mm(dv, rn)
+        grn = (mm(wk[...], dk) + mm(wv[...], dv)).astype(BF16)
+        grn_out[...] = grn.T.reshape(grn_out.shape)
+
+
+def attend_back(q, inv, mixed, gmid, p, key, vt, rn_all, wk, wv, wo):
     tokens = q.shape[0]
     bands, scenes, per_band, _ = rn_all.shape
     keys = bands * per_band
-    steps = tokens // scenes // QT
-    tile = lambda s, i: (s * steps + i, 0)
+    steps = tokens // scenes // QTB
+    tile = pl.BlockSpec((QTB, C), lambda s, i: (s * steps + i, 0))
     return pl.pallas_call(
         attend_back_kernel,
         name="attend_back",
         grid=(scenes, steps),
         in_specs=[
-            pl.BlockSpec((QT, C), tile),
-            pl.BlockSpec((QT, 128), tile),
-            pl.BlockSpec((QT, C), tile),
-            pl.BlockSpec((QT, C), tile),
+            tile,
+            tile,
+            tile,
+            tile,
+            pl.BlockSpec((1, HEADS, QTB, keys), lambda s, i: (s, 0, i, 0)),
+            pl.BlockSpec((1, keys, C), lambda s, i: (s, 0, 0)),
+            pl.BlockSpec((1, C, keys), lambda s, i: (s, 0, 0)),
             pl.BlockSpec((bands, 1, per_band, C), lambda s, i: (0, s, 0, 0)),
-            full((16, C)),
             full((C, C)),
             full((C, C)),
             full((C, C)),
         ],
         out_specs=[
-            pl.BlockSpec((QT, C), tile),
+            tile,
             pl.BlockSpec((bands, 1, per_band, C), lambda s, i: (0, s, 0, 0)),
             full((C, C)),
             full((C, C)),
             full((C, C)),
-            full((8, C)),
+            full((16, C)),
         ],
         out_shape=(
             shape_of((tokens, C), BF16),
@@ -654,17 +668,15 @@
             shape_of((C, C), F32),
             shape_of((C, C), F32),
             shape_of((C, C), F32),
-            shape_of((8, C), F32),
+            shape_of((16, C), F32),
         ),
         scratch_shapes=[
-            pltpu.VMEM((C, keys), BF16),
-            pltpu.VMEM((C, keys), BF16),
             pltpu.VMEM((HEADS, keys, HD), BF16),
             pltpu.VMEM((C, keys), F32),
             pltpu.VMEM((C, keys), F32),
         ],
         compiler_params=PARAMS,
-    )(q, lse, mixed, gmid, rn_all, vec, wk, wv, wo)
+    )(q, inv, mixed, gmid, p, key, vt, rn_all, wk, wv, wo)
 
 
 def tail_kernel(
@@ -822,238 +834,396 @@
         )
 
 
-def gather_kernel(own, out, up_sem, down_sem, a_sem, b_sem, c_sem, recv):
+DMA = pltpu.SemaphoreType.DMA
+PART = 208
+
+
+def compact(block):
+    half = BLOCK_ROWS // 2
+    tail = jnp.concatenate([block[:half, 256:], block[half:, 256:]], axis=1)
+    spare = jnp.zeros((2 * PART - 2 * BLOCK_ROWS - half, 128), block.dtype)
+    return jnp.concatenate([block[:, 0:128], block[:, 128:256], tail, spare], axis=0)
+
+
+def restore(rows):
+    half = BLOCK_ROWS // 2
+    tail = rows[2 * BLOCK_ROWS : 2 * BLOCK_ROWS + half]
+    return jnp.concatenate(
+        [
+            rows[:BLOCK_ROWS],
+            rows[BLOCK_ROWS : 2 * BLOCK_ROWS],
+            jnp.concatenate([tail[:, 0:64], tail[:, 64:128]], axis=0),
+        ],
+        axis=1,
+    )
+
+
+PLANE = [(da, db) for da in range(2) for db in range(2)]
+
+
+def gather_kernel(own_ref, out, own, p_z, p_a, p_b, p_c, q_z, q_a, q_b, q_c, recv):
     at = Place()
     line = at.line
     first, second, sibling, up, down = at.partners()
+    own[...] = compact(own_ref[...].astype(F32)).reshape(2, PART, 128).astype(BF16)
     at.meet()
     can_up, can_down = at.z < line - 1, at.z > 0
 
-    def block_of(z, da, db):
+    def index_of(z, da, db, c):
         x, y = at.spot(da, db, at.c)
-        return at.block(z, x, y, at.c)
-
-    def push(index, src, sem, where):
-        remote(src, out.at[index], sem, recv.at[index], where).start()
-
-    def landed(index):
-        remote(out.at[index], out.at[index], c_sem.at[0], recv.at[index], sibling).wait_recv()
-
-    def slot_sends(z, da, db, src):
-        index = block_of(z, da, db)
+        return at.block(z, x, y, c)
+
+    def push(part, index, src, sem, where):
+        remote(src, out.at[index, part], sem, recv.at[index, part], where).start()
+
+    def landed(part, index):
+        remote(
+            out.at[index, part], out.at[index, part], p_a.at[0], recv.at[index, part], sibling
+        ).wait_recv()
+
+    def here(part, index, is_own):
+        return own.at[part] if is_own else out.at[index, part]
+
+    def along_z(part, z, k, index, src, way, sems):
+        if way >= 0:
+
+            @pl.when(can_up)
+            def _():
+                push(part, index, src, sems.at[0, k, z], up)
+
+        if way <= 0:
+
+            @pl.when(can_down)
+            def _():
+                push(part, index, src, sems.at[1, k, z], down)
+
+    def first_order(z, da, db, way, is_own=False):
+        index = index_of(z, da, db, at.c)
+        if not is_own:
+            landed(0, index)
+        src = here(0, index, is_own)
         if da == 0 and db == 0:
-            push(index, src, a_sem.at[z], first)
+            along_z(0, z, 0, index, src, way, p_z)
+            push(0, index, src, p_a.at[z], first)
         if db == 0:
-            push(index, src, b_sem.at[da * line + z], second)
-        push(index, src, c_sem.at[(da * 2 + db) * line + z], sibling)
-
-    mine = block_of(at.z, 0, 0)
-
-    @pl.when(can_up)
-    def _():
-        push(mine, own, up_sem.at[at.z], up)
-
-    @pl.when(can_down)
-    def _():
-        push(mine, own, down_sem.at[at.z], down)
-
-    slot_sends(at.z, 0, 0, own)
+            push(0, index, src, p_b.at[da, z], second)
+        push(0, index, src, p_c.at[2 * da + db, z], sibling)
+
+    def second_order(z, da, db, way, is_own=False):
+        index = index_of(z, da, db, at.c)
+        if not is_own:
+            landed(1, index)
+        src = here(1, index, is_own)
+        if way == 0:
+            if da == 0 and db == 0:
+                push(1, index, src, q_a, first)
+            if db == 0:
+                push(1, index, src, q_b.at[da], second)
+        along_z(1, z, 2 * da + db, index, src, way, q_z)
+        push(1, index, src, q_c.at[2 * da + db, z], sibling)
+
+    def hop(d, order, places):
+        for z in range(line):
+            if z >= d:
+
+                @pl.when(at.z == z)
+                def _():
+                    for da, db in places:
+                        order(z - d, da, db, 1)
+
+            if z + d < line:
+
+                @pl.when(at.z == z)
+                def _():
+                    for da, db in places:
+                        order(z + d, da, db, -1)
+
+    def flat_hops(da, db):
+        first_order(at.z, da, db, 0)
+        for d in range(1, line):
+            hop(d, lambda z, da, db, way: first_order(z, da, db, way), [(da, db)])
+
+    second_order(at.z, 0, 0, 0, True)
+    first_order(at.z, 0, 0, 0, True)
+    mine = index_of(at.z, 0, 0, at.c)
     out[mine] = own[...]
-
-    def along(da, db, act):
-        for d in range(1, line):
-
-            @pl.when(at.z - d >= 0)
-            def _():
-                act(at.z - d, da, db, 1)
-
-            @pl.when(at.z + d < line)
-            def _():
-                act(at.z + d, da, db, -1)
-
-    def relay(z, da, db, way):
-        index = block_of(z, da, db)
-        landed(index)
-        if da == 0 and db == 0:
-            if way > 0:
-
-                @pl.when(can_up)
-                def _():
-                    push(index, out.at[index], up_sem.at[z], up)
-
-            else:
-
-                @pl.when(can_down)
-                def _():
-                    push(index, out.at[index], down_sem.at[z], down)
-
-        slot_sends(z, da, db, out.at[index])
-
-    along(0, 0, relay)
-    for da, db in ((1, 0), (0, 1), (1, 1)):
-        relay(at.z, da, db, 0)
-        along(da, db, relay)
-    for da in range(2):
-        for db in range(2):
-            for z in range(line):
-                x, y = at.spot(da, db, at.c)
-                landed(at.block(z, x, y, 1 - at.c))
-    def sent(sem, where):
-        remote(own, out.at[mine], sem, recv.at[mine], where).wait_send()
-
+    second_order(at.z, 1, 0, 0)
+    hop(1, first_order, [(0, 0)])
+    second_order(at.z, 0, 1, 0)
+    second_order(at.z, 1, 1, 0)
+    hop(2, first_order, [(0, 0)])
+    hop(1, second_order, PLANE)
+    hop(3, first_order, [(0, 0)])
+    flat_hops(1, 0)
+    hop(2, second_order, PLANE)
+    flat_hops(0, 1)
+    flat_hops(1, 1)
+    hop(3, second_order, PLANE)
     for z in range(line):
+        for da, db in PLANE:
+            for part in range(2):
+                landed(part, index_of(z, da, db, 1 - at.c))
+
+    def sent(part, sem, where):
+        remote(own.at[part], out.at[mine, part], sem, recv.at[mine, part], where).wait_send()
+
+    sent(1, q_a, first)
+    for z in range(line):
+        for k in range(4):
+            sent(0, p_c.at[k, z], sibling)
+            sent(1, q_c.at[k, z], sibling)
+        sent(0, p_a.at[z], first)
+        for da in range(2):
+            sent(0, p_b.at[da, z], second)
 
         @pl.when(jnp.logical_and(can_up, z <= at.z))
         def _():
-            sent(up_sem.at[z], up)
+            sent(0, p_z.at[0, 0, z], up)
+            for k in range(4):
+                sent(1, q_z.at[0, k, z], up)
 
         @pl.when(jnp.logical_and(can_down, z >= at.z))
         def _():
-            sent(down_sem.at[z], down)
-
-        sent(a_sem.at[z], first)
-        for da in range(2):
-            sent(b_sem.at[da * line + z], second)
-            for db in range(2):
-                sent(c_sem.at[(da * 2 + db) * line + z], sibling)
+            sent(0, p_z.at[1, 0, z], down)
+            for k in range(4):
+                sent(1, q_z.at[1, k, z], down)
+
+    for da in range(2):
+        sent(1, q_b.at[da], second)
 
 
 def gather_blocks(own):
-    dma = pltpu.SemaphoreType.DMA
     return pl.pallas_call(
         gather_kernel,
         name="gather",
-        out_shape=shape_of((BLOCKS,) + own.shape, own.dtype),
+        out_shape=shape_of((BLOCKS, 2, PART, 128), BF16),
         in_specs=[VM],
         out_specs=VM,
-        scratch_shapes=[dma((4,)), dma((4,)), dma((4,)), dma((8,)), dma((16,)), dma((BLOCKS,))],
+        scratch_shapes=[
+            pltpu.VMEM((2, PART, 128), BF16),
+            DMA((2, 1, 4)), DMA((4,)), DMA((2, 4)), DMA((4, 4)),
+            DMA((2, 4, 4)), DMA, DMA((2,)), DMA((4, 4)),
+            DMA((BLOCKS, 2)),
+        ],
         compiler_params=comm_params(1),
     )(own)
 
 
 def scatter_kernel(
-    parts, out, rc, acc, ra, acc2, rb, acc3, rup, rdown, sup, sdown,
-    c_sem, a_sem, b_sem, up_sem, down_sem, c_in, a_in, b_in, up_in, down_in,
+    parts, out,
+    rc, acc, ra, acc2, rb, acc3, rz, sz,
+    qc, qacc, qrz, qsz, qplane, qra, qacc2, qrb,
+    c_out, a_out, b_out, z_out, qc_out, qz_out, qa_out, qb_out,
+    c_in, a_in, b_in, z_in, qc_in, qz_in, qa_in, qb_in,
 ):
     at = Place()
     line = at.line
     first, second, sibling, up, down = at.partners()
     at.meet()
-    can_up, can_down = at.z < line - 1, at.z > 0
     slots = [(da, db, z) for da in (1, 0) for db in (1, 0) for z in range(line)]
 
-    def add(left, right):
-        return (left.astype(F32) + right.astype(F32)).astype(BF16)
+    def add(*terms):
+        total = terms[0].astype(F32)
+        for term in terms[1:]:
+            total = total + term.astype(F32)
+        return total.astype(BF16)
+
+    def source(k, c):
+        da, db, z = slots[k]
+        x, y = at.spot(da, db, c)
+        return at.block(z, x, y, c)
 
     def c_copy(k):
+        src = parts.at[source(k, 1 - at.c), 0]
+        return remote(src, rc.at[k], c_out.at[k], c_in.at[k], sibling)
+
+    def qc_copy(k):
+        src = parts.at[source(k, 1 - at.c), 1]
+        return remote(src, qc.at[k], qc_out.at[k], qc_in.at[k], sibling)
+
+    def a_copy(j):
+        return remote(acc.at[j], ra.at[j], a_out.at[j], a_in.at[j], first)
+
+    def b_copy(j):
+        return remote(acc2.at[j], rb.at[j], b_out.at[j], b_in.at[j], second)
+
+    def z_copy(way, z):
+        return remote(
+            sz.at[way, z], rz.at[way, z], z_out.at[way, z], z_in.at[way, z], (up, down)[way]
+        )
+
+    def qz_copy(way, k, src=None):
+        src = qsz.at[way, k] if src is None else src
+        return remote(src, qrz.at[way, k], qz_out.at[way, k], qz_in.at[way, k], (up, down)[way])
+
+    def qa_copy(j):
+        return remote(qplane.at[j], qra.at[j], qa_out.at[j], qa_in.at[j], first)
+
+    def qb_copy():
+        return remote(qacc2.at[0], qrb, qb_out, qb_in, second)
+
+    count = 4 * line
+    for k in range(count):
+        qc_copy(k).start()
+        c_copy(k).start()
+    for k in range(count):
         da, db, z = slots[k]
-        x, y = at.spot(da, db, 1 - at.c)
-        return remote(
-            parts.at[at.block(z, x, y, 1 - at.c)], rc.at[k], c_sem.at[k], c_in.at[k], sibling
-        )
-
-    def a_copy(j):
-        return remote(acc.at[j], ra.at[j], a_sem.at[j], a_in.at[j], first)
-
-    def b_copy(j):
-        return remote(acc2.at[j], rb.at[j], b_sem.at[j], b_in.at[j], second)
-
-    def up_copy(z):
-        return remote(sup.at[z], rup.at[z], up_sem.at[z], up_in.at[z], up)
-
-    def down_copy(z):
-        return remote(sdown.at[z], rdown.at[z], down_sem.at[z], down_in.at[z], down)
-
-    for k in range(4 * line):
-        c_copy(k).start()
-    for k in range(4 * line):
+        qc_copy(k).wait_recv()
+        mine = source(k, at.c)
+        qacc[k] = add(parts[mine, 1], qc[k])
+        if z > 0:
+
+            @pl.when(at.z == 0)
+            def _():
+                qz_copy(0, k, qacc.at[k]).start()
+
+        if z < line - 1:
+
+            @pl.when(at.z == line - 1)
+            def _():
+                qz_copy(1, k, qacc.at[k]).start()
+
         c_copy(k).wait_recv()
-        da, db, z = slots[k]
-        x, y = at.spot(da, db, at.c)
-        acc[k] = add(parts[at.block(z, x, y, at.c)], rc[k])
+        acc[k] = add(parts[mine, 0], rc[k])
         if da:
             a_copy(k).start()
-    for j in range(2 * line):
+
+    def q_hop(d):
+        for k in range(count):
+            z = slots[k][2]
+            if z >= d:
+
+                @pl.when(at.z == d)
+                def _():
+                    qz_copy(0, k).wait_recv()
+                    if z > d:
+                        qsz[0, k] = add(qacc[k], qrz[0, k])
+                        qz_copy(0, k).start()
+
+            if z <= line - 1 - d:
+
+                @pl.when(at.z == line - 1 - d)
+                def _():
+                    qz_copy(1, k).wait_recv()
+                    if z < line - 1 - d:
+                        qsz[1, k] = add(qacc[k], qrz[1, k])
+                        qz_copy(1, k).start()
+
+    def p_hop(d):
+        for z in reversed(range(d, line)):
+
+            @pl.when(at.z == d)
+            def _():
+                if d > 0:
+                    z_copy(0, z).wait_recv()
+                if z > d:
+                    sz[0, z] = add(acc3[z], rz[0, z]) if d > 0 else acc3[z]
+                    z_copy(0, z).start()
+
+        for z in range(line - d):
+
+            @pl.when(at.z == line - 1 - d)
+            def _():
+                if d > 0:
+                    z_copy(1, z).wait_recv()
+                if z < line - 1 - d:
+                    sz[1, z] = add(acc3[z], rz[1, z]) if d > 0 else acc3[z]
+                    z_copy(1, z).start()
+
+    def inflows(z):
+        return [way for way, there in ((0, z > 0), (1, z < line - 1)) if there]
+
+    for j in range(line):
         a_copy(j).wait_recv()
         acc2[j] = add(acc[2 * line + j], ra[j])
-        if j < line:
-            b_copy(j).start()
+        b_copy(j).start()
+    q_hop(1)
+    for j in range(line, 2 * line):
+        a_copy(j).wait_recv()
+        acc2[j] = add(acc[2 * line + j], ra[j])
+    q_hop(2)
     for z in range(line):
         b_copy(z).wait_recv()
         acc3[z] = add(acc2[line + z], rb[z])
-    for z in reversed(range(line)):
-
-        @pl.when(z > at.z)
+    p_hop(0)
+    q_hop(3)
+    for z in range(line):
+
+        @pl.when(at.z == z)
         def _():
-            sup[z] = acc3[z]
-
-            @pl.when(can_down)
-            def _():
-                up_copy(z).wait_recv()
-                sup[z] = add(acc3[z], rup[z])
-
-            up_copy(z).start()
-
-        mirror = line - 1 - z
-
-        @pl.when(mirror < at.z)
+            for j in range(4):
+                k = j * line + z
+                qplane[j] = add(qacc[k], *[qrz[way, k] for way in inflows(z)])
+
+    qa_copy(0).start()
+    qa_copy(1).start()
+    p_hop(1)
+    for j in range(2):
+        qa_copy(j).wait_recv()
+        qacc2[j] = add(qplane[2 + j], qra[j])
+        if j == 0:
+            qb_copy().start()
+    p_hop(2)
+    qb_copy().wait_recv()
+    q_total = qacc2[1].astype(F32) + qrb[...].astype(F32)
+    p_hop(3)
+    for z in range(line):
+
+        @pl.when(at.z == z)
         def _():
-            sdown[mirror] = acc3[mirror]
-
-            @pl.when(can_up)
-            def _():
-                down_copy(mirror).wait_recv()
-                sdown[mirror] = add(acc3[mirror], rdown[mirror])
-
-            down_copy(mirror).start()
-
-    for z in range(line):
-
-        @pl.when(z == at.z)
+            total = acc3[z].astype(F32)
+            for way in inflows(z):
+                total = total + rz[way, z].astype(F32)
+            out[...] = restore(jnp.concatenate([total, q_total], axis=0))
+
+    for k in range(count):
+        c_copy(k).wait_send()
+        qc_copy(k).wait_send()
+        z = slots[k][2]
+
+        @pl.when(at.z < z)
         def _():
-            out[...] = acc3[z].astype(F32)
-
-            @pl.when(can_down)
-            def _():
-                up_copy(z).wait_recv()
-                out[...] += rup[z].astype(F32)
-
-            @pl.when(can_up)
-            def _():
-                down_copy(z).wait_recv()
-                out[...] += rdown[z].astype(F32)
-
-    for k in range(4 * line):
-        c_copy(k).wait_send()
+            qz_copy(0, k).wait_send()
+
+        @pl.when(at.z > z)
+        def _():
+            qz_copy(1, k).wait_send()
+
     for j in range(2 * line):
         a_copy(j).wait_send()
     for z in range(line):
         b_copy(z).wait_send()
 
-        @pl.when(z > at.z)
+        @pl.when(at.z < z)
         def _():
-            up_copy(z).wait_send()
-
-        @pl.when(z < at.z)
+            z_copy(0, z).wait_send()
+
+        @pl.when(at.z > z)
         def _():
-            down_copy(z).wait_send()
+            z_copy(1, z).wait_send()
+
+    qa_copy(0).wait_send()
+    qa_copy(1).wait_send()
+    qb_copy().wait_send()
 
 
 def scatter_blocks(parts):
-    one = parts.shape[1:]
-    dma = pltpu.SemaphoreType.DMA
-    room = lambda n: pltpu.VMEM((n,) + one, BF16)
+    room = lambda *n: pltpu.VMEM(n + (PART, 128), BF16)
+    sems = lambda: [
+        DMA((16,)), DMA((8,)), DMA((4,)), DMA((2, 4)), DMA((16,)), DMA((2, 16)), DMA((2,)), DMA,
+    ]
     return pl.pallas_call(
         scatter_kernel,
         name="scatter",
-        out_shape=shape_of(one, F32),
+        out_shape=shape_of((BLOCK_ROWS, C), F32),
         in_specs=[VM],
         out_specs=VM,
         scratch_shapes=[
-            room(16), room(16), room(8), room(8), room(4), room(4),
-            room(4), room(4), room(4), room(4),
+            room(16), room(16), room(8), room(8), room(4), room(4), room(2, 4), room(2, 4),
+            room(16), room(16), room(2, 16), room(2, 16), room(4), room(2), room(2), room(),
         ]
-        + [dma((n,)) for n in (16, 8, 4, 4, 4, 16, 8, 4, 4, 4)],
+        + sems()
+        + sems(),
         compiler_params=comm_params(2),
     )(parts)
 
@@ -1227,13 +1397,14 @@
     flat = lax.all_gather(params, ("dp", "space"), axis=0, tiled=True)
     want = ROWS * C
     flat = flat[:want] if flat.shape[0] >= want else jnp.pad(flat, (0, want - flat.shape[0]))
-    return flat.reshape(BLOCKS, BLOCK_ROWS, C)
+    blocks = jax.vmap(compact)(flat.reshape(BLOCKS, BLOCK_ROWS, C))
+    return blocks.reshape(BLOCKS, 2, PART, 128)
 
 
 def scatter_grads(blocks, size):
     if blocks_fit(size):
         return scatter_blocks(blocks).reshape(size)
-    flat = blocks.reshape(-1)
+    flat = jax.vmap(restore)(blocks.reshape(BLOCKS, 2 * PART, 128)).reshape(-1)
     want = size * lax.axis_size("dp") * lax.axis_size("space")
     flat = flat[:want] if flat.shape[0] >= want else jnp.pad(flat, (0, want - flat.shape[0]))
     own = lax.psum_scatter(flat, ("dp", "space"), scatter_dimension=0, tiled=True)
@@ -1252,14 +1423,14 @@
     q, red, rn = front(x, vec, wq, wr)
     rn_all, cot_top, cot_low = share(rn, cotangent)
     rn_all = rn_all.reshape(bands, count, per_band, C)
-    mixed, lse, mid, n2 = attend(x, q, rn_all, vec, wk, wv, wo)
+    mixed, inv, mid, n2, p, key, vt = attend(x, q, rn_all, vec, wk, wv, wo)
     n2 = n2.reshape(scenes.shape)
     n2_top, n2_low = halo(n2)
     y, gmid, gwe, gws, ghid, gvec2 = mix(
         n2, n2_top, n2_low, cotangent, cot_top, cot_low, mid, edge, vec, hid, we, ws
     )
     dq, grn_all, gwk, gwv, gwo, gvec1 = attend_back(
-        q, lse, mixed, gmid, rn_all, vec, wk, wv, wo
+        q, inv, mixed, gmid, p, key, vt, rn_all, wk, wv, wo
     )
     grn = merge(grn_all.reshape(bands, count * per_band, C))
     gx, gwq, gwr, gvec0 = tail(x, gmid, dq, grn, red, vec, wq, wr)

time: 271 us -> 252 us (0.930)
  Pallas kernels: 266 us -> 247 us
    pallas_call x3, Pallas kernels: 80.3 us -> 69.7 us  [the longest x1 34.7 us: scatter_blocks(): pl.pallas_call(scatter_kernel, name='scatter', out_shape=shape_of((BLOCK_...]
    pallas_call x1, Pallas kernels: 39.1 us -> 31.6 us  [attend_back(): pl.pallas_call(attend_back_kernel, name='attend_back', grid=(scenes, step...]
where the time goes in v3:
time: 252 us
  Pallas kernels  247 us (98%)
  local copies, waits for them, and re-layouts  3.46 us (1%)
    pallas_call x1, Pallas kernels, mix(): pl.pallas_call(mix_kernel, name='mix', grid=(FF // CH,), in_specs=[whole(...  61.1 us
    pallas_call x1, Pallas kernels, scatter_blocks(): pl.pallas_call(scatter_kernel, name='scatter', out_shape=shape_of((BLOCK_...  34.7 us
    pallas_call x1, Pallas kernels, attend_back(): pl.pallas_call(attend_back_kernel, name='attend_back', grid=(scenes, step...  31.6 us
    pallas_call x1, Pallas kernels, gather_blocks(): pl.pallas_call(gather_kernel, name='gather', out_shape=shape_of((BLOCKS,...  28.2 us
    pallas_call x1, Pallas kernels, attend(): pl.pallas_call(attend_kernel, name='attend', grid=(scenes, steps), in_spe...  26.6 us
    pallas_call x1, Pallas kernels, merge(): pl.pallas_call(merge_kernel, name='merge', out_shape=shape_of(one, F32),...  17.6 us
    pallas_call x1, Pallas kernels, share(): pl.pallas_call(share_kernel, name='share', out_shape=(shape_of((bands,) +...  14.4 us
    pallas_call x1, Pallas kernels, tail(): pl.pallas_call(tail_kernel, name='tail', grid=(tokens // TILE,), in_specs...  11 us

profile of v3, /device:TPU:0, one launch (start us, length us, event | category | flops | bytes accessed | tf_op | source)
XLA Modules:
  0.0 251.7 jit_solution(4755235860400025570)
XLA Ops:
  0.6 0.6 add_convert_fusion.edge
  1.2 1.7 reshape.31.own_ref
  2.9 28.2 %gather.1.g_ref = bf16[32,2,208,128]{3,2,1,0:T(8,128)(2,1)} custom-call(bf16[162,320]{1,0:T(8,128)(2,1)} %reshape.31.own_ref), custom_call_target="tpu_custom_call" | custom-call | tf_op jit(solution)/shard_map/gather/pallas_call | solution.py:996
  31.1 5.3 %unpack.1 = (bf16[320,320]{1,0:T(8,128)(2,1)}, bf16[1280,320]{1,0:T(8,128)(2,1)}, bf16[320,320]{1,0:T(8,128)(2,1)}, bf16[320,320]{1,0:T(8,128)(2,1)}, bf16[320,3...) custom-call(bf16[32,2,208,128]{3,2,1,0:T(8,128)(2,1)} %gather.1.g_ref), custom_call_target="tpu_custom_call" | custom-call | tf_op jit(solution)/shard_map/unpack/pallas_call | solution.py:119
  36.4 6.6 %front.1 = (bf16[2048,320]{1,0:T(8,128)(2,1)}, f32[512,320]{1,0:T(8,128)}, bf16[512,320]{1,0:T(8,128)(2,1)}) custom-call(bf16[2048,320]{1,0:T(8,128)(2,1)} %bitcast.8, f32[16,320]{1,0:T(8,128)} %get-tuple-element.43.vec, bf16[320,320]{1,0:T(8,128)(2,1)} %get-tuple-element.44.wq, bf16[1280,320]{1,0:T(8,128)(2,1)} %get-tuple-element.45.wr), custom_call_target="tpu_custom_call" | custom-call | tf_op jit(solution)/shard_map/front/pallas_call | solution.py:235
  43.0 14.4 %share.1 = (bf16[4,512,320]{2,1,0:T(8,128)(2,1)}, bf16[2,1,64,320]{3,2,1,0:T(8,128)(2,1)}, bf16[2,1,64,320]{3,2,1,0:T(8,128)(2,1)}) custom-call(bf16[512,320]{1,0:T(8,128)(2,1)} %get-tuple-element.47.rn, bf16[2,16,64,320]{3,2,1,0:T(8,128)(2,1)} %cot.3), custom_call_target="tpu_custom_call" | custom-call | tf_op jit(solution)/shard_map/share/pallas_call | solution.py:1311
  57.4 26.6 %attend.1 = (bf16[2048,320]{1,0:T(8,128)(2,1)}, f32[2048,320]{1,0:T(8,128)}, f32[2048,320]{1,0:T(8,128)}, bf16[2048,320]{1,0:T(8,128)(2,1)}, bf16[2,5,1024,1024]...) custom-call(bf16[2048,320]{1,0:T(8,128)(2,1)} %bitcast.9, ...), custom_call_target="tpu_custom_call" | custom-call | tf_op jit(solution)/shard_map/attend/pallas_call | solution.py:309
  83.9 3.2 %halo.1 = (bf16[2,2,64,320]{3,2,1,0:T(8,128)(2,1)}, bf16[2,2,64,320]{3,2,1,0:T(8,128)(2,1)}) custom-call(bf16[2,16,64,320]{3,2,1,0:T(8,128)(2,1)} %bitcast.13), custom_call_target="tpu_custom_call" | custom-call | tf_op jit(solution)/shard_map/halo/pallas_call | solution.py:1334
  87.1 61.1 %mix.1 = (bf16[2048,320]{1,0:T(8,128)(2,1)}, f32[2048,320]{1,0:T(8,128)}, f32[320,1280]{1,0:T(8,128)}, f32[320,1280]{1,0:T(8,128)}, f32[16,1280]{1,0:T(8,128)}, /*index=5*/f32[8,320]{1,0:T(8,128)}) custom-call(bf16[2,16,64,320]{3,2,1,0:T(8,128)(2,1)} %bitcast.14, bf16[2,2,64,320]{3,2,1,0:T(8,128)(2,1)} %get-tuple-element.53.n2_top, ...), custom_call_target="tpu_custom_call" | custom-call | tf_op jit(solution)/shard_map/mix/pallas_call | solution.py:528
  148.3 31.6 %attend_back.1 = (bf16[2048,320]{1,0:T(8,128)(2,1)}, bf16[4,2,256,320]{3,2,1,0:T(8,128)(2,1)}, f32[320,320]{1,0:T(8,128)}, f32[320,320]{1,0:T(8,128)}, f32[320,320]{1,0:T(8,128)}, /*index=5*/f32[16,320]{1,0:T(8,128)}) custom-call(bf16[2048,320]{1,0:T(8,128)(2,1)} %get-tuple-element.46.q_ref, f32[2048,320]{1,0:T(8,128)} %get-tuple-element.63.inv_ref, ...), custom_call_target="tpu_custom_call" | custom-call | tf_op jit(solution)/shard_map/attend_back/pallas_call | solution.py:640
  179.9 17.6 %merge.1.grn_ref = f32[512,320]{1,0:T(8,128)} custom-call(bf16[4,512,320]{2,1,0:T(8,128)(2,1)} %bitcast.15), custom_call_target="tpu_custom_call" | custom-call | tf_op jit(solution)/shard_map/merge/pallas_call | solution.py:1369
  197.4 11.0 %tail.1 = (f32[2048,320]{1,0:T(8,128)}, f32[320,320]{1,0:T(8,128)}, f32[1280,320]{1,0:T(8,128)}, f32[8,320]{1,0:T(8,128)}) custom-call(bf16[2048,320]{1,0:T(8,128)(2,1)} %bitcast.10, f32[2048,320]{1,0:T(8,128)} %get-tuple-element.62.gmid_ref, bf16[2048,320]{1,0:T(8,128)(2,1)} %get-tuple-element.68.dq_ref, f32[512,320]{1,0:T(8,128)} %merge.1.grn_ref, ...), custom_call_target="tpu_custom_call" | custom-call | tf_op jit(solution)/shard_map/tail/pallas_call | solution.py:729
  208.4 6.8 %pack.1.parts = bf16[32,2,208,128]{3,2,1,0:T(8,128)(2,1)} custom-call(f32[320,320]{1,0:T(8,128)} %get-tuple-element.72.gwq, f32[1280,320]{1,0:T(8,128)} %get-tuple-element.73.gwr, f32[320,320]{1,0:T(8,128)} %get-tuple-element.74.gwk, f32[320,320]{1,0:T(8,128)} %get-tuple-element.75.gwv, f32[320,320]{1,0:T(8,128)} %get-tuple-element.76.gwo, ...), custom_call_target="tpu_custom_call" | custom-call | tf_op jit(solution)/shard_map/pack/pallas_call | solution.py:186
  215.2 34.7 %scatter.1 = f32[162,320]{1,0:T(8,128)} custom-call(bf16[32,2,208,128]{3,2,1,0:T(8,128)(2,1)} %pack.1.parts), custom_call_target="tpu_custom_call" | custom-call | tf_op jit(solution)/shard_map/scatter/pallas_call | solution.py:1215
  249.9 1.8 reshape.37

commit v4 on v3

--- a/solution.py
+++ b/solution.py
@@ -44,7 +44,18 @@
 ) = range(11)
 HIDDEN_ROWS = 11
 
-PARAMS = pltpu.CompilerParams(vmem_limit_bytes=60 * 1024 * 1024)
+ROOM = dict(
+    unpack=30, front=14, attend=34, mix=30, attend_back=26, tail=16, pack=32,
+    gather=8, scatter=18, share=3, halo=2, merge=8,
+)
+
+
+def params(name):
+    return pltpu.CompilerParams(vmem_limit_bytes=ROOM[name] * 1024 * 1024)
+
+
+ANY = pl.BlockSpec(memory_space=pl.ANY)
+VM = pl.BlockSpec(memory_space=pltpu.VMEM)
 
 
 def shape_of(dims, kind):
@@ -131,7 +142,7 @@
             shape_of((16, FF), F32),
         ),
         scratch_shapes=[pltpu.VMEM((ROWS, C), F32), pltpu.VMEM((3, ROWS, 128), F32)],
-        compiler_params=PARAMS,
+        compiler_params=params("unpack"),
     )(blocks)
 
 
@@ -188,7 +199,7 @@
         name="pack",
         out_shape=shape_of((BLOCKS, 2, PART, 128), BF16),
         scratch_shapes=[pltpu.VMEM((3, ROWS, 128), F32)],
-        compiler_params=PARAMS,
+        compiler_params=params("pack"),
     )(*pieces)
 
 
@@ -253,7 +264,7 @@
             shape_of((tokens // 4, C), BF16),
         ),
         scratch_shapes=[pltpu.VMEM((3, TILE, 128), F32)],
-        compiler_params=PARAMS,
+        compiler_params=params("front"),
     )(x, vec, wq, wr)
 
 
@@ -278,7 +289,9 @@
             vones[h, :, 0:HD] = value[:, h * HD : (h + 1) * HD]
             vones[h, :, HD:] = jnp.ones((keys, HD), BF16)
 
-    outs, invs = [], []
+    lane = lax.broadcasted_iota(jnp.int32, (QT, 128), 1)
+    invs = jnp.zeros((QT, 128), F32)
+    outs = []
     for h in range(HEADS):
         scores = mm(q_ref[:, h * HD : (h + 1) * HD], kt[h * HD : (h + 1) * HD, :])
         top = jnp.max(scores, axis=-1, keepdims=True)
@@ -287,8 +300,8 @@
         both = mm(probs, vones[h])
         inv = 1.0 / both[:, HD:]
         outs.append(both[:, 0:HD] * inv)
-        invs.append(inv)
-    inv_out[...] = jnp.concatenate(invs, axis=1)
+        invs = jnp.where(lane == h, inv[:, 0:1], invs)
+    inv_out[...] = invs
     mixed = jnp.concatenate(outs, axis=1).astype(BF16)
     mixed_out[...] = mixed
     middle = x_ref[...].astype(F32) + mm(mixed, wo[...]) + vec[V_OUTPUT : V_OUTPUT + 1, :]
@@ -321,7 +334,7 @@
         ],
         out_specs=[
             tile,
-            tile,
+            pl.BlockSpec((QT, 128), lambda s, i: (s * steps + i, 0)),
             tile,
             tile,
             pl.BlockSpec((1, HEADS, QT, keys), lambda s, i: (s, 0, i, 0)),
@@ -330,7 +343,7 @@
         ],
         out_shape=(
             shape_of((tokens, C), BF16),
-            shape_of((tokens, C), F32),
+            shape_of((tokens, 128), F32),
             shape_of((tokens, C), F32),
             shape_of((tokens, C), BF16),
             shape_of((scenes, HEADS, per_scene, keys), BF16),
@@ -338,7 +351,7 @@
             shape_of((scenes, C, keys), BF16),
         ),
         scratch_shapes=[pltpu.VMEM((C, keys), BF16), pltpu.VMEM((HEADS, keys, 2 * HD), BF16)],
-        compiler_params=PARAMS,
+        compiler_params=params("attend"),
     )(x, q, rn_all, vec, wk, wv, wo)
 
 
@@ -371,151 +384,151 @@
     y_out, gmid_out, gwe_out, gws_out, ghid_out, gvec_out,
     nx, cx, nt, ct, e_scr, e_low, ga_scr, gc_scr, act_scr, ge_scr, branch, gn2,
 ):
-    step = pl.program_id(0)
     scenes, rows = n2.shape[0], n2.shape[1]
     ext = (rows + 4) * W
     gext = (rows + 2) * W
     own = rows * W
     top, low = edge[0], edge[1]
 
-    @pl.when(step == 0)
-    def _():
-        def inside(value, there):
-            return jnp.where(there > 0, value.astype(F32), 0.0).astype(BF16)
+    def inside(value, there):
+        return jnp.where(there > 0, value.astype(F32), 0.0).astype(BF16)
+
+    for s in range(scenes):
+        mine = n2[s].reshape(own, C)
+        nx[s * ext : s * ext + 2 * W, :] = n2_top[s].reshape(2 * W, C)
+        nx[s * ext + 2 * W : s * ext + 2 * W + own, :] = mine
+        nx[s * ext + 2 * W + own : (s + 1) * ext, :] = n2_low[s].reshape(2 * W, C)
+        nt[0:C, s * own : (s + 1) * own] = mine.T
+        mine = cot[s].reshape(own, C)
+        cx[s * gext : s * gext + W, :] = inside(cot_top[s].reshape(W, C), top)
+        cx[s * gext + W : s * gext + W + own, :] = mine
+        cx[s * gext + W + own : (s + 1) * gext, :] = inside(cot_low[s].reshape(W, C), low)
+        ct[:, s * own : (s + 1) * own] = mine.T
+    nt[C:, :] = jnp.ones((16, scenes * own), BF16)
+    branch[...] = jnp.zeros_like(branch)
+    gn2[...] = jnp.zeros_like(gn2)
+
+    def chunk(step, carry):
+        cols = pl.ds(pl.multiple_of(step * CH, CH), CH)
+        wcol = we[:, cols]
+        wrow = ws[cols, :]
+        body = (mm(nx[...], wcol) + hid[0:1, cols]).astype(BF16)
+        e_low[...] = body
+        e_scr[...] = body.astype(F32)
+        ga_scr[...] = mm_nt(cx[...], wrow)
+        for there, start in ((top, 0), (low, 2 * W + own)):
+
+            @pl.when(there == 0)
+            def _():
+                for s in range(scenes):
+                    e_scr[s * ext + start : s * ext + start + 2 * W, :] = jnp.zeros((2 * W, CH), F32)
+
+        col = lax.broadcasted_iota(jnp.int32, (8, CH), 0)
+        first, last = col == 0, col == 7
+
+        def right(value):
+            moved = pltpu.roll(value, 1, axis=0)
+            return jnp.concatenate([jnp.where(first, 0.0, moved[0:8]), moved[8:]], axis=0)
+
+        def left(value):
+            moved = pltpu.roll(value, W - 1, axis=0)
+            return jnp.concatenate([moved[: W - 8], jnp.where(last, 0.0, moved[W - 8 :])], axis=0)
+
+        def fold(value):
+            value = value[0:32] + value[32:64]
+            value = value[0:16] + value[16:32]
+            return (value[0:8] + value[8:16]).astype(F32)
+
+        taps = [hid[1 + k : 2 + k, cols] * SHRINK_IN for k in range(9)]
+        low_taps = [hid[1 + k : 2 + k, cols].astype(BF16) for k in range(9)]
+        conv_bias = hid[10:11, cols] * SHRINK_IN
 
         for s in range(scenes):
-            mine = n2[s].reshape(own, C)
-            nx[s * ext : s * ext + 2 * W, :] = n2_top[s].reshape(2 * W, C)
-            nx[s * ext + 2 * W : s * ext + 2 * W + own, :] = mine
-            nx[s * ext + 2 * W + own : (s + 1) * ext, :] = n2_low[s].reshape(2 * W, C)
-            nt[0:C, s * own : (s + 1) * own] = mine.T
-            mine = cot[s].reshape(own, C)
-            cx[s * gext : s * gext + W, :] = inside(cot_top[s].reshape(W, C), top)
-            cx[s * gext + W : s * gext + W + own, :] = mine
-            cx[s * gext + W + own : (s + 1) * gext, :] = inside(cot_low[s].reshape(W, C), low)
-            ct[:, s * own : (s + 1) * own] = mine.T
-        nt[C:, :] = jnp.ones((16, scenes * own), BF16)
-        branch[...] = jnp.zeros_like(branch)
-        gn2[...] = jnp.zeros_like(gn2)
-
-    wcol = we[...]
-    wrow = ws[...]
-    body = (mm(nx[...], wcol) + hid[0:1, :]).astype(BF16)
-    e_low[...] = body
-    e_scr[...] = body.astype(F32)
-    ga_scr[...] = mm_nt(cx[...], wrow)
-    for there, start in ((top, 0), (low, 2 * W + own)):
-
-        @pl.when(there == 0)
-        def _():
-            for s in range(scenes):
-                e_scr[s * ext + start : s * ext + start + 2 * W, :] = jnp.zeros((2 * W, CH), F32)
-
-    col = lax.broadcasted_iota(jnp.int32, (8, CH), 0)
-    first, last = col == 0, col == 7
-
-    def right(value):
-        moved = pltpu.roll(value, 1, axis=0)
-        return jnp.concatenate([jnp.where(first, 0.0, moved[0:8]), moved[8:]], axis=0)
-
-    def left(value):
-        moved = pltpu.roll(value, W - 1, axis=0)
-        return jnp.concatenate([moved[: W - 8], jnp.where(last, 0.0, moved[W - 8 :])], axis=0)
-
-    def fold(value):
-        value = value[0:32] + value[32:64]
-        value = value[0:16] + value[16:32]
-        return (value[0:8] + value[8:16]).astype(F32)
-
-    taps = [hid[1 + k : 2 + k, :] * SHRINK_IN for k in range(9)]
-    low_taps = [hid[1 + k : 2 + k, :].astype(BF16) for k in range(9)]
-    conv_bias = hid[10:11, :] * SHRINK_IN
-
-    for s in range(scenes):
-
-        def forward(r, carry):
-            at = pl.multiple_of(s * ext + r * W, W)
-            lines = [e_scr[pl.ds(at + a * W, W), :] for a in range(3)]
-            sums = [
-                lines[0] * taps[b] + lines[1] * taps[3 + b] + lines[2] * taps[6 + b]
-                for b in range(3)
-            ]
-            u = conv_bias + right(sums[0]) + sums[1] + left(sums[2])
-            cdf, bell = gelu_parts(u)
-            gat = pl.multiple_of(s * gext + r * W, W)
-            gc = ga_scr[pl.ds(gat, W), :] * (cdf + u * bell)
-            act_scr[pl.ds(gat, W), :] = (u * cdf).astype(BF16)
-            gc_scr[0, pl.ds(gat, W), :] = left(gc).astype(BF16)
-            gc_scr[1, pl.ds(gat, W), :] = gc.astype(BF16)
-            gc_scr[2, pl.ds(gat, W), :] = right(gc).astype(BF16)
-            return carry
-
-        lax.fori_loop(0, rows + 2, forward, 0)
-
-    def backward(s, r, carry):
-        line = e_low[pl.ds(pl.multiple_of(s * ext + (r + 2) * W, W), W), :]
-        grads = list(carry)
-        total = None
-        for a in range(3):
-            gat = pl.multiple_of(s * gext + (r + 2 - a) * W, W)
-            for b in range(3):
-                g = gc_scr[b, pl.ds(gat, W), :]
-                term = g * low_taps[3 * a + b]
-                total = term if total is None else total + term
-                grads[3 * a + b] = grads[3 * a + b] + fold(g * line)
-                if a == 1 and b == 1:
-                    grads[9] = grads[9] + fold(g)
-        ge_scr[pl.ds(pl.multiple_of(s * own + r * W, W), W), :] = total
-        return tuple(grads)
-
-    sums = tuple(jnp.zeros((8, CH), F32) for _ in range(10))
-    for s in range(scenes):
-        sums = lax.fori_loop(0, rows, functools.partial(backward, s), sums)
-    for k in range(10):
-        ghid_out[1 + k : 2 + k, :] = row_sum(sums[k]) * SLOPE
-
-    ge = ge_scr[...]
-    grads = mm(nt[...], ge)
-    gwe_out[...] = grads[0:C, :] * SLOPE
-    ghid_out[0:1, :] = grads[C : C + 1, :] * SLOPE
-    gn2[...] += mm_nt(ge, wcol)
-    gws = None
-    for s in range(scenes):
-        at = slice(s * own, (s + 1) * own)
-        act = act_scr[s * gext + W : s * gext + W + own, :]
-        branch[at, :] += mm(act, wrow)
-        term = mm(ct[:, at], act)
-        gws = term if gws is None else gws + term
-    gws_out[...] = gws * ACT_SCALE
-
-    @pl.when(step == pl.num_programs(0) - 1)
-    def _():
-        size = 4 * W
-        per = own // size
-        gain = vec[V_GAIN2 : V_GAIN2 + 1, :]
-
-        def finish(i, carry):
-            at = pl.multiple_of(i * size, size)
-            s = i // per
-            line = (i % per) * 4
-            middle = mid[pl.ds(at, size), :]
-            y_out[pl.ds(at, size), :] = (
-                middle + branch[pl.ds(at, size), :] * ACT_SCALE + vec[V_SHRINK : V_SHRINK + 1, :]
-            ).astype(BF16)
-            grad = gn2[pl.ds(at, size), :] * SLOPE
-            unit, rstd = norm_parts(middle)
-            direct = cot[s, pl.ds(line, 4)].reshape(size, C).astype(F32)
-            gmid_out[pl.ds(at, size), :] = direct + norm_back(grad, unit, rstd, gain)
-            return (
-                carry[0] + row_sum(grad * unit),
-                carry[1] + row_sum(grad),
-                carry[2] + row_sum(direct),
-            )
-
-        zero = jnp.zeros((1, C), F32)
-        sums = lax.fori_loop(0, scenes * per, finish, (zero, zero, zero))
-        for i in range(3):
-            gvec_out[i : i + 1, :] = sums[i]
+
+            def forward(r, carry):
+                at = pl.multiple_of(s * ext + r * W, W)
+                lines = [e_scr[pl.ds(at + a * W, W), :] for a in range(3)]
+                sums = [
+                    lines[0] * taps[b] + lines[1] * taps[3 + b] + lines[2] * taps[6 + b]
+                    for b in range(3)
+                ]
+                u = conv_bias + right(sums[0]) + sums[1] + left(sums[2])
+                cdf, bell = gelu_parts(u)
+                gat = pl.multiple_of(s * gext + r * W, W)
+                gc = ga_scr[pl.ds(gat, W), :] * (cdf + u * bell)
+                act_scr[pl.ds(gat, W), :] = (u * cdf).astype(BF16)
+                gc_scr[0, pl.ds(gat, W), :] = left(gc).astype(BF16)
+                gc_scr[1, pl.ds(gat, W), :] = gc.astype(BF16)
+                gc_scr[2, pl.ds(gat, W), :] = right(gc).astype(BF16)
+                return carry
+
+            lax.fori_loop(0, rows + 2, forward, 0)
+
+        def backward(s, r, carry):
+            line = e_low[pl.ds(pl.multiple_of(s * ext + (r + 2) * W, W), W), :]
+            grads = list(carry)
+            total = None
+            for a in range(3):
+                gat = pl.multiple_of(s * gext + (r + 2 - a) * W, W)
+                for b in range(3):
+                    g = gc_scr[b, pl.ds(gat, W), :]
+                    term = g * low_taps[3 * a + b]
+                    total = term if total is None else total + term
+                    grads[3 * a + b] = grads[3 * a + b] + fold(g * line)
+                    if a == 1 and b == 1:
+                        grads[9] = grads[9] + fold(g)
+            ge_scr[pl.ds(pl.multiple_of(s * own + r * W, W), W), :] = total
+            return tuple(grads)
+
+        sums = tuple(jnp.zeros((8, CH), F32) for _ in range(10))
+        for s in range(scenes):
+            sums = lax.fori_loop(0, rows, functools.partial(backward, s), sums)
+        for k in range(10):
+            ghid_out[1 + k : 2 + k, cols] = row_sum(sums[k]) * SLOPE
+
+        ge = ge_scr[...]
+        grads = mm(nt[...], ge)
+        gwe_out[:, cols] = grads[0:C, :] * SLOPE
+        ghid_out[0:1, cols] = grads[C : C + 1, :] * SLOPE
+        gn2[...] += mm_nt(ge, wcol)
+        gws = None
+        for s in range(scenes):
+            at = slice(s * own, (s + 1) * own)
+            act = act_scr[s * gext + W : s * gext + W + own, :]
+            branch[at, :] += mm(act, wrow)
+            term = mm(ct[:, at], act)
+            gws = term if gws is None else gws + term
+        gws_out[:, cols] = gws * ACT_SCALE
+        return carry
+
+    lax.fori_loop(0, FF // CH, chunk, 0)
+
+    size = 4 * W
+    per = own // size
+    gain = vec[V_GAIN2 : V_GAIN2 + 1, :]
+
+    def finish(i, carry):
+        at = pl.multiple_of(i * size, size)
+        s = i // per
+        line = (i % per) * 4
+        middle = mid[pl.ds(at, size), :]
+        y_out[pl.ds(at, size), :] = (
+            middle + branch[pl.ds(at, size), :] * ACT_SCALE + vec[V_SHRINK : V_SHRINK + 1, :]
+        ).astype(BF16)
+        grad = gn2[pl.ds(at, size), :] * SLOPE
+        unit, rstd = norm_parts(middle)
+        direct = cot[s, pl.ds(line, 4)].reshape(size, C).astype(F32)
+        gmid_out[pl.ds(at, size), :] = direct + norm_back(grad, unit, rstd, gain)
+        return (
+            carry[0] + row_sum(grad * unit),
+            carry[1] + row_sum(grad),
+            carry[2] + row_sum(direct),
+        )
+
+    zero = jnp.zeros((1, C), F32)
+    sums = lax.fori_loop(0, scenes * per, finish, (zero, zero, zero))
+    for i in range(3):
+        gvec_out[i : i + 1, :] = sums[i]
 
 
 def mix(n2, n2_top, n2_low, cot, cot_top, cot_low, mid, edge, vec, hid, we, ws):
@@ -523,34 +536,11 @@
     tokens = scenes * rows * W
     ext = scenes * (rows + 4) * W
     gext = scenes * (rows + 2) * W
-    once = dict(pipeline_mode=pl.Buffered(1))
-    whole = lambda a: pl.BlockSpec(a.shape, lambda j: (0,) * a.ndim, **once)
     return pl.pallas_call(
         mix_kernel,
         name="mix",
-        grid=(FF // CH,),
-        in_specs=[
-            whole(n2),
-            whole(n2_top),
-            whole(n2_low),
-            whole(cot),
-            whole(cot_top),
-            whole(cot_low),
-            whole(mid),
-            pl.BlockSpec(memory_space=pltpu.SMEM),
-            whole(vec),
-            pl.BlockSpec((16, CH), lambda j: (0, j)),
-            pl.BlockSpec((C, CH), lambda j: (0, j)),
-            pl.BlockSpec((CH, C), lambda j: (j, 0)),
-        ],
-        out_specs=[
-            full((tokens, C)),
-            full((tokens, C)),
-            pl.BlockSpec((C, CH), lambda j: (0, j)),
-            pl.BlockSpec((C, CH), lambda j: (0, j)),
-            pl.BlockSpec((16, CH), lambda j: (0, j)),
-            full((8, C)),
-        ],
+        in_specs=[VM] * 7 + [pl.BlockSpec(memory_space=pltpu.SMEM)] + [VM] * 4,
+        out_specs=[VM] * 6,
         out_shape=(
             shape_of((tokens, C), BF16),
             shape_of((tokens, C), F32),
@@ -573,7 +563,7 @@
             pltpu.VMEM((tokens, C), F32),
             pltpu.VMEM((tokens, C), F32),
         ],
-        compiler_params=PARAMS,
+        compiler_params=params("mix"),
     )(n2, n2_top, n2_low, cot, cot_top, cot_low, mid, edge, vec, hid, we, ws)
 
 
@@ -603,7 +593,10 @@
     gvec_out[8:9, :] += row_sum(gatt.astype(F32))
     mixed = mixed_ref[...]
     gwo_out[...] += mm_tn(mixed, gatt)
-    scaled = (mm_nt(gatt, wo[...]) * inv_ref[...]).astype(BF16)
+    inv = jnp.concatenate(
+        [jnp.broadcast_to(inv_ref[:, h : h + 1], (QTB, HD)) for h in range(HEADS)], axis=1
+    )
+    scaled = (mm_nt(gatt, wo[...]) * inv).astype(BF16)
     prod = scaled.astype(F32) * mixed.astype(F32)
     q_t = q_ref[...].T
     g_t = scaled.T
@@ -643,7 +636,7 @@
         grid=(scenes, steps),
         in_specs=[
             tile,
-            tile,
+            pl.BlockSpec((QTB, 128), lambda s, i: (s * steps + i, 0)),
             tile,
             tile,
             pl.BlockSpec((1, HEADS, QTB, keys), lambda s, i: (s, 0, i, 0)),
@@ -675,7 +668,7 @@
             pltpu.VMEM((C, keys), F32),
             pltpu.VMEM((C, keys), F32),
         ],
-        compiler_params=PARAMS,
+        compiler_params=params("attend_back"),
     )(q, inv, mixed, gmid, p, key, vt, rn_all, wk, wv, wo)
 
 
@@ -741,12 +734,8 @@
             shape_of((8, C), F32),
         ),
         scratch_shapes=[pltpu.VMEM((3, TILE, 128), F32), pltpu.VMEM((3, TILE, 128), F32)],
-        compiler_params=PARAMS,
+        compiler_params=params("tail"),
     )(x, gmid, dq, grn, red, vec, wq, wr)
-
-
-ANY = pl.BlockSpec(memory_space=pl.ANY)
-VM = pl.BlockSpec(memory_space=pltpu.VMEM)
 
 
 def flip(value, by):
@@ -785,9 +774,9 @@
     pl.semaphore_wait(barrier, count)
 
 
-def comm_params(number):
+def comm_params(name, number):
     return pltpu.CompilerParams(
-        collective_id=number, has_side_effects=True, vmem_limit_bytes=60 * 1024 * 1024
+        collective_id=number, has_side_effects=True, vmem_limit_bytes=ROOM[name] * 1024 * 1024
     )
 
 
@@ -1005,7 +994,7 @@
             DMA((2, 4, 4)), DMA, DMA((2,)), DMA((4, 4)),
             DMA((BLOCKS, 2)),
         ],
-        compiler_params=comm_params(1),
+        compiler_params=comm_params("gather", 1),
     )(own)
 
 
@@ -1224,7 +1213,7 @@
         ]
         + sems()
         + sems(),
-        compiler_params=comm_params(2),
+        compiler_params=comm_params("scatter", 2),
     )(parts)
 
 
@@ -1319,7 +1308,7 @@
         in_specs=[VM, ANY],
         out_specs=(ANY, ANY, ANY),
         scratch_shapes=[dma((3,)), dma((bands,)), dma, dma, dma, dma, dma],
-        compiler_params=comm_params(3),
+        compiler_params=comm_params("share", 3),
     )(rn, cot)
 
 
@@ -1338,7 +1327,7 @@
         in_specs=[ANY],
         out_specs=(ANY, ANY),
         scratch_shapes=[dma, dma, dma, dma],
-        compiler_params=comm_params(4),
+        compiler_params=comm_params("halo", 4),
     )(value)
 
 
@@ -1381,7 +1370,7 @@
             dma,
             dma,
         ],
-        compiler_params=comm_params(5),
+        compiler_params=comm_params("merge", 5),
     )(parts)
 
 
@@ -1391,10 +1380,10 @@
     )
 
 
-def gather_params(params):
-    if blocks_fit(params.shape[0]):
-        return gather_blocks(params.reshape(BLOCK_ROWS, C))
-    flat = lax.all_gather(params, ("dp", "space"), axis=0, tiled=True)
+def gather_flat(shard):
+    if blocks_fit(shard.shape[0]):
+        return gather_blocks(shard.reshape(BLOCK_ROWS, C))
+    flat = lax.all_gather(shard, ("dp", "space"), axis=0, tiled=True)
     want = ROWS * C
     flat = flat[:want] if flat.shape[0] >= want else jnp.pad(flat, (0, want - flat.shape[0]))
     blocks = jax.vmap(compact)(flat.reshape(BLOCKS, BLOCK_ROWS, C))
@@ -1411,14 +1400,14 @@
     return own.astype(F32)
 
 
-def on_device(scenes, params, cotangent):
+def on_device(scenes, shard, cotangent):
     count, rows, breadth = scenes.shape[0], scenes.shape[1], scenes.shape[2]
     tokens = count * rows * breadth
     bands = lax.axis_size("space")
     per_band = rows * breadth // 4
     band = lax.axis_index("space")
     edge = jnp.stack([band > 0, band < bands - 1]).astype(F32)
-    wq, wr, wk, wv, wo, we, ws, vec, hid = unpack(gather_params(params))
+    wq, wr, wk, wv, wo, we, ws, vec, hid = unpack(gather_flat(shard))
     x = scenes.reshape(tokens, C)
     q, red, rn = front(x, vec, wq, wr)
     rn_all, cot_top, cot_low = share(rn, cotangent)
@@ -1435,8 +1424,8 @@
     grn = merge(grn_all.reshape(bands, count * per_band, C))
     gx, gwq, gwr, gvec0 = tail(x, gmid, dq, grn, red, vec, wq, wr)
     blocks = pack(gwq, gwr, gwk, gwv, gwo, gwe, gws, gvec0, gvec1, gvec2, ghid)
-    shard = scatter_grads(blocks, params.shape[0])
-    return y.reshape(scenes.shape), gx.reshape(scenes.shape), shard
+    grads = scatter_grads(blocks, shard.shape[0])
+    return y.reshape(scenes.shape), gx.reshape(scenes.shape), grads
 
 
 def solution(mesh):

time: 252 us -> 219 us (0.87)
  Pallas kernels: 247 us -> 216 us
    pallas_call x1, Pallas kernels: 6.81 us -> 1.99 us  [pack(): pl.pallas_call(pack_kernel, name='pack', out_shape=shape_of((BLOCKS, 2, P...]
    pallas_call x1, Pallas kernels: 61.1 us -> 56.7 us  [mix(): pl.pallas_call(mix_kernel, name='mix', in_specs=[VM] * 7 + [pl.BlockSpec(...]
    pallas_call x1, Pallas kernels: 5.33 us -> 2.12 us  [unpack(): pl.pallas_call(unpack_kernel, name='unpack', out_shape=(shape_of((C, C),...]
    pallas_call x1, Pallas kernels: 28.2 us -> 25.6 us  [gather_blocks(): pl.pallas_call(gather_kernel, name='gather', out_shape=shape_of((BLOCKS,...]
    pallas_call x1, Pallas kernels: 34.7 us -> 32.1 us  [scatter_blocks(): pl.pallas_call(scatter_kernel, name='scatter', out_shape=shape_of((BLOCK_...]
where the time goes in v4:
time: 219 us
  Pallas kernels  216 us (99%)
    pallas_call x1, Pallas kernels, mix(): pl.pallas_call(mix_kernel, name='mix', in_specs=[VM] * 7 + [pl.BlockSpec(...  56.7 us
    pallas_call x1, Pallas kernels, scatter_blocks(): pl.pallas_call(scatter_kernel, name='scatter', out_shape=shape_of((BLOCK_...  32.1 us
    pallas_call x1, Pallas kernels, attend_back(): pl.pallas_call(attend_back_kernel, name='attend_back', grid=(scenes, step...  29.1 us
    pallas_call x1, Pallas kernels, gather_blocks(): pl.pallas_call(gather_kernel, name='gather', out_shape=shape_of((BLOCKS,...  25.6 us
    pallas_call x1, Pallas kernels, attend(): pl.pallas_call(attend_kernel, name='attend', grid=(scenes, steps), in_spe...  24.1 us
    pallas_call x1, Pallas kernels, merge(): pl.pallas_call(merge_kernel, name='merge', out_shape=shape_of(one, F32),...  15.4 us
    pallas_call x1, Pallas kernels, share(): pl.pallas_call(share_kernel, name='share', out_shape=(shape_of((bands,) +...  13 us
    pallas_call x1, Pallas kernels, tail(): pl.pallas_call(tail_kernel, name='tail', grid=(tokens // TILE,), in_specs...  8.75 us

profile of v4, /device:TPU:0, one launch (start us, length us, event | category | flops | bytes accessed | tf_op | source)
XLA Modules:
  0.0 218.8 jit_solution(1660801536737231015)
XLA Ops:
  0.6 0.1 add_convert_fusion.edge
  0.7 1.0 reshape.31.own_ref
  1.7 25.6 %gather.1.g_ref = bf16[32,2,208,128]{3,2,1,0:T(8,128)(2,1)S(1)} custom-call(bf16[162,320]{1,0:T(8,128)(2,1)S(1)} %reshape.31.own_ref), custom_call_target="tpu_custom_call" | custom-call | tf_op jit(solution)/shard_map/gather/pallas_call | solution.py:985
  27.4 0.0 copy-start
  27.4 2.1 unpack.1
  29.5 0.0 copy-start.1
  29.5 0.0 copy-done
  29.5 4.5 %front.1 = (bf16[2048,320]{1,0:T(8,128)(2,1)S(1)}, f32[512,320]{1,0:T(8,128)S(1)}, bf16[512,320]{1,0:T(8,128)(2,1)S(1)}) custom-call(bf16[2048,320]{1,0:T(8,128)(2,1)S(1)} %bitcast.8, f32[16,320]{1,0:T(8,128)S(1)} %get-tuple-element.43.vec, bf16[320,320]{1,0:T(8,128)(2,1)S(1)} %get-tuple-element.44.wq, bf16[1280,320]{1,0:T(8,128)(2,1)S(1)} %get-tuple-element.45.wr), custom_call_target="tpu_custom_call" | custom-call | tf_op jit(solution)/shard_map/front/pallas_call | solution.py:246
  34.0 0.0 copy-start.2
  34.0 0.0 copy-done.1
  34.0 13.0 %share.1 = (bf16[4,512,320]{2,1,0:T(8,128)(2,1)S(1)}, bf16[2,1,64,320]{3,2,1,0:T(8,128)(2,1)S(1)}, bf16[2,1,64,320]{3,2,1,0:T(8,128)(2,1)S(1)}) custom-call(bf16[512,320]{1,0:T(8,128)(2,1)S(1)} %get-tuple-element.47.rn, bf16[2,16,64,320]{3,2,1,0:T(8,128)(2,1)S(1)} %copy-done.1), custom_call_target="tpu_custom_call" | custom-call | tf_op jit(solution)/shard_map/share/pallas_call | solution.py:1300
  47.0 0.0 copy-done.2
  47.0 24.1 %attend.1 = (bf16[2048,320]{1,0:T(8,128)(2,1)S(1)}, f32[2048,128]{1,0:T(8,128)S(1)}, f32[2048,320]{1,0:T(8,128)S(1)}, bf16[2048,320]{1,0:T(8,128)(2,1)S(1)}, bf1...) custom-call(bf16[2048,320]{1,0:T(8,128)(2,1)S(1)} %bitcast.9, ...), custom_call_target="tpu_custom_call" | custom-call | tf_op jit(solution)/shard_map/attend/pallas_call | solution.py:322
  71.1 2.9 %halo.1 = (bf16[2,2,64,320]{3,2,1,0:T(8,128)(2,1)S(1)}, bf16[2,2,64,320]{3,2,1,0:T(8,128)(2,1)S(1)}) custom-call(bf16[2,16,64,320]{3,2,1,0:T(8,128)(2,1)S(1)} %bitcast.11), custom_call_target="tpu_custom_call" | custom-call | tf_op jit(solution)/shard_map/halo/pallas_call | solution.py:1323
  74.0 56.7 %mix.1 = (bf16[2048,320]{1,0:T(8,128)(2,1)}, f32[2048,320]{1,0:T(8,128)S(1)}, f32[320,1280]{1,0:T(8,128)S(1)}, f32[320,1280]{1,0:T(8,128)S(1)}, f32[16,1280]{1,0:T(8,128)S(1)}, /*index=5*/f32[8,320]{1,0:T(8,128)S(1)}) custom-call(bf16[2,16,64,320]{3,2,1,0:T(8,128)(2,1)S(1)} %bitcast.12, bf16[2,2,64,320]{3,2,1,0:T(8,128)(2,1)S(1)} %get-tuple-element.53.n2_top, ...), custom_call_target="tpu_custom_call" | custom-call | tf_op jit(solution)/shard_map/mix/pallas_call | solution.py:539
  130.7 29.1 %attend_back.1 = (bf16[2048,320]{1,0:T(8,128)(2,1)S(1)}, bf16[4,2,256,320]{3,2,1,0:T(8,128)(2,1)S(1)}, f32[320,320]{1,0:T(8,128)S(1)}, f32[320,320]{1,0:T(8,128)...) custom-call(bf16[2048,320]{1,0:T(8,128)(2,1)S(1)} %get-tuple-element.46.q_ref, ...), custom_call_target="tpu_custom_call" | custom-call | tf_op jit(solution)/shard_map/attend_back/pallas_call | solution.py:633
  159.8 0.0 copy-start.3
  159.8 15.4 %merge.1.grn_ref = f32[512,320]{1,0:T(8,128)S(1)} custom-call(bf16[4,512,320]{2,1,0:T(8,128)(2,1)S(1)} %bitcast.15), custom_call_target="tpu_custom_call" | custom-call | tf_op jit(solution)/shard_map/merge/pallas_call | solution.py:1358
  175.2 0.0 copy-done.3
  175.2 8.8 %tail.1 = (f32[2048,320]{1,0:T(8,128)}, f32[320,320]{1,0:T(8,128)S(1)}, f32[1280,320]{1,0:T(8,128)S(1)}, f32[8,320]{1,0:T(8,128)S(1)}) custom-call(bf16[2048,320]{1,0:T(8,128)(2,1)S(1)} %bitcast.10, f32[2048,320]{1,0:T(8,128)S(1)} %get-tuple-element.62.gmid_ref, bf16[2048,320]{1,0:T(8,128)(2,1)S(1)} %get-tuple-element.68.dq_ref, ...), custom_call_target="tpu_custom_call" | custom-call | tf_op jit(solution)/shard_map/tail/pallas_call | solution.py:722
  183.9 2.0 pack.1.parts
  185.9 32.1 %scatter.1 = f32[162,320]{1,0:T(8,128)S(1)} custom-call(bf16[32,2,208,128]{3,2,1,0:T(8,128)(2,1)S(1)} %pack.1.parts), custom_call_target="tpu_custom_call" | custom-call | tf_op jit(solution)/shard_map/scatter/pallas_call | solution.py:1204
  218.0 0.8 reshape.37
Async XLA Ops:
  27.4 2.2 copy-start
  29.5 4.5 %copy-start.1 = (bf16[2,16,64,320]{3,2,1,0:T(8,128)(2,1)S(1)}, bf16[2,16,64,320]{3,2,1,0:T(8,128)(2,1)}, u32[]{:S(2)}) copy-start(bf16[2,16,64,320]{3,2,1,0:T(8,128)(2,1)} %cot.3) | copy-start | bytes 3932164
  34.0 13.0 %copy-start.2 = (f32[512,320]{1,0:T(8,128)}, f32[512,320]{1,0:T(8,128)S(1)}, u32[]{:S(2)}) copy-start(f32[512,320]{1,0:T(8,128)S(1)} %get-tuple-element.70.red_ref) | copy-start | bytes 1966084
  159.8 15.4 %copy-start.3 = (f32[512,320]{1,0:T(8,128)S(1)}, f32[512,320]{1,0:T(8,128)}, u32[]{:S(2)}) copy-start(f32[512,320]{1,0:T(8,128)} %copy-done.2) | copy-start | bytes 1966084

commit v5 on v4

--- a/solution.py
+++ b/solution.py
@@ -45,7 +45,7 @@
 HIDDEN_ROWS = 11
 
 ROOM = dict(
-    unpack=30, front=14, attend=34, mix=30, attend_back=26, tail=16, pack=32,
+    unpack=30, front=14, attend=34, mix=33, attend_back=26, tail=16, pack=32,
     gather=8, scatter=18, share=3, halo=2, merge=8,
 )
 
@@ -102,7 +102,7 @@
 def unpack_kernel(g_ref, wq, wr, wk, wv, wo, we, ws, vec, hid, rows, tiles):
     for i in range(BLOCKS):
         at = i * BLOCK_ROWS
-        block = restore(g_ref[i].astype(F32).reshape(2 * PART, 128))
+        block = restore(g_ref[i].astype(F32))
         rows[at : at + BLOCK_ROWS, :] = block
         tiles[0, at : at + BLOCK_ROWS, :] = block[:, 0:128]
         tiles[1, at : at + BLOCK_ROWS, :] = block[:, 128:256]
@@ -179,7 +179,7 @@
     put(VECTOR_ROWS[V_OUTPUT], gvec1[8:9, :])
     put(USED_ROWS, jnp.zeros((ROWS - USED_ROWS, C), F32))
     half = BLOCK_ROWS // 2
-    spare = jnp.zeros((2 * PART - 2 * BLOCK_ROWS - half, 128), F32)
+    spare = jnp.zeros((SPAN - 2 * BLOCK_ROWS - half, 128), F32)
     for i in range(BLOCKS):
         at = i * BLOCK_ROWS
         tail = jnp.concatenate(
@@ -190,14 +190,14 @@
             axis=1,
         )
         rows = [tiles[0, at : at + BLOCK_ROWS, :], tiles[1, at : at + BLOCK_ROWS, :], tail, spare]
-        out[i] = jnp.concatenate(rows, axis=0).reshape(2, PART, 128).astype(BF16)
+        out[i] = jnp.concatenate(rows, axis=0).astype(BF16)
 
 
 def pack(*pieces):
     return pl.pallas_call(
         pack_kernel,
         name="pack",
-        out_shape=shape_of((BLOCKS, 2, PART, 128), BF16),
+        out_shape=shape_of((BLOCKS, SPAN, 128), BF16),
         scratch_shapes=[pltpu.VMEM((3, ROWS, 128), F32)],
         compiler_params=params("pack"),
     )(*pieces)
@@ -356,6 +356,7 @@
 
 
 CH = 256
+AHEAD = 2
 
 
 SHRINK_IN = math.sqrt(0.5 * math.log2(math.e))
@@ -382,7 +383,7 @@
 def mix_kernel(
     n2, n2_top, n2_low, cot, cot_top, cot_low, mid, edge, vec, hid, we, ws,
     y_out, gmid_out, gwe_out, gws_out, ghid_out, gvec_out,
-    nx, cx, nt, ct, e_scr, e_low, ga_scr, gc_scr, act_scr, ge_scr, branch, gn2,
+    nx, cx, nt, ct, wx, wt, e_scr, e_low, ga_scr, gc_scr, act_scr, ge_scr, branch, gn2,
 ):
     scenes, rows = n2.shape[0], n2.shape[1]
     ext = (rows + 4) * W
@@ -395,15 +396,29 @@
 
     for s in range(scenes):
         mine = n2[s].reshape(own, C)
-        nx[s * ext : s * ext + 2 * W, :] = n2_top[s].reshape(2 * W, C)
-        nx[s * ext + 2 * W : s * ext + 2 * W + own, :] = mine
-        nx[s * ext + 2 * W + own : (s + 1) * ext, :] = n2_low[s].reshape(2 * W, C)
+        nx[s * ext : s * ext + 2 * W, 0:C] = inside(n2_top[s].reshape(2 * W, C), top)
+        nx[s * ext + 2 * W : s * ext + 2 * W + own, 0:C] = mine
+        nx[s * ext + 2 * W + own : (s + 1) * ext, 0:C] = inside(n2_low[s].reshape(2 * W, C), low)
+        nx[s * ext : (s + 1) * ext, C:] = jnp.ones((ext, 64), BF16)
+        for there, start in ((top, 0), (low, 2 * W + own)):
+
+            @pl.when(there == 0)
+            def _():
+                spot = slice(s * ext + start, s * ext + start + 2 * W)
+                nx[spot, C:] = jnp.zeros((2 * W, 64), BF16)
+
         nt[0:C, s * own : (s + 1) * own] = mine.T
         mine = cot[s].reshape(own, C)
         cx[s * gext : s * gext + W, :] = inside(cot_top[s].reshape(W, C), top)
         cx[s * gext + W : s * gext + W + own, :] = mine
         cx[s * gext + W + own : (s + 1) * gext, :] = inside(cot_low[s].reshape(W, C), low)
         ct[:, s * own : (s + 1) * own] = mine.T
+    wx[0:C, :] = we[...]
+    wx[C : C + 16, :] = jnp.concatenate(
+        [hid[0:1, :], jnp.zeros((15, FF), F32)], axis=0
+    ).astype(BF16)
+    wx[C + 16 :, :] = jnp.zeros((48, FF), BF16)
+    wt[...] = ws[...].T
     nt[C:, :] = jnp.ones((16, scenes * own), BF16)
     branch[...] = jnp.zeros_like(branch)
     gn2[...] = jnp.zeros_like(gn2)
@@ -412,16 +427,16 @@
         cols = pl.ds(pl.multiple_of(step * CH, CH), CH)
         wcol = we[:, cols]
         wrow = ws[cols, :]
-        body = (mm(nx[...], wcol) + hid[0:1, cols]).astype(BF16)
-        e_low[...] = body
-        e_scr[...] = body.astype(F32)
-        ga_scr[...] = mm_nt(cx[...], wrow)
-        for there, start in ((top, 0), (low, 2 * W + own)):
-
-            @pl.when(there == 0)
-            def _():
-                for s in range(scenes):
-                    e_scr[s * ext + start : s * ext + start + 2 * W, :] = jnp.zeros((2 * W, CH), F32)
+        wx_col = wx[:, cols]
+        wt_col = wt[:, cols]
+
+        def expand(at, size):
+            part = mm(nx[pl.ds(at, size), :], wx_col).astype(BF16)
+            e_low[pl.ds(at, size), :] = part
+            e_scr[pl.ds(at, size), :] = part.astype(F32)
+
+        def activ_grad(at, size):
+            ga_scr[pl.ds(at, size), :] = mm(cx[pl.ds(at, size), :], wt_col)
 
         col = lax.broadcasted_iota(jnp.int32, (8, CH), 0)
         first, last = col == 0, col == 7
@@ -445,7 +460,7 @@
 
         for s in range(scenes):
 
-            def forward(r, carry):
+            def forward_row(r):
                 at = pl.multiple_of(s * ext + r * W, W)
                 lines = [e_scr[pl.ds(at + a * W, W), :] for a in range(3)]
                 sums = [
@@ -460,9 +475,18 @@
                 gc_scr[0, pl.ds(gat, W), :] = left(gc).astype(BF16)
                 gc_scr[1, pl.ds(gat, W), :] = gc.astype(BF16)
                 gc_scr[2, pl.ds(gat, W), :] = right(gc).astype(BF16)
+
+            def forward(i, carry):
+                r = i * AHEAD
+                for j in range(AHEAD):
+                    forward_row(r + j)
+                expand(pl.multiple_of(s * ext + (r + AHEAD + 2) * W, W), AHEAD * W)
+                activ_grad(pl.multiple_of(s * gext + (r + AHEAD) * W, W), AHEAD * W)
                 return carry
 
-            lax.fori_loop(0, rows + 2, forward, 0)
+            expand(s * ext, (AHEAD + 2) * W)
+            activ_grad(s * gext, AHEAD * W)
+            lax.fori_loop(0, (rows + 2) // AHEAD, forward, 0)
 
         def backward(s, r, carry):
             line = e_low[pl.ds(pl.multiple_of(s * ext + (r + 2) * W, W), W), :]
@@ -550,13 +574,15 @@
             shape_of((8, C), F32),
         ),
         scratch_shapes=[
-            pltpu.VMEM((ext, C), BF16),
-            pltpu.VMEM((gext, C), BF16),
+            pltpu.VMEM((ext + AHEAD * W, C + 64), BF16),
+            pltpu.VMEM((gext + AHEAD * W, C), BF16),
             pltpu.VMEM((C + 16, tokens), BF16),
             pltpu.VMEM((C, tokens), BF16),
-            pltpu.VMEM((ext, CH), F32),
-            pltpu.VMEM((ext, CH), BF16),
-            pltpu.VMEM((gext, CH), F32),
+            pltpu.VMEM((C + 64, FF), BF16),
+            pltpu.VMEM((C, FF), BF16),
+            pltpu.VMEM((ext + AHEAD * W, CH), F32),
+            pltpu.VMEM((ext + AHEAD * W, CH), BF16),
+            pltpu.VMEM((gext + AHEAD * W, CH), F32),
             pltpu.VMEM((3, gext, CH), BF16),
             pltpu.VMEM((gext, CH), BF16),
             pltpu.VMEM((tokens, CH), BF16),
@@ -824,13 +850,15 @@
 
 
 DMA = pltpu.SemaphoreType.DMA
-PART = 208
+SPAN = 416
+PART = 288
+BOTH = (pl.ds(0, PART), pl.ds(PART, SPAN - PART))
 
 
 def compact(block):
     half = BLOCK_ROWS // 2
     tail = jnp.concatenate([block[:half, 256:], block[half:, 256:]], axis=1)
-    spare = jnp.zeros((2 * PART - 2 * BLOCK_ROWS - half, 128), block.dtype)
+    spare = jnp.zeros((SPAN - 2 * BLOCK_ROWS - half, 128), block.dtype)
     return jnp.concatenate([block[:, 0:128], block[:, 128:256], tail, spare], axis=0)
 
 
@@ -854,7 +882,7 @@
     at = Place()
     line = at.line
     first, second, sibling, up, down = at.partners()
-    own[...] = compact(own_ref[...].astype(F32)).reshape(2, PART, 128).astype(BF16)
+    own[...] = compact(own_ref[...].astype(F32)).astype(BF16)
     at.meet()
     can_up, can_down = at.z < line - 1, at.z > 0
 
@@ -863,15 +891,15 @@
         return at.block(z, x, y, c)
 
     def push(part, index, src, sem, where):
-        remote(src, out.at[index, part], sem, recv.at[index, part], where).start()
+        remote(src, out.at[index, BOTH[part]], sem, recv.at[index, part], where).start()
 
     def landed(part, index):
         remote(
-            out.at[index, part], out.at[index, part], p_a.at[0], recv.at[index, part], sibling
+            out.at[index, BOTH[part]], out.at[index, BOTH[part]], p_a.at[0], recv.at[index, part], sibling
         ).wait_recv()
 
     def here(part, index, is_own):
-        return own.at[part] if is_own else out.at[index, part]
+        return own.at[BOTH[part]] if is_own else out.at[index, BOTH[part]]
 
     def along_z(part, z, k, index, src, way, sems):
         if way >= 0:
@@ -954,7 +982,7 @@
                 landed(part, index_of(z, da, db, 1 - at.c))
 
     def sent(part, sem, where):
-        remote(own.at[part], out.at[mine, part], sem, recv.at[mine, part], where).wait_send()
+        remote(own.at[BOTH[part]], out.at[mine, BOTH[part]], sem, recv.at[mine, part], where).wait_send()
 
     sent(1, q_a, first)
     for z in range(line):
@@ -985,11 +1013,11 @@
     return pl.pallas_call(
         gather_kernel,
         name="gather",
-        out_shape=shape_of((BLOCKS, 2, PART, 128), BF16),
+        out_shape=shape_of((BLOCKS, SPAN, 128), BF16),
         in_specs=[VM],
         out_specs=VM,
         scratch_shapes=[
-            pltpu.VMEM((2, PART, 128), BF16),
+            pltpu.VMEM((SPAN, 128), BF16),
             DMA((2, 1, 4)), DMA((4,)), DMA((2, 4)), DMA((4, 4)),
             DMA((2, 4, 4)), DMA, DMA((2,)), DMA((4, 4)),
             DMA((BLOCKS, 2)),
@@ -1023,11 +1051,11 @@
         return at.block(z, x, y, c)
 
     def c_copy(k):
-        src = parts.at[source(k, 1 - at.c), 0]
+        src = parts.at[source(k, 1 - at.c), BOTH[0]]
         return remote(src, rc.at[k], c_out.at[k], c_in.at[k], sibling)
 
     def qc_copy(k):
-        src = parts.at[source(k, 1 - at.c), 1]
+        src = parts.at[source(k, 1 - at.c), BOTH[1]]
         return remote(src, qc.at[k], qc_out.at[k], qc_in.at[k], sibling)
 
     def a_copy(j):
@@ -1059,7 +1087,7 @@
         da, db, z = slots[k]
         qc_copy(k).wait_recv()
         mine = source(k, at.c)
-        qacc[k] = add(parts[mine, 1], qc[k])
+        qacc[k] = add(parts[mine, BOTH[1]], qc[k])
         if z > 0:
 
             @pl.when(at.z == 0)
@@ -1073,7 +1101,7 @@
                 qz_copy(1, k, qacc.at[k]).start()
 
         c_copy(k).wait_recv()
-        acc[k] = add(parts[mine, 0], rc[k])
+        acc[k] = add(parts[mine, BOTH[0]], rc[k])
         if da:
             a_copy(k).start()
 
@@ -1198,6 +1226,7 @@
 
 def scatter_blocks(parts):
     room = lambda *n: pltpu.VMEM(n + (PART, 128), BF16)
+    less = lambda *n: pltpu.VMEM(n + (SPAN - PART, 128), BF16)
     sems = lambda: [
         DMA((16,)), DMA((8,)), DMA((4,)), DMA((2, 4)), DMA((16,)), DMA((2, 16)), DMA((2,)), DMA,
     ]
@@ -1209,7 +1238,7 @@
         out_specs=VM,
         scratch_shapes=[
             room(16), room(16), room(8), room(8), room(4), room(4), room(2, 4), room(2, 4),
-            room(16), room(16), room(2, 16), room(2, 16), room(4), room(2), room(2), room(),
+            less(16), less(16), less(2, 16), less(2, 16), less(4), less(2), less(2), less(),
         ]
         + sems()
         + sems(),
@@ -1387,13 +1416,13 @@
     want = ROWS * C
     flat = flat[:want] if flat.shape[0] >= want else jnp.pad(flat, (0, want - flat.shape[0]))
     blocks = jax.vmap(compact)(flat.reshape(BLOCKS, BLOCK_ROWS, C))
-    return blocks.reshape(BLOCKS, 2, PART, 128)
+    return blocks
 
 
 def scatter_grads(blocks, size):
     if blocks_fit(size):
         return scatter_blocks(blocks).reshape(size)
-    flat = jax.vmap(restore)(blocks.reshape(BLOCKS, 2 * PART, 128)).reshape(-1)
+    flat = jax.vmap(restore)(blocks).reshape(-1)
     want = size * lax.axis_size("dp") * lax.axis_size("space")
     flat = flat[:want] if flat.shape[0] >= want else jnp.pad(flat, (0, want - flat.shape[0]))
     own = lax.psum_scatter(flat, ("dp", "space"), scatter_dimension=0, tiled=True)

time: 219 us -> 213 us (0.973)
  Pallas kernels: 216 us -> 210 us
    pallas_call x1, Pallas kernels: 32.1 us -> 26.6 us  [scatter_blocks(): pl.pallas_call(scatter_kernel, name='scatter', out_shape=shape_of((BLOCK_...]
where the time goes in v5:
time: 213 us; the launch traced here: 212 us
  Pallas kernels  210 us (99%)
    pallas_call x1, Pallas kernels, mix(): pl.pallas_call(mix_kernel, name='mix', in_specs=[VM] * 7 + [pl.BlockSpec(...  55.3 us
    pallas_call x1, Pallas kernels, attend_back(): pl.pallas_call(attend_back_kernel, name='attend_back', grid=(scenes, step...  29.2 us
    pallas_call x1, Pallas kernels, scatter_blocks(): pl.pallas_call(scatter_kernel, name='scatter', out_shape=shape_of((BLOCK_...  26.6 us
    pallas_call x1, Pallas kernels, gather_blocks(): pl.pallas_call(gather_kernel, name='gather', out_shape=shape_of((BLOCKS,...  26.5 us
    pallas_call x1, Pallas kernels, attend(): pl.pallas_call(attend_kernel, name='attend', grid=(scenes, steps), in_spe...  24.1 us
    pallas_call x1, Pallas kernels, merge(): pl.pallas_call(merge_kernel, name='merge', out_shape=shape_of(one, F32),...  15.3 us
    pallas_call x1, Pallas kernels, share(): pl.pallas_call(share_kernel, name='share', out_shape=(shape_of((bands,) +...  13 us
    pallas_call x1, Pallas kernels, tail(): pl.pallas_call(tail_kernel, name='tail', grid=(tokens // TILE,), in_specs...  8.83 us

profile of v5, /device:TPU:0, one launch (start us, length us, event | category | flops | bytes accessed | tf_op | source)
XLA Modules:
  0.0 212.4 jit_solution(10520600969678911870)
XLA Ops:
  0.6 0.1 add_convert_fusion.edge
  0.7 1.0 reshape.31.own_ref
  1.7 26.5 %gather.1.g_ref = bf16[32,416,128]{2,1,0:T(8,128)(2,1)S(1)} custom-call(bf16[162,320]{1,0:T(8,128)(2,1)S(1)} %reshape.31.own_ref), custom_call_target="tpu_custom_call" | custom-call | tf_op jit(solution)/shard_map/gather/pallas_call | solution.py:1013
  28.3 0.0 copy-start
  28.3 2.1 unpack.1
  30.4 0.0 copy-start.1
  30.4 0.0 copy-done
  30.4 4.5 %front.1 = (bf16[2048,320]{1,0:T(8,128)(2,1)S(1)}, f32[512,320]{1,0:T(8,128)S(1)}, bf16[512,320]{1,0:T(8,128)(2,1)S(1)}) custom-call(bf16[2048,320]{1,0:T(8,128)(2,1)S(1)} %bitcast.8, f32[16,320]{1,0:T(8,128)S(1)} %get-tuple-element.43.vec, bf16[320,320]{1,0:T(8,128)(2,1)S(1)} %get-tuple-element.44.wq, bf16[1280,320]{1,0:T(8,128)(2,1)S(1)} %get-tuple-element.45.wr), custom_call_target="tpu_custom_call" | custom-call | tf_op jit(solution)/shard_map/front/pallas_call | solution.py:246
  34.9 0.0 copy-start.2
  34.9 0.0 copy-done.1
  34.9 13.0 %share.1 = (bf16[4,512,320]{2,1,0:T(8,128)(2,1)S(1)}, bf16[2,1,64,320]{3,2,1,0:T(8,128)(2,1)S(1)}, bf16[2,1,64,320]{3,2,1,0:T(8,128)(2,1)S(1)}) custom-call(bf16[512,320]{1,0:T(8,128)(2,1)S(1)} %get-tuple-element.47.rn, bf16[2,16,64,320]{3,2,1,0:T(8,128)(2,1)S(1)} %copy-done.1), custom_call_target="tpu_custom_call" | custom-call | tf_op jit(solution)/shard_map/share/pallas_call | solution.py:1329
  47.9 0.0 copy-done.2
  47.9 24.1 %attend.1 = (bf16[2048,320]{1,0:T(8,128)(2,1)S(1)}, f32[2048,128]{1,0:T(8,128)S(1)}, f32[2048,320]{1,0:T(8,128)S(1)}, bf16[2048,320]{1,0:T(8,128)(2,1)S(1)}, bf1...) custom-call(bf16[2048,320]{1,0:T(8,128)(2,1)S(1)} %bitcast.9, ...), custom_call_target="tpu_custom_call" | custom-call | tf_op jit(solution)/shard_map/attend/pallas_call | solution.py:322
  72.1 2.2 %halo.1 = (bf16[2,2,64,320]{3,2,1,0:T(8,128)(2,1)S(1)}, bf16[2,2,64,320]{3,2,1,0:T(8,128)(2,1)S(1)}) custom-call(bf16[2,16,64,320]{3,2,1,0:T(8,128)(2,1)S(1)} %bitcast.11), custom_call_target="tpu_custom_call" | custom-call | tf_op jit(solution)/shard_map/halo/pallas_call | solution.py:1352
  74.3 55.3 %mix.1 = (bf16[2048,320]{1,0:T(8,128)(2,1)}, f32[2048,320]{1,0:T(8,128)S(1)}, f32[320,1280]{1,0:T(8,128)S(1)}, f32[320,1280]{1,0:T(8,128)S(1)}, f32[16,1280]{1,0:T(8,128)S(1)}, /*index=5*/f32[8,320]{1,0:T(8,128)S(1)}) custom-call(bf16[2,16,64,320]{3,2,1,0:T(8,128)(2,1)S(1)} %bitcast.12, bf16[2,2,64,320]{3,2,1,0:T(8,128)(2,1)S(1)} %get-tuple-element.53.n2_top, ...), custom_call_target="tpu_custom_call" | custom-call | tf_op jit(solution)/shard_map/mix/pallas_call | solution.py:563
  129.6 29.2 %attend_back.1 = (bf16[2048,320]{1,0:T(8,128)(2,1)S(1)}, bf16[4,2,256,320]{3,2,1,0:T(8,128)(2,1)S(1)}, f32[320,320]{1,0:T(8,128)S(1)}, f32[320,320]{1,0:T(8,128)...) custom-call(bf16[2048,320]{1,0:T(8,128)(2,1)S(1)} %get-tuple-element.46.q_ref, ...), custom_call_target="tpu_custom_call" | custom-call | tf_op jit(solution)/shard_map/attend_back/pallas_call | solution.py:659
  158.8 0.0 copy-start.3
  158.8 15.3 %merge.1.grn_ref = f32[512,320]{1,0:T(8,128)S(1)} custom-call(bf16[4,512,320]{2,1,0:T(8,128)(2,1)S(1)} %bitcast.15), custom_call_target="tpu_custom_call" | custom-call | tf_op jit(solution)/shard_map/merge/pallas_call | solution.py:1387
  174.2 0.0 copy-done.3
  174.2 8.8 %tail.1 = (f32[2048,320]{1,0:T(8,128)}, f32[320,320]{1,0:T(8,128)S(1)}, f32[1280,320]{1,0:T(8,128)S(1)}, f32[8,320]{1,0:T(8,128)S(1)}) custom-call(bf16[2048,320]{1,0:T(8,128)(2,1)S(1)} %bitcast.10, f32[2048,320]{1,0:T(8,128)S(1)} %get-tuple-element.62.gmid_ref, bf16[2048,320]{1,0:T(8,128)(2,1)S(1)} %get-tuple-element.68.dq_ref, ...), custom_call_target="tpu_custom_call" | custom-call | tf_op jit(solution)/shard_map/tail/pallas_call | solution.py:748
  183.0 2.0 pack.1.parts
  185.0 26.6 %scatter.1 = f32[162,320]{1,0:T(8,128)S(1)} custom-call(bf16[32,416,128]{2,1,0:T(8,128)(2,1)S(1)} %pack.1.parts), custom_call_target="tpu_custom_call" | custom-call | tf_op jit(solution)/shard_map/scatter/pallas_call | solution.py:1233
  211.6 0.8 reshape.37
Async XLA Ops:
  28.3 2.2 %copy-start = (bf16[2,16,64,320]{3,2,1,0:T(8,128)(2,1)S(1)}, bf16[2,16,64,320]{3,2,1,0:T(8,128)(2,1)}, u32[]{:S(2)}) copy-start(bf16[2,16,64,320]{3,2,1,0:T(8,128)(2,1)} %param.3) | copy-start | bytes 3932164
  30.4 4.5 %copy-start.1 = (bf16[2,16,64,320]{3,2,1,0:T(8,128)(2,1)S(1)}, bf16[2,16,64,320]{3,2,1,0:T(8,128)(2,1)}, u32[]{:S(2)}) copy-start(bf16[2,16,64,320]{3,2,1,0:T(8,128)(2,1)} %cot.3) | copy-start | bytes 3932164
  34.9 13.0 %copy-start.2 = (f32[512,320]{1,0:T(8,128)}, f32[512,320]{1,0:T(8,128)S(1)}, u32[]{:S(2)}) copy-start(f32[512,320]{1,0:T(8,128)S(1)} %get-tuple-element.70.red_ref) | copy-start | bytes 1966084
  158.8 15.4 %copy-start.3 = (f32[512,320]{1,0:T(8,128)S(1)}, f32[512,320]{1,0:T(8,128)}, u32[]{:S(2)}) copy-start(f32[512,320]{1,0:T(8,128)} %copy-done.2) | copy-start | bytes 1966084

commit v6 on v5

--- a/solution.py
+++ b/solution.py
@@ -45,8 +45,8 @@
 HIDDEN_ROWS = 11
 
 ROOM = dict(
-    unpack=30, front=14, attend=34, mix=33, attend_back=26, tail=16, pack=32,
-    gather=8, scatter=18, share=3, halo=2, merge=8,
+    unpack=30, front=14, attend=34, mix=32, attend_back=26, tail=15, pack=32,
+    gather=8, scatter=18, share=3, halo=2,
 )
 
 
@@ -146,7 +146,11 @@
     )(blocks)
 
 
-def pack_kernel(gwq, gwr, gwk, gwv, gwo, gwe, gws, gvec0, gvec1, gvec2, ghid, out, tiles):
+def pack_kernel(
+    gwq, gwr, gwk, gwv, gwo, gwe, gws, gvec0, gvec1, gvec2, ghid, gmid, gnorm, out, gx, tiles
+):
+    gx[...] = gmid[...] + gnorm[...]
+
     def put(start, value):
         count = value.shape[0]
         tiles[0, start : start + count, :] = value[:, 0:128]
@@ -179,7 +183,7 @@
     put(VECTOR_ROWS[V_OUTPUT], gvec1[8:9, :])
     put(USED_ROWS, jnp.zeros((ROWS - USED_ROWS, C), F32))
     half = BLOCK_ROWS // 2
-    spare = jnp.zeros((SPAN - 2 * BLOCK_ROWS - half, 128), F32)
+    spare = jnp.zeros((2 * SPAN - 2 * BLOCK_ROWS - half, 128), F32)
     for i in range(BLOCKS):
         at = i * BLOCK_ROWS
         tail = jnp.concatenate(
@@ -190,14 +194,15 @@
             axis=1,
         )
         rows = [tiles[0, at : at + BLOCK_ROWS, :], tiles[1, at : at + BLOCK_ROWS, :], tail, spare]
-        out[i] = jnp.concatenate(rows, axis=0).astype(BF16)
+        rows = jnp.concatenate(rows, axis=0)
+        out[i] = jnp.concatenate([rows[:SPAN], rows[SPAN:]], axis=1).astype(BF16)
 
 
 def pack(*pieces):
     return pl.pallas_call(
         pack_kernel,
         name="pack",
-        out_shape=shape_of((BLOCKS, SPAN, 128), BF16),
+        out_shape=(shape_of((BLOCKS, SPAN, 256), BF16), shape_of(pieces[-1].shape, F32)),
         scratch_shapes=[pltpu.VMEM((3, ROWS, 128), F32)],
         compiler_params=params("pack"),
     )(*pieces)
@@ -698,72 +703,6 @@
     )(q, inv, mixed, gmid, p, key, vt, rn_all, wk, wv, wo)
 
 
-def tail_kernel(
-    x_ref, gmid_ref, dq_ref, grn_ref, red_ref, vec, wq, wr,
-    gx_out, gwq_out, gwr_out, gvec_out, scr, gscr,
-):
-    @pl.when(pl.program_id(0) == 0)
-    def _():
-        for ref in (gwq_out, gwr_out, gvec_out):
-            ref[...] = jnp.zeros_like(ref)
-
-    runit, rrstd = norm_parts(red_ref[...])
-    grn = grn_ref[...].astype(F32)
-    gred = norm_back(grn, runit, rrstd, vec[V_RGAIN : V_RGAIN + 1, :]).astype(BF16)
-    unit, rstd = norm_parts(x_ref[...].astype(F32))
-    gain = vec[V_GAIN1 : V_GAIN1 + 1, :]
-    normed = (unit * gain + vec[V_SHIFT1 : V_SHIFT1 + 1, :]).astype(BF16)
-    split_tiles(scr, normed.astype(F32))
-    pieces = patch_pieces(scr)
-    back = {}
-    for k in range(4):
-        at = slice(k * C, (k + 1) * C)
-        gwr_out[at, :] += mm_tn(pieces[k].astype(BF16), gred)
-        back[k] = mm_nt(gred, wr[at, :]).reshape(TILE // (2 * W), 1, W // 2, C)
-    for b in range(2):
-        cols = jnp.concatenate([back[b], back[2 + b]], axis=1).reshape(TILE // 2, C)
-        spot = pl.ds(b, TILE // 2, stride=2)
-        gscr[0, spot, :] = cols[:, 0:128]
-        gscr[1, spot, :] = cols[:, 128:256]
-        gscr[2, spot, :] = jnp.concatenate(
-            [cols[:, 256:320], jnp.zeros((TILE // 2, 64), F32)], axis=1
-        )
-    dq = dq_ref[...]
-    gwq_out[...] += mm_tn(normed, dq)
-    placed = jnp.concatenate([gscr[0], gscr[1], gscr[2][:, 0:64]], axis=1)
-    gnormed = mm_nt(dq, wq[...]) + placed
-    gx_out[...] = gmid_ref[...] + norm_back(gnormed, unit, rstd, gain)
-    gvec_out[0:1, :] += row_sum(dq.astype(F32))
-    gvec_out[1:2, :] += row_sum(gred.astype(F32))
-    gvec_out[2:3, :] += row_sum(grn * runit)
-    gvec_out[3:4, :] += row_sum(grn)
-    gvec_out[4:5, :] += row_sum(gnormed * unit)
-    gvec_out[5:6, :] += row_sum(gnormed)
-
-
-def tail(x, gmid, dq, grn, red, vec, wq, wr):
-    tokens = x.shape[0]
-    tile = pl.BlockSpec((TILE, C), lambda i: (i, 0))
-    rtile = pl.BlockSpec((RTILE, C), lambda i: (i, 0))
-    return pl.pallas_call(
-        tail_kernel,
-        name="tail",
-        grid=(tokens // TILE,),
-        in_specs=[
-            tile, tile, tile, rtile, rtile, full((16, C)), full((C, C)), full((4 * C, C))
-        ],
-        out_specs=[tile, full((C, C)), full((4 * C, C)), full((8, C))],
-        out_shape=(
-            shape_of((tokens, C), F32),
-            shape_of((C, C), F32),
-            shape_of((4 * C, C), F32),
-            shape_of((8, C), F32),
-        ),
-        scratch_shapes=[pltpu.VMEM((3, TILE, 128), F32), pltpu.VMEM((3, TILE, 128), F32)],
-        compiler_params=params("tail"),
-    )(x, gmid, dq, grn, red, vec, wq, wr)
-
-
 def flip(value, by):
     return value + by * (1 - 2 * value)
 
@@ -850,20 +789,22 @@
 
 
 DMA = pltpu.SemaphoreType.DMA
-SPAN = 416
-PART = 288
+SPAN = 208
+PART = 144
 BOTH = (pl.ds(0, PART), pl.ds(PART, SPAN - PART))
 
 
 def compact(block):
     half = BLOCK_ROWS // 2
     tail = jnp.concatenate([block[:half, 256:], block[half:, 256:]], axis=1)
-    spare = jnp.zeros((SPAN - 2 * BLOCK_ROWS - half, 128), block.dtype)
-    return jnp.concatenate([block[:, 0:128], block[:, 128:256], tail, spare], axis=0)
-
-
-def restore(rows):
+    spare = jnp.zeros((2 * SPAN - 2 * BLOCK_ROWS - half, 128), block.dtype)
+    rows = jnp.concatenate([block[:, 0:128], block[:, 128:256], tail, spare], axis=0)
+    return jnp.concatenate([rows[:SPAN], rows[SPAN:]], axis=1)
+
+
+def restore(block):
     half = BLOCK_ROWS // 2
+    rows = jnp.concatenate([block[:, 0:128], block[:, 128:256]], axis=0)
     tail = rows[2 * BLOCK_ROWS : 2 * BLOCK_ROWS + half]
     return jnp.concatenate(
         [
@@ -1013,11 +954,11 @@
     return pl.pallas_call(
         gather_kernel,
         name="gather",
-        out_shape=shape_of((BLOCKS, SPAN, 128), BF16),
+        out_shape=shape_of((BLOCKS, SPAN, 256), BF16),
         in_specs=[VM],
         out_specs=VM,
         scratch_shapes=[
-            pltpu.VMEM((SPAN, 128), BF16),
+            pltpu.VMEM((SPAN, 256), BF16),
             DMA((2, 1, 4)), DMA((4,)), DMA((2, 4)), DMA((4, 4)),
             DMA((2, 4, 4)), DMA, DMA((2,)), DMA((4, 4)),
             DMA((BLOCKS, 2)),
@@ -1040,6 +981,8 @@
     slots = [(da, db, z) for da in (1, 0) for db in (1, 0) for z in range(line)]
 
     def add(*terms):
+        if len(terms) == 2:
+            return terms[0] + terms[1]
         total = terms[0].astype(F32)
         for term in terms[1:]:
             total = total + term.astype(F32)
@@ -1225,8 +1168,8 @@
 
 
 def scatter_blocks(parts):
-    room = lambda *n: pltpu.VMEM(n + (PART, 128), BF16)
-    less = lambda *n: pltpu.VMEM(n + (SPAN - PART, 128), BF16)
+    room = lambda *n: pltpu.VMEM(n + (PART, 256), BF16)
+    less = lambda *n: pltpu.VMEM(n + (SPAN - PART, 256), BF16)
     sems = lambda: [
         DMA((16,)), DMA((8,)), DMA((4,)), DMA((2, 4)), DMA((16,)), DMA((2, 16)), DMA((2,)), DMA,
     ]
@@ -1360,47 +1303,140 @@
     )(value)
 
 
-def merge_kernel(parts, out, rc, acc, rb, c_sem, c_in, b_sem, b_in):
+CHUNKS = 4
+
+
+def tail_kernel(
+    parts, x_ref, dq_ref, red_ref, vec, wq, wr,
+    gx_out, gwq_out, gwr_out, gvec_out,
+    rc, acc, rb, grn_scr, gn_scr, unit_scr, rstd_scr, pieces_scr, scr, gscr,
+    c_sem, c_in, b_sem, b_in,
+):
     band, sibling, across = bands_of()
     greet([({"space": sibling}, None), ({"space": across}, None)])
     far = across + sibling - band
-    first = remote(parts.at[far], rc.at[0], c_sem.at[0], c_in.at[0], {"space": sibling})
-    second = remote(parts.at[sibling], rc.at[1], c_sem.at[1], c_in.at[1], {"space": sibling})
-    onward = remote(acc, rb, b_sem, b_in, {"space": across})
-    first.start()
-    second.start()
-    first.wait_recv()
-    acc[...] = (parts[across].astype(F32) + rc[0].astype(F32)).astype(BF16)
-    onward.start()
-    second.wait_recv()
-    out[...] = parts[band].astype(F32) + rc[1].astype(F32)
-    onward.wait_recv()
-    out[...] += rb[...].astype(F32)
-    first.wait_send()
-    second.wait_send()
-    onward.wait_send()
-
-
-def merge(parts):
+    size = rc.shape[1] // CHUNKS
+    chunks = [pl.ds(j * size, size) for j in range(CHUNKS)]
+
+    def copy_first(j):
+        src, dst = parts.at[far, chunks[j]], rc.at[0, chunks[j]]
+        return remote(src, dst, c_sem.at[0, j], c_in.at[0, j], {"space": sibling})
+
+    def copy_second(j):
+        src, dst = parts.at[sibling, chunks[j]], rc.at[1, chunks[j]]
+        return remote(src, dst, c_sem.at[1, j], c_in.at[1, j], {"space": sibling})
+
+    def copy_onward(j):
+        src, dst = acc.at[chunks[j]], rb.at[chunks[j]]
+        return remote(src, dst, b_sem.at[j], b_in.at[j], {"space": across})
+
+    for j in range(CHUNKS):
+        copy_first(j).start()
+    for j in range(CHUNKS):
+        copy_second(j).start()
+    tiles = x_ref.shape[0] // TILE
+    gain = vec[V_GAIN1 : V_GAIN1 + 1, :]
+    for ref in (gwq_out, gwr_out, gvec_out):
+        ref[...] = jnp.zeros_like(ref)
+    for j in range(CHUNKS):
+        copy_first(j).wait_recv()
+        acc[chunks[j], :] = parts[across, chunks[j]] + rc[0, chunks[j]]
+        copy_onward(j).start()
+
+    def before(i, carry):
+        rows = pl.ds(pl.multiple_of(i * TILE, TILE), TILE)
+        unit, rstd = norm_parts(x_ref[rows, :].astype(F32))
+        unit_scr[rows, :] = unit
+        rstd_scr[rows, :] = jnp.broadcast_to(rstd, (TILE, 128))
+        normed = (unit * gain + vec[V_SHIFT1 : V_SHIFT1 + 1, :]).astype(BF16)
+        split_tiles(scr, normed.astype(F32))
+        pieces = patch_pieces(scr)
+        spot = pl.ds(pl.multiple_of(i * RTILE, RTILE), RTILE)
+        for k in range(4):
+            pieces_scr[k, spot, :] = pieces[k].astype(BF16)
+        dq = dq_ref[rows, :]
+        gwq_out[...] += mm_tn(normed, dq)
+        gn_scr[rows, :] = mm_nt(dq, wq[...])
+        gvec_out[0:1, :] += row_sum(dq.astype(F32))
+        return carry
+
+    lax.fori_loop(0, tiles, before, 0)
+    def after(i, carry):
+        rows = pl.ds(pl.multiple_of(i * TILE, TILE), TILE)
+        spot = pl.ds(pl.multiple_of(i * RTILE, RTILE), RTILE)
+        runit, rrstd = norm_parts(red_ref[spot, :])
+        grn = grn_scr[spot, :]
+        gred = norm_back(grn, runit, rrstd, vec[V_RGAIN : V_RGAIN + 1, :]).astype(BF16)
+        back = {}
+        for k in range(4):
+            at = slice(k * C, (k + 1) * C)
+            gwr_out[at, :] += mm_tn(pieces_scr[k, spot, :], gred)
+            back[k] = mm_nt(gred, wr[at, :]).reshape(TILE // (2 * W), 1, W // 2, C)
+        for b in range(2):
+            cols = jnp.concatenate([back[b], back[2 + b]], axis=1).reshape(TILE // 2, C)
+            places = pl.ds(b, TILE // 2, stride=2)
+            gscr[0, places, :] = cols[:, 0:128]
+            gscr[1, places, :] = cols[:, 128:256]
+            gscr[2, places, :] = jnp.concatenate(
+                [cols[:, 256:320], jnp.zeros((TILE // 2, 64), F32)], axis=1
+            )
+        placed = jnp.concatenate([gscr[0], gscr[1], gscr[2][:, 0:64]], axis=1)
+        gnormed = gn_scr[rows, :] + placed
+        unit = unit_scr[rows, :]
+        gx_out[rows, :] = norm_back(gnormed, unit, rstd_scr[rows, 0:1], gain)
+        gvec_out[1:2, :] += row_sum(gred.astype(F32))
+        gvec_out[2:3, :] += row_sum(grn * runit)
+        gvec_out[3:4, :] += row_sum(grn)
+        gvec_out[4:5, :] += row_sum(gnormed * unit)
+        gvec_out[5:6, :] += row_sum(gnormed)
+        return carry
+
+    for j in range(CHUNKS):
+        copy_second(j).wait_recv()
+        copy_onward(j).wait_recv()
+        own = parts[band, chunks[j]].astype(F32)
+        grn_scr[chunks[j], :] = own + (
+            rc[1, chunks[j]].astype(F32) + rb[chunks[j], :].astype(F32)
+        )
+        lax.fori_loop(j * tiles // CHUNKS, (j + 1) * tiles // CHUNKS, after, 0)
+    for j in range(CHUNKS):
+        copy_first(j).wait_send()
+        copy_second(j).wait_send()
+        copy_onward(j).wait_send()
+
+
+def tail(parts, x, dq, red, vec, wq, wr):
     one = parts.shape[1:]
-    dma = pltpu.SemaphoreType.DMA
+    tokens = x.shape[0]
     return pl.pallas_call(
-        merge_kernel,
-        name="merge",
-        out_shape=shape_of(one, F32),
-        in_specs=[VM],
-        out_specs=VM,
+        tail_kernel,
+        name="tail",
+        out_shape=(
+            shape_of((tokens, C), F32),
+            shape_of((C, C), F32),
+            shape_of((4 * C, C), F32),
+            shape_of((8, C), F32),
+        ),
+        in_specs=[VM] * 7,
+        out_specs=(VM,) * 4,
         scratch_shapes=[
             pltpu.VMEM((2,) + one, BF16),
             pltpu.VMEM(one, BF16),
             pltpu.VMEM(one, BF16),
-            dma((2,)),
-            dma((2,)),
-            dma,
-            dma,
+            pltpu.VMEM(one, F32),
+            pltpu.VMEM((tokens, C), F32),
+            pltpu.VMEM((tokens, C), F32),
+            pltpu.VMEM((tokens, 128), F32),
+            pltpu.VMEM((4,) + one, BF16),
+            pltpu.VMEM((3, TILE, 128), F32),
+            pltpu.VMEM((3, TILE, 128), F32),
+            DMA((2, CHUNKS)),
+            DMA((2, CHUNKS)),
+            DMA((CHUNKS,)),
+            DMA((CHUNKS,)),
         ],
-        compiler_params=comm_params("merge", 5),
-    )(parts)
+        compiler_params=comm_params("tail", 5),
+    )(parts, x, dq, red, vec, wq, wr)
 
 
 def blocks_fit(size):
@@ -1450,9 +1486,11 @@
     dq, grn_all, gwk, gwv, gwo, gvec1 = attend_back(
         q, inv, mixed, gmid, p, key, vt, rn_all, wk, wv, wo
     )
-    grn = merge(grn_all.reshape(bands, count * per_band, C))
-    gx, gwq, gwr, gvec0 = tail(x, gmid, dq, grn, red, vec, wq, wr)
-    blocks = pack(gwq, gwr, gwk, gwv, gwo, gwe, gws, gvec0, gvec1, gvec2, ghid)
+    parts = grn_all.reshape(bands, count * per_band, C)
+    gnorm, gwq, gwr, gvec0 = tail(parts, x, dq, red, vec, wq, wr)
+    blocks, gx = pack(
+        gwq, gwr, gwk, gwv, gwo, gwe, gws, gvec0, gvec1, gvec2, ghid, gmid, gnorm
+    )
     grads = scatter_grads(blocks, shard.shape[0])
     return y.reshape(scenes.shape), gx.reshape(scenes.shape), grads
 

time: 213 us -> 206 us (0.967)
  Pallas kernels: 210 us -> 204 us
    pallas_call x3 -> x2, Pallas kernels: 26.2 us -> 20.5 us  [the longest x1 16.5 us: tail(): pl.pallas_call(tail_kernel, name='tail', out_shape=(shape_of((tokens, C),...]
where the time goes in v6:
time: 206 us
  Pallas kernels  204 us (99%)
    pallas_call x1, Pallas kernels, mix(): pl.pallas_call(mix_kernel, name='mix', in_specs=[VM] * 7 + [pl.BlockSpec(...  55.3 us
    pallas_call x1, Pallas kernels, attend_back(): pl.pallas_call(attend_back_kernel, name='attend_back', grid=(scenes, step...  29.3 us
    pallas_call x1, Pallas kernels, gather_blocks(): pl.pallas_call(gather_kernel, name='gather', out_shape=shape_of((BLOCKS,...  26.5 us
    pallas_call x1, Pallas kernels, scatter_blocks(): pl.pallas_call(scatter_kernel, name='scatter', out_shape=shape_of((BLOCK_...  26 us
    pallas_call x1, Pallas kernels, attend(): pl.pallas_call(attend_kernel, name='attend', grid=(scenes, steps), in_spe...  24.1 us
    pallas_call x1, Pallas kernels, tail(): pl.pallas_call(tail_kernel, name='tail', out_shape=(shape_of((tokens, C),...  16.5 us
    pallas_call x1, Pallas kernels, share(): pl.pallas_call(share_kernel, name='share', out_shape=(shape_of((bands,) +...  13 us
    pallas_call x1, Pallas kernels, front(): pl.pallas_call(front_kernel, name='front', grid=(tokens // TILE,), in_spe...  4.45 us

profile of v6, /device:TPU:0, one launch (start us, length us, event | category | flops | bytes accessed | tf_op | source)
XLA Modules:
  0.0 206.3 jit_solution(12592445086272177784)
XLA Ops:
  0.6 0.1 add_convert_fusion.edge
  0.7 1.0 reshape.31.own_ref
  1.7 26.5 %gather.1.g_ref = bf16[32,208,256]{2,1,0:T(8,128)(2,1)S(1)} custom-call(bf16[162,320]{1,0:T(8,128)(2,1)S(1)} %reshape.31.own_ref), custom_call_target="tpu_custom_call" | custom-call | tf_op jit(solution)/shard_map/gather/pallas_call | solution.py:954
  28.3 0.0 copy-start
  28.3 2.1 %unpack.1 = (bf16[320,320]{1,0:T(8,128)(2,1)S(1)}, bf16[1280,320]{1,0:T(8,128)(2,1)S(1)}, bf16[320,320]{1,0:T(8,128)(2,1)S(1)}, bf16[320,320]{1,0:T(8,128)(2,1)S...) custom-call(bf16[32,208,256]{2,1,0:T(8,128)(2,1)S(1)} %gather.1.g_ref), custom_call_target="tpu_custom_call" | custom-call | tf_op jit(solution)/shard_map/unpack/pallas_call | solution.py:130
  30.4 0.0 copy-start.1
  30.5 0.0 copy-done
  30.5 4.5 %front.1 = (bf16[2048,320]{1,0:T(8,128)(2,1)S(1)}, f32[512,320]{1,0:T(8,128)S(1)}, bf16[512,320]{1,0:T(8,128)(2,1)S(1)}) custom-call(bf16[2048,320]{1,0:T(8,128)(2,1)S(1)} %bitcast.8, f32[16,320]{1,0:T(8,128)S(1)} %get-tuple-element.45.vec, bf16[320,320]{1,0:T(8,128)(2,1)S(1)} %get-tuple-element.46.wq, bf16[1280,320]{1,0:T(8,128)(2,1)S(1)} %get-tuple-element.47.wr), custom_call_target="tpu_custom_call" | custom-call | tf_op jit(solution)/shard_map/front/pallas_call | solution.py:251
  34.9 0.0 copy-done.1
  34.9 13.0 %share.1 = (bf16[4,512,320]{2,1,0:T(8,128)(2,1)S(1)}, bf16[2,1,64,320]{3,2,1,0:T(8,128)(2,1)S(1)}, bf16[2,1,64,320]{3,2,1,0:T(8,128)(2,1)S(1)}) custom-call(bf16[512,320]{1,0:T(8,128)(2,1)S(1)} %get-tuple-element.49.rn, bf16[2,16,64,320]{3,2,1,0:T(8,128)(2,1)S(1)} %copy-done.1), custom_call_target="tpu_custom_call" | custom-call | tf_op jit(solution)/shard_map/share/pallas_call | solution.py:1272
  47.9 24.1 %attend.1 = (bf16[2048,320]{1,0:T(8,128)(2,1)S(1)}, f32[2048,128]{1,0:T(8,128)S(1)}, f32[2048,320]{1,0:T(8,128)S(1)}, bf16[2048,320]{1,0:T(8,128)(2,1)S(1)}, bf1...) custom-call(bf16[2048,320]{1,0:T(8,128)(2,1)S(1)} %bitcast.9, ...), custom_call_target="tpu_custom_call" | custom-call | tf_op jit(solution)/shard_map/attend/pallas_call | solution.py:327
  72.1 2.3 %halo.1 = (bf16[2,2,64,320]{3,2,1,0:T(8,128)(2,1)S(1)}, bf16[2,2,64,320]{3,2,1,0:T(8,128)(2,1)S(1)}) custom-call(bf16[2,16,64,320]{3,2,1,0:T(8,128)(2,1)S(1)} %bitcast.11), custom_call_target="tpu_custom_call" | custom-call | tf_op jit(solution)/shard_map/halo/pallas_call | solution.py:1295
  74.3 55.3 %mix.1 = (bf16[2048,320]{1,0:T(8,128)(2,1)}, f32[2048,320]{1,0:T(8,128)S(1)}, f32[320,1280]{1,0:T(8,128)S(1)}, f32[320,1280]{1,0:T(8,128)S(1)}, f32[16,1280]{1,0:T(8,128)S(1)}, /*index=5*/f32[8,320]{1,0:T(8,128)S(1)}) custom-call(bf16[2,16,64,320]{3,2,1,0:T(8,128)(2,1)S(1)} %bitcast.12, bf16[2,2,64,320]{3,2,1,0:T(8,128)(2,1)S(1)} %get-tuple-element.55.n2_top, ...), custom_call_target="tpu_custom_call" | custom-call | tf_op jit(solution)/shard_map/mix/pallas_call | solution.py:568
  129.6 29.3 %attend_back.1 = (bf16[2048,320]{1,0:T(8,128)(2,1)S(1)}, bf16[4,2,256,320]{3,2,1,0:T(8,128)(2,1)S(1)}, f32[320,320]{1,0:T(8,128)S(1)}, f32[320,320]{1,0:T(8,128)...) custom-call(bf16[2048,320]{1,0:T(8,128)(2,1)S(1)} %get-tuple-element.48.q_ref, ...), custom_call_target="tpu_custom_call" | custom-call | tf_op jit(solution)/shard_map/attend_back/pallas_call | solution.py:664
  158.9 16.5 %tail.1 = (f32[2048,320]{1,0:T(8,128)S(1)}, f32[320,320]{1,0:T(8,128)S(1)}, f32[1280,320]{1,0:T(8,128)S(1)}, f32[8,320]{1,0:T(8,128)S(1)}) custom-call(bf16[4,512,320]{2,1,0:T(8,128)(2,1)S(1)} %bitcast.15, bf16[2048,320]{1,0:T(8,128)(2,1)S(1)} %bitcast.10, bf16[2048,320]{1,0:T(8,128)(2,1)S(1)} %get-tuple-element.71.dq_ref, ...), custom_call_target="tpu_custom_call" | custom-call | tf_op jit(solution)/shard_map/tail/pallas_call | solution.py:1411
  175.4 4.0 %pack.1 = (bf16[32,208,256]{2,1,0:T(8,128)(2,1)S(1)}, f32[2048,320]{1,0:T(8,128)}) custom-call(f32[320,320]{1,0:T(8,128)S(1)} %get-tuple-element.73.gwq, f32[1280,320]{1,0:T(8,128)S(1)} %get-tuple-element.74.gwr, f32[320,320]{1,0:T(8,128)S(1)} %get-tuple-element.75.gwk, f32[320,320]{1,0:T(8,128)S(1)} %get-tuple-element.76.gwv, ...), custom_call_target="tpu_custom_call" | custom-call | tf_op jit(solution)/shard_map/pack/pallas_call | solution.py:202
  179.4 26.0 %scatter.1 = f32[162,320]{1,0:T(8,128)S(1)} custom-call(bf16[32,208,256]{2,1,0:T(8,128)(2,1)S(1)} %get-tuple-element.86.parts), custom_call_target="tpu_custom_call" | custom-call | tf_op jit(solution)/shard_map/scatter/pallas_call | solution.py:1176
  205.5 0.8 reshape.37
Async XLA Ops:
  28.3 2.2 %copy-start = (bf16[2,16,64,320]{3,2,1,0:T(8,128)(2,1)S(1)}, bf16[2,16,64,320]{3,2,1,0:T(8,128)(2,1)}, u32[]{:S(2)}) copy-start(bf16[2,16,64,320]{3,2,1,0:T(8,128)(2,1)} %param.3) | copy-start | bytes 3932164
  30.4 4.5 %copy-start.1 = (bf16[2,16,64,320]{3,2,1,0:T(8,128)(2,1)S(1)}, bf16[2,16,64,320]{3,2,1,0:T(8,128)(2,1)}, u32[]{:S(2)}) copy-start(bf16[2,16,64,320]{3,2,1,0:T(8,128)(2,1)} %cot.3) | copy-start | bytes 3932164

commit v7 on v6

--- a/solution.py
+++ b/solution.py
@@ -45,8 +45,8 @@
 HIDDEN_ROWS = 11
 
 ROOM = dict(
-    unpack=30, front=14, attend=34, mix=32, attend_back=26, tail=15, pack=32,
-    gather=8, scatter=18, share=3, halo=2,
+    unpack=30, front=10, attend=34, mix=32, attend_back=26, tail=15, pack=32,
+    gather=8, scatter=18, halo=2,
 )
 
 
@@ -227,50 +227,6 @@
         for a in range(2):
             pieces[2 * a + b] = cols[:, a].reshape(RTILE, C)
     return pieces
-
-
-def front_kernel(x_ref, vec, wq, wr, q_out, red_out, rn_out, scr):
-    unit, _ = norm_parts(x_ref[...].astype(F32))
-    normed = (unit * vec[V_GAIN1 : V_GAIN1 + 1, :] + vec[V_SHIFT1 : V_SHIFT1 + 1, :]).astype(BF16)
-    queries = (mm(normed, wq[...]) + vec[V_QUERY : V_QUERY + 1, :]).astype(BF16)
-    q_out[...] = queries * jnp.asarray(1.0 / math.sqrt(HD), BF16)
-    split_tiles(scr, normed.astype(F32))
-    pieces = patch_pieces(scr)
-    reduced = vec[V_REDUCE : V_REDUCE + 1, :]
-    for k in range(4):
-        reduced = reduced + mm(pieces[k].astype(BF16), wr[k * C : (k + 1) * C, :])
-    red_out[...] = reduced
-    unit, _ = norm_parts(reduced)
-    rn_out[...] = (unit * vec[V_RGAIN : V_RGAIN + 1, :] + vec[V_RSHIFT : V_RSHIFT + 1, :]).astype(
-        BF16
-    )
-
-
-def front(x, vec, wq, wr):
-    tokens = x.shape[0]
-    return pl.pallas_call(
-        front_kernel,
-        name="front",
-        grid=(tokens // TILE,),
-        in_specs=[
-            pl.BlockSpec((TILE, C), lambda i: (i, 0)),
-            full((16, C)),
-            full((C, C)),
-            full((4 * C, C)),
-        ],
-        out_specs=[
-            pl.BlockSpec((TILE, C), lambda i: (i, 0)),
-            pl.BlockSpec((RTILE, C), lambda i: (i, 0)),
-            pl.BlockSpec((RTILE, C), lambda i: (i, 0)),
-        ],
-        out_shape=(
-            shape_of((tokens, C), BF16),
-            shape_of((tokens // 4, C), F32),
-            shape_of((tokens // 4, C), BF16),
-        ),
-        scratch_shapes=[pltpu.VMEM((3, TILE, 128), F32)],
-        compiler_params=params("front"),
-    )(x, vec, wq, wr)
 
 
 QT = 512
@@ -1195,7 +1151,7 @@
     return band, pair * 2 + 1 - core, (1 - pair) * 2 + core
 
 
-def swap_kernel(width, value, above, below, up_sem, down_sem, up_in, down_in, ready):
+def swap_kernel(width, value, above, below, up_sem, down_sem, up_in, down_in):
     band = lax.axis_index("space")
     rows = value.shape[1]
     ends = lax.axis_size("space") - 1
@@ -1235,58 +1191,102 @@
     )
 
 
-def share_kernel(
-    rn, cot, rn_all, above, below, send, recv, own_sem, up_sem, down_sem, up_in, down_in
+def front_kernel(
+    x_ref, cot, vec, wq, wr, q_out, red_out, rn_all, above, below,
+    normed_scr, scr, send, recv, up_sem, down_sem, up_in, down_in,
 ):
     band, sibling, across = bands_of()
+    far = across + sibling - band
     bands_meet((sibling, across))
-    to_sibling = remote(rn, rn_all.at[band], send.at[0], recv.at[band], {"space": sibling})
-    to_across = remote(rn, rn_all.at[band], send.at[1], recv.at[band], {"space": across})
-    to_across.start()
-    to_sibling.start()
-    own = pltpu.make_async_copy(rn, rn_all.at[band], own_sem)
-    own.start()
-    finish = swap_kernel(1, cot, above, below, up_sem, down_sem, up_in, down_in, None)
-
-    def landed(index):
-        remote(rn, rn_all.at[index], send.at[0], recv.at[index], {"space": sibling}).wait_recv()
-
-    landed(across)
-    onward = remote(
-        rn_all.at[across], rn_all.at[across], send.at[2], recv.at[across], {"space": sibling}
-    )
-    onward.start()
-    landed(sibling)
-    landed(across + sibling - band)
-    own.wait()
-    to_across.wait_send()
-    to_sibling.wait_send()
-    onward.wait_send()
+    finish = swap_kernel(1, cot, above, below, up_sem, down_sem, up_in, down_in)
+    tiles = x_ref.shape[0] // TILE
+
+    def spot_of(i):
+        return pl.ds(pl.multiple_of(i * RTILE, RTILE), RTILE)
+
+    def rows_of(i):
+        return pl.ds(pl.multiple_of(i * TILE, TILE), TILE)
+
+    def carry_on(index, way, i):
+        tile = rn_all.at[index, spot_of(i)]
+        where = {"space": across if way == 0 else sibling}
+        return remote(tile, tile, send.at[way, i], recv.at[index, i], where)
+
+    def reduce(i, carry):
+        unit, _ = norm_parts(x_ref[rows_of(i), :].astype(F32))
+        normed = unit * vec[V_GAIN1 : V_GAIN1 + 1, :] + vec[V_SHIFT1 : V_SHIFT1 + 1, :]
+        normed = normed.astype(BF16)
+        normed_scr[rows_of(i), :] = normed
+        split_tiles(scr, normed.astype(F32))
+        pieces = patch_pieces(scr)
+        reduced = vec[V_REDUCE : V_REDUCE + 1, :]
+        for k in range(4):
+            reduced = reduced + mm(pieces[k].astype(BF16), wr[k * C : (k + 1) * C, :])
+        red_out[spot_of(i), :] = reduced
+        unit, _ = norm_parts(reduced)
+        rnorm = unit * vec[V_RGAIN : V_RGAIN + 1, :] + vec[V_RSHIFT : V_RSHIFT + 1, :]
+        rn_all[band, spot_of(i)] = rnorm.astype(BF16)
+        carry_on(band, 0, i).start()
+        carry_on(band, 1, i).start()
+        return carry
+
+    def query(i, carry):
+        queries = (mm(normed_scr[rows_of(i), :], wq[...]) + vec[V_QUERY : V_QUERY + 1, :]).astype(
+            BF16
+        )
+        q_out[rows_of(i), :] = queries * jnp.asarray(1.0 / math.sqrt(HD), BF16)
+        carry_on(across, 2, i).wait_recv()
+        carry_on(across, 2, i).start()
+        return carry
+
+    def close(i, carry):
+        carry_on(sibling, 1, i).wait_recv()
+        carry_on(far, 1, i).wait_recv()
+        carry_on(band, 0, i).wait_send()
+        carry_on(band, 1, i).wait_send()
+        carry_on(across, 2, i).wait_send()
+        return carry
+
+    lax.fori_loop(0, tiles, reduce, 0)
+    lax.fori_loop(0, tiles, query, 0)
+    lax.fori_loop(0, tiles, close, 0)
     finish()
 
 
-def share(rn, cot):
+def front(x, cot, vec, wq, wr):
+    tokens = x.shape[0]
+    tiles = tokens // TILE
     bands = lax.axis_size("space")
-    dma = pltpu.SemaphoreType.DMA
     edge = (cot.shape[0], 1) + cot.shape[2:]
     return pl.pallas_call(
-        share_kernel,
-        name="share",
+        front_kernel,
+        name="front",
         out_shape=(
-            shape_of((bands,) + rn.shape, rn.dtype),
+            shape_of((tokens, C), BF16),
+            shape_of((tokens // 4, C), F32),
+            shape_of((bands, tokens // 4, C), BF16),
             shape_of(edge, cot.dtype),
             shape_of(edge, cot.dtype),
         ),
-        in_specs=[VM, ANY],
-        out_specs=(ANY, ANY, ANY),
-        scratch_shapes=[dma((3,)), dma((bands,)), dma, dma, dma, dma, dma],
-        compiler_params=comm_params("share", 3),
-    )(rn, cot)
+        in_specs=[VM, ANY, VM, VM, VM],
+        out_specs=(VM, VM, VM, ANY, ANY),
+        scratch_shapes=[
+            pltpu.VMEM((tokens, C), BF16),
+            pltpu.VMEM((3, TILE, 128), F32),
+            DMA((3, tiles)),
+            DMA((bands, tiles)),
+            DMA,
+            DMA,
+            DMA,
+            DMA,
+        ],
+        compiler_params=comm_params("front", 3),
+    )(x, cot, vec, wq, wr)
 
 
 def halo_kernel(value, above, below, up_sem, down_sem, up_in, down_in):
     bands_meet(())
-    swap_kernel(2, value, above, below, up_sem, down_sem, up_in, down_in, None)()
+    swap_kernel(2, value, above, below, up_sem, down_sem, up_in, down_in)()
 
 
 def halo(value):
@@ -1474,8 +1474,7 @@
     edge = jnp.stack([band > 0, band < bands - 1]).astype(F32)
     wq, wr, wk, wv, wo, we, ws, vec, hid = unpack(gather_flat(shard))
     x = scenes.reshape(tokens, C)
-    q, red, rn = front(x, vec, wq, wr)
-    rn_all, cot_top, cot_low = share(rn, cotangent)
+    q, red, rn_all, cot_top, cot_low = front(x, cotangent, vec, wq, wr)
     rn_all = rn_all.reshape(bands, count, per_band, C)
     mixed, inv, mid, n2, p, key, vt = attend(x, q, rn_all, vec, wk, wv, wo)
     n2 = n2.reshape(scenes.shape)

time: 206 us -> 203 us (0.985)
  Pallas kernels: 204 us -> 200 us
    pallas_call x2 -> x1, Pallas kernels: 17.4 us -> 14.4 us  [front(): pl.pallas_call(front_kernel, name='front', out_shape=(shape_of((tokens, C...]
where the time goes in v7:
time: 203 us
  Pallas kernels  200 us (99%)
    pallas_call x1, Pallas kernels, mix(): pl.pallas_call(mix_kernel, name='mix', in_specs=[VM] * 7 + [pl.BlockSpec(...  55.3 us
    pallas_call x1, Pallas kernels, attend_back(): pl.pallas_call(attend_back_kernel, name='attend_back', grid=(scenes, step...  29.3 us
    pallas_call x1, Pallas kernels, gather_blocks(): pl.pallas_call(gather_kernel, name='gather', out_shape=shape_of((BLOCKS,...  26.5 us
    pallas_call x1, Pallas kernels, scatter_blocks(): pl.pallas_call(scatter_kernel, name='scatter', out_shape=shape_of((BLOCK_...  26.1 us
    pallas_call x1, Pallas kernels, attend(): pl.pallas_call(attend_kernel, name='attend', grid=(scenes, steps), in_spe...  24.2 us
    pallas_call x1, Pallas kernels, tail(): pl.pallas_call(tail_kernel, name='tail', out_shape=(shape_of((tokens, C),...  17 us
    pallas_call x1, Pallas kernels, front(): pl.pallas_call(front_kernel, name='front', out_shape=(shape_of((tokens, C...  14.4 us

profile of v7, /device:TPU:0, one launch (start us, length us, event | category | flops | bytes accessed | tf_op | source)
XLA Modules:
  0.0 203.1 jit_solution(11019439425312671321)
XLA Ops:
  0.6 0.1 add_convert_fusion.edge
  0.7 1.0 reshape.31.own_ref
  1.7 26.5 %gather.1.g_ref = bf16[32,208,256]{2,1,0:T(8,128)(2,1)S(1)} custom-call(bf16[162,320]{1,0:T(8,128)(2,1)S(1)} %reshape.31.own_ref), custom_call_target="tpu_custom_call" | custom-call | tf_op jit(solution)/shard_map/gather/pallas_call | solution.py:910
  28.3 0.0 copy-start
  28.3 0.0 copy-start.1
  28.3 2.1 %unpack.1 = (bf16[320,320]{1,0:T(8,128)(2,1)S(1)}, bf16[1280,320]{1,0:T(8,128)(2,1)S(1)}, bf16[320,320]{1,0:T(8,128)(2,1)S(1)}, bf16[320,320]{1,0:T(8,128)(2,1)S...) custom-call(bf16[32,208,256]{2,1,0:T(8,128)(2,1)S(1)} %gather.1.g_ref), custom_call_target="tpu_custom_call" | custom-call | tf_op jit(solution)/shard_map/unpack/pallas_call | solution.py:130
  30.5 0.0 copy-done
  30.5 0.0 copy-done.1
  30.5 14.4 %front.1 = (bf16[2048,320]{1,0:T(8,128)(2,1)S(1)}, f32[512,320]{1,0:T(8,128)S(1)}, bf16[4,512,320]{2,1,0:T(8,128)(2,1)S(1)}, bf16[2,1,64,320]{3,2,1,0:T(8,128)(2,1)S(1)}, bf16[2,1,64,320]{3,2,1,0:T(8,128)(2,1)S(1)}) custom-call(bf16[2048,320]{1,0:T(8,128)(2,1)S(1)} %bitcast.8, bf16[2,16,64,320]{3,2,1,0:T(8,128)(2,1)S(1)} %copy-done.1, ...), custom_call_target="tpu_custom_call" | custom-call | tf_op jit(solution)/shard_map/front/pallas_call | solution.py:1261
  44.9 24.2 %attend.1 = (bf16[2048,320]{1,0:T(8,128)(2,1)S(1)}, f32[2048,128]{1,0:T(8,128)S(1)}, f32[2048,320]{1,0:T(8,128)S(1)}, bf16[2048,320]{1,0:T(8,128)(2,1)S(1)}, bf1...) custom-call(bf16[2048,320]{1,0:T(8,128)(2,1)S(1)} %bitcast.9, ...), custom_call_target="tpu_custom_call" | custom-call | tf_op jit(solution)/shard_map/attend/pallas_call | solution.py:283
  69.0 1.5 halo.1
  70.5 55.3 %mix.1 = (bf16[2048,320]{1,0:T(8,128)(2,1)}, f32[2048,320]{1,0:T(8,128)S(1)}, f32[320,1280]{1,0:T(8,128)S(1)}, f32[320,1280]{1,0:T(8,128)S(1)}, f32[16,1280]{1,0:T(8,128)S(1)}, /*index=5*/f32[8,320]{1,0:T(8,128)S(1)}) custom-call(bf16[2,16,64,320]{3,2,1,0:T(8,128)(2,1)S(1)} %bitcast.12, bf16[2,2,64,320]{3,2,1,0:T(8,128)(2,1)S(1)} %get-tuple-element.53.n2_top, ...), custom_call_target="tpu_custom_call" | custom-call | tf_op jit(solution)/shard_map/mix/pallas_call | solution.py:524
  125.8 29.3 %attend_back.1 = (bf16[2048,320]{1,0:T(8,128)(2,1)S(1)}, bf16[4,2,256,320]{3,2,1,0:T(8,128)(2,1)S(1)}, f32[320,320]{1,0:T(8,128)S(1)}, f32[320,320]{1,0:T(8,128)...) custom-call(bf16[2048,320]{1,0:T(8,128)(2,1)S(1)} %get-tuple-element.47.q_ref, ...), custom_call_target="tpu_custom_call" | custom-call | tf_op jit(solution)/shard_map/attend_back/pallas_call | solution.py:620
  155.1 17.0 %tail.1 = (f32[2048,320]{1,0:T(8,128)S(1)}, f32[320,320]{1,0:T(8,128)S(1)}, f32[1280,320]{1,0:T(8,128)S(1)}, f32[8,320]{1,0:T(8,128)S(1)}) custom-call(bf16[4,512,320]{2,1,0:T(8,128)(2,1)S(1)} %bitcast.15, bf16[2048,320]{1,0:T(8,128)(2,1)S(1)} %bitcast.10, bf16[2048,320]{1,0:T(8,128)(2,1)S(1)} %get-tuple-element.69.dq_ref, ...), custom_call_target="tpu_custom_call" | custom-call | tf_op jit(solution)/shard_map/tail/pallas_call | solution.py:1411
  172.1 4.0 %pack.1 = (bf16[32,208,256]{2,1,0:T(8,128)(2,1)S(1)}, f32[2048,320]{1,0:T(8,128)}) custom-call(f32[320,320]{1,0:T(8,128)S(1)} %get-tuple-element.71.gwq, f32[1280,320]{1,0:T(8,128)S(1)} %get-tuple-element.72.gwr, f32[320,320]{1,0:T(8,128)S(1)} %get-tuple-element.73.gwk, f32[320,320]{1,0:T(8,128)S(1)} %get-tuple-element.74.gwv, ...), custom_call_target="tpu_custom_call" | custom-call | tf_op jit(solution)/shard_map/pack/pallas_call | solution.py:202
  176.1 26.1 %scatter.1 = f32[162,320]{1,0:T(8,128)S(1)} custom-call(bf16[32,208,256]{2,1,0:T(8,128)(2,1)S(1)} %get-tuple-element.84.parts), custom_call_target="tpu_custom_call" | custom-call | tf_op jit(solution)/shard_map/scatter/pallas_call | solution.py:1132
  202.2 0.8 reshape.37
Async XLA Ops:
  28.3 2.2 %copy-start = (bf16[2,16,64,320]{3,2,1,0:T(8,128)(2,1)S(1)}, bf16[2,16,64,320]{3,2,1,0:T(8,128)(2,1)}, u32[]{:S(2)}) copy-start(bf16[2,16,64,320]{3,2,1,0:T(8,128)(2,1)} %param.3) | copy-start | bytes 3932164
  28.3 2.2 %copy-start.1 = (bf16[2,16,64,320]{3,2,1,0:T(8,128)(2,1)S(1)}, bf16[2,16,64,320]{3,2,1,0:T(8,128)(2,1)}, u32[]{:S(2)}) copy-start(bf16[2,16,64,320]{3,2,1,0:T(8,128)(2,1)} %cot.3) | copy-start | bytes 3932164
